TPU v7x, 32 devices: a whole 2x2x4 slice. The times are simulated.
32 devices in a mesh: gz: 16 (over z, y, x), gy: 2 (over core).
Axes of the slice: x: 2, y: 2, z: 4, core: 2. Of those that a mesh axis runs over, the one named last changes fastest.
Arguments:
- fodf: float32 [192, 16, 32, 128], P(None, 'gy', 'gz'), may hold values from 0 to 21, as said below
- directions: float32 [3, 192], replicated, may hold values from -1 to 1, as said below
- signs: int32 [3, 192], replicated, may hold values from -1 to 1, as said below
Outputs:
- enhanced: float32 [192, 16, 32, 128], P(None, 'gy', 'gz')
Inputs may be any that keep to these rules, and one draw needn't show every extreme that they name: `fodf`: Non-negative densities. `directions`: unit vectors; orientation k + 96 is the antipode of orientation k; no component is zero. `signs`: each sign is the sign of the matching component of directions; along each axis exactly 96 orientations have sign 1.
All inputs are finite; a program needn't handle non-finite values.
Results may differ from a plain program's by a relative error of at most 0.0003.
Values sent between devices are 32-bit elements; how exact they have to be, the bound alone decides.
No kernel may reach another device: no remote copies, remote signals or barrier semaphores. Data moves between devices by JAX's collectives and lax.ppermute only.
A program may use at most 64 MiB of HBM per device.

v0:
```python
import functools
import math

import jax
import jax.numpy as jnp
from jax import lax
from jax.experimental import pallas as pl
from jax.experimental.pallas import tpu as pltpu
from jax.sharding import PartitionSpec as P

LMAX = 8
ITERS = 4
TIME_STEP = 0.5
DIFFUSION = 0.02

VMEM = pltpu.VMEM
SMEM = pltpu.SMEM


def double_factorial(value):
    result = 1
    while value > 1:
        result = result * value
        value = value - 2
    return result


def harmonic_rows(directions):
    along_x, along_y, along_z = (directions[0], directions[1], directions[2])
    cosines = [jnp.ones_like(along_x)]
    sines = [jnp.zeros_like(along_x)]
    for order in range(1, LMAX + 1):
        cosines.append(cosines[-1] * along_x - sines[-1] * along_y)
        sines.append(cosines[-2] * along_y + sines[-1] * along_x)
    legendre = {}
    for order in range(LMAX + 1):
        legendre[order, order] = double_factorial(2 * order - 1) * jnp.ones_like(along_z)
        if order + 1 <= LMAX:
            legendre[order + 1, order] = (2 * order + 1) * along_z * legendre[order, order]
        for degree in range(order + 2, LMAX + 1):
            legendre[degree, order] = (
                (2 * degree - 1) * along_z * legendre[degree - 1, order]
                - (degree + order - 1) * legendre[degree - 2, order]
            ) / (degree - order)
    basis_rows = []
    eigen_values = []
    for degree in range(0, LMAX + 1, 2):
        for order in range(degree + 1):
            weight_norm = math.sqrt(
                (2 * degree + 1) * math.factorial(degree - order) / math.factorial(degree + order)
            )
            basis_rows.append(weight_norm * legendre[degree, order] * cosines[order])
            eigen_values.append(-float(degree * (degree + 1)))
            if order > 0:
                basis_rows.append(weight_norm * legendre[degree, order] * sines[order])
                eigen_values.append(-float(degree * (degree + 1)))
    return (jnp.stack(basis_rows, 0), jnp.array(eigen_values, dtype=directions.dtype))


def angular_matrix(half):
    basis, eigen_values = harmonic_rows(half)
    gram = 2.0 * jnp.dot(basis, basis.T, precision=lax.Precision.HIGHEST)
    chol_lower = jnp.linalg.cholesky(gram)
    partial_solve = lax.linalg.triangular_solve(chol_lower, basis, left_side=True, lower=True)
    analysis = lax.linalg.triangular_solve(
        chol_lower, partial_solve, left_side=True, lower=True, transpose_a=True
    )
    synthesis = basis.T * (TIME_STEP * DIFFUSION * eigen_values)[None, :]
    return jnp.dot(synthesis, analysis, precision=lax.Precision.HIGHEST)


def exchange(even_load, odd_load, axis):
    peers = lax.axis_size(axis)
    first = [(i, i ^ 1) for i in range(peers)]
    second = [(i, i + 1 if i % 2 else i - 1) for i in range(1, peers - 1)]
    got = [lax.ppermute(even_load, axis, first)]
    if second:
        got.append(lax.ppermute(odd_load, axis, second))
    return got


class Plan:
    def __init__(self, shape, z_peers, y_peers):
        self.kk, self.ny, self.nz, self.nx = shape
        self.half = self.kk // 2
        self.rows = self.ny * self.nz
        self.z_two = z_peers > 2
        self.y_two = y_peers > 2
        self.layer = jax.ShapeDtypeStruct((self.ny, self.half, self.nx), jnp.float32)
        self.rest = jax.ShapeDtypeStruct((2, self.nz - 1, self.ny, self.half, self.nx), jnp.float32)
        self.edge = jax.ShapeDtypeStruct((self.nz, self.half, self.nx), jnp.float32)
        self.field = jax.ShapeDtypeStruct((self.kk * self.rows, self.nx), jnp.float32)


def column(table, index, shape):
    return jnp.broadcast_to(table[:, index : index + 1], shape)


def from_below(even, got):
    first = got[0]
    if len(got) == 1:
        return jnp.where(even, jnp.zeros_like(first), first)
    return jnp.where(even, got[1], first)


def from_above(even, got):
    first = got[0]
    if len(got) == 1:
        return jnp.where(even, first, jnp.zeros_like(first))
    return jnp.where(even, first, got[1])


def write_edges(even, rising_y, get_p, get_n, plan, outs):
    for z in range(plan.nz):
        top, low = plan.ny - 1, 0
        up = jnp.where(rising_y, get_p(z, top), get_n(z, top))
        down = jnp.where(rising_y, get_n(z, low), get_p(z, low))
        outs[0][z] = jnp.where(even, up, down)
        if plan.y_two:
            outs[1][z] = jnp.where(even, down, up)


def open_body(plan, flags, table, field, even_ref, odd_ref, rest_ref, *edges):
    shape = (plan.half, plan.nx)
    even = flags[0] == 0
    rising_z = column(table, 6, shape) > 0
    rising_y = column(table, 5, shape) > 0
    kept = {}
    for y in range(plan.ny):
        for z in range(plan.nz):
            row = y * plan.nz + z
            a = field[pl.ds(row, plan.half, stride=plan.rows), :]
            b = field[pl.ds(row + plan.half * plan.rows, plan.half, stride=plan.rows), :]
            p = jnp.where(rising_z, a, b)
            n = jnp.where(rising_z, b, a)
            if z < plan.nz - 1:
                rest_ref[0, z, y] = p
            if z > 0:
                rest_ref[1, z - 1, y] = n
            if z == plan.nz - 1:

                @pl.when(even)
                def _():
                    even_ref[y] = p

                @pl.when(jnp.logical_not(even))
                def _():
                    odd_ref[y] = p

            if z == 0:

                @pl.when(even)
                def _():
                    odd_ref[y] = n

                @pl.when(jnp.logical_not(even))
                def _():
                    even_ref[y] = n

            if y in (0, plan.ny - 1):
                kept[z, y] = (p, n)
    write_edges(
        flags[1] == 0,
        rising_y,
        lambda z, y: kept[z, y][0],
        lambda z, y: kept[z, y][1],
        plan,
        edges,
    )


def member_reader(plan, even, state, got, speed_z):
    even_ref, odd_ref, rest_ref = state

    def get_p(z, y):
        if z == plan.nz - 1:
            return jnp.where(even, even_ref[y], odd_ref[y])
        value = rest_ref[0, z, y]
        if got is not None and z == 0:
            value = value + speed_z * from_below(even, [g[y] for g in got])
        return value

    def get_n(z, y):
        if z == 0:
            return jnp.where(even, odd_ref[y], even_ref[y])
        value = rest_ref[1, z - 1, y]
        if got is not None and z == plan.nz - 1:
            value = value + speed_z * from_above(even, [g[y] for g in got])
        return value

    return get_p, get_n


def edge_body(plan, flags, table, even_ref, odd_ref, rest_ref, *refs):
    count = 1 + plan.z_two
    got, edges = refs[:count], refs[count:]
    shape = (plan.half, plan.nx)
    get_p, get_n = member_reader(
        plan, flags[0] == 0, (even_ref, odd_ref, rest_ref), got, column(table, 3, shape)
    )
    write_edges(flags[1] == 0, column(table, 5, shape) > 0, get_p, get_n, plan, edges)


def step_body(plan, first, flags, table, matrix, even_ref, odd_ref, rest_ref, *refs):
    z_count = 0 if first else 1 + plan.z_two
    y_count = 1 + plan.y_two
    got = None if first else refs[:z_count]
    y_got = refs[z_count : z_count + y_count]
    new_even, new_odd, new_rest, full, sums, turn = refs[z_count + y_count :]
    half, nx, ny, nz = plan.half, plan.nx, plan.ny, plan.nz
    shape = (half, nx)
    even = flags[0] == 0
    y_even = flags[1] == 0
    get_p, get_n = member_reader(
        plan, even, (even_ref, odd_ref, rest_ref), got, column(table, 3, shape)
    )
    for z in range(nz):
        low = from_below(y_even, [g[z] for g in y_got])
        high = from_above(y_even, [g[z] for g in y_got])
        full[0, z, 0] = low
        full[1, z, 0] = low
        full[0, z, ny + 1] = high
        full[1, z, ny + 1] = high
        for y in range(ny):
            p = get_p(z, y)
            n = get_n(z, y)
            full[0, z, y + 1] = p
            full[1, z, y + 1] = n
            row = z * ny + y
            sums[:, row * nx : (row + 1) * nx] = p + n
    turn[...] = jnp.dot(
        matrix[...],
        sums[...],
        precision=lax.Precision.HIGHEST,
        preferred_element_type=jnp.float32,
    )
    lane = lax.broadcasted_iota(jnp.int32, (8, nx), 1)
    first_lane = lane == 0
    last_lane = lane == nx - 1
    for part in range(half // 8):
        rows = pl.ds(part * 8, 8)
        tab = table[rows, :]
        tile = (8, nx)
        rest_speed = column(tab, 0, tile)
        speed_x = column(tab, 1, tile)
        speed_y = column(tab, 2, tile)
        speed_z = column(tab, 3, tile)
        rising_x = column(tab, 4, tile) > 0
        rising_y = column(tab, 5, tile) > 0
        for z in range(nz):
            for y in range(ny):
                row = z * ny + y
                p = full[0, z, y + 1, rows, :]
                n = full[1, z, y + 1, rows, :]
                u = jnp.where(rising_x, p, n)
                v = jnp.where(rising_x, n, p)
                u = jnp.where(first_lane, 0.0, pltpu.roll(u, 1, 1))
                v = jnp.where(last_lane, 0.0, pltpu.roll(v, nx - 1, 1))
                angular = turn[rows, row * nx : (row + 1) * nx]
                new_p = rest_speed * p + speed_x * jnp.where(rising_x, u, v) + angular
                new_n = rest_speed * n + speed_x * jnp.where(rising_x, v, u) + angular
                new_p = new_p + speed_y * jnp.where(
                    rising_y, full[0, z, y, rows, :], full[0, z, y + 2, rows, :]
                )
                new_n = new_n + speed_y * jnp.where(
                    rising_y, full[1, z, y + 2, rows, :], full[1, z, y, rows, :]
                )
                if z > 0:
                    new_p = new_p + speed_z * full[0, z - 1, y + 1, rows, :]
                if z < nz - 1:
                    new_n = new_n + speed_z * full[1, z + 1, y + 1, rows, :]
                if z < nz - 1:
                    new_rest[0, z, y, rows, :] = new_p
                if z > 0:
                    new_rest[1, z - 1, y, rows, :] = new_n
                if z == nz - 1:
                    full_p = new_p

                    @pl.when(even)
                    def _():
                        new_even[y, rows, :] = full_p

                    @pl.when(jnp.logical_not(even))
                    def _():
                        new_odd[y, rows, :] = full_p

                if z == 0:
                    full_n = new_n

                    @pl.when(even)
                    def _():
                        new_odd[y, rows, :] = full_n

                    @pl.when(jnp.logical_not(even))
                    def _():
                        new_even[y, rows, :] = full_n


def close_body(plan, flags, table, even_ref, odd_ref, rest_ref, *refs):
    got, field = refs[:-1], refs[-1]
    shape = (plan.half, plan.nx)
    rising_z = column(table, 6, shape) > 0
    get_p, get_n = member_reader(
        plan, flags[0] == 0, (even_ref, odd_ref, rest_ref), got, column(table, 3, shape)
    )
    for y in range(plan.ny):
        for z in range(plan.nz):
            row = y * plan.nz + z
            p = get_p(z, y)
            n = get_n(z, y)
            field[pl.ds(row, plan.half, stride=plan.rows), :] = jnp.where(rising_z, p, n)
            field[pl.ds(row + plan.half * plan.rows, plan.half, stride=plan.rows), :] = jnp.where(
                rising_z, n, p
            )


def call(body, outs, args, scratch=()):
    in_specs = [pl.BlockSpec(memory_space=SMEM)] + [pl.BlockSpec(memory_space=VMEM)] * (len(args) - 1)
    moved = sum(math.prod(a.shape) * 4 for a in list(args) + list(outs))
    return pl.pallas_call(
        body,
        out_shape=outs,
        in_specs=in_specs,
        out_specs=[pl.BlockSpec(memory_space=VMEM)] * len(outs),
        scratch_shapes=list(scratch),
        cost_estimate=pl.CostEstimate(flops=8 * moved, bytes_accessed=moved, transcendentals=0),
        compiler_params=pltpu.CompilerParams(vmem_limit_bytes=32 << 20),
    )(*args)


def shards(fodf, directions, signs):
    plan = Plan(fodf.shape, lax.axis_size("gz"), lax.axis_size("gy"))
    half = plan.half
    flags = jnp.stack([lax.axis_index("gz") % 2, lax.axis_index("gy") % 2]).astype(jnp.int32)
    near = directions[:, :half]
    turn = signs[:, :half].astype(jnp.float32)
    speeds = TIME_STEP * jnp.abs(near)
    columns = jnp.concatenate(
        [1.0 - jnp.sum(speeds, 0, keepdims=True), speeds, turn[:2] * turn[2:], turn[2:]], 0
    )
    table = columns.T
    field = fodf.reshape(plan.field.shape)
    edge_outs = [plan.edge] * (1 + plan.y_two)
    state_outs = [plan.layer, plan.layer, plan.rest]
    opened = call(
        functools.partial(open_body, plan), state_outs + edge_outs, [flags, table, field]
    )
    state, edges = opened[:3], opened[3:]
    matrix = angular_matrix(near)
    got = []
    for step in range(ITERS):
        if step > 0:
            edges = call(
                functools.partial(edge_body, plan), edge_outs, [flags, table, *state, *got]
            )
        arriving = exchange(state[0], state[1], "gz")
        y_got = exchange(edges[0], edges[-1], "gy")
        state = call(
            functools.partial(step_body, plan, step == 0),
            state_outs,
            [flags, table, matrix, *state, *got, *y_got],
            [
                VMEM((2, plan.nz, plan.ny + 2, half, plan.nx), jnp.float32),
                VMEM((half, plan.rows * plan.nx), jnp.float32),
                VMEM((half, plan.rows * plan.nx), jnp.float32),
            ],
        )
        got = arriving
    field = call(
        functools.partial(close_body, plan), [plan.field], [flags, table, *state, *got]
    )[0]
    return field.reshape(fodf.shape)


def solution(mesh):
    placed = (P(None, "gy", "gz", None), P(), P())
    return jax.shard_map(
        shards, mesh=mesh, in_specs=placed, out_specs=P(None, "gy", "gz", None), check_vma=False
    )
```

profile of v0, /device:TPU:2, one launch (start us, length us, event | category | flops | bytes accessed | tf_op | source)
XLA Modules:
  0.0 112.0 jit_solution(12635104136037133334)
XLA Ops:
  0.0 0.7 slice_convert_fusion
  0.7 0.7 fusion.12
  1.6 1.4 %copy-done = f32[192,8,2,128]{3,2,1,0:T(2,128)S(1)} copy-done((f32[192,8,2,128]{3,2,1,0:T(2,128)S(1)}, f32[192,8,2,128]{3,2,1,0:T(2,128)}, u32[]{:S(2)}) %copy-start) | copy-done | bytes 1572888
  3.1 1.5 %shard_map.46 = (f32[8,96,128]{2,1,0:T(8,128)S(1)}, f32[8,96,128]{2,1,0:T(8,128)S(1)}, f32[2,1,8,96,128]{4,3,2,1,0:T(8,128)S(1)}, f32[2,96,128]{2,1,0:T(8,128)S(1)}) custom-call(s32[2]{0:T(128)S(1)} %pad_add_fusion.flags, f32[96,7]{1,0:T(8,128)S(1)} %bitcast.23, f32[3072,128]{1,0:T(8,128)S(1)} %bitcast.32), custom_call_target="tpu_custom_call" | custom-call | flops 25973824 | bytes 3246728 | tf_op jit(solution)/shard_map/pallas_call | solution.py:320
  4.7 4.9 %collective-permute-start.2 = (f32[8,96,128]{2,1,0:T(8,128)S(1)}, f32[8,96,128]{2,1,0:T(8,128)S(1)}, u32[]{:S(2)}, u32[]{:S(2)}) collective-permute-start(f32[8,96,128]{2,1,0:T(8,128)S(1)} %get-tuple-element.22.odd_ref), channel_id=1, source_target_pairs={{2,4},{4,2},{6,8},{8,6},{10,12},{12,10},{14,16},{16,14},{18,20},{2... | collective-permute-start | bytes 1179656 | tf_op jit(solution)/shard_map/ppermute | solution.py:78
  10.2 4.1 %cholesky.16 = f32[45,45]{1,0:T(8,128)S(1)} custom-call(f32[45,45]{1,0:T(8,128)S(1)} %bitcast_add_fusion), custom_call_target="Cholesky" | custom-call | tf_op jit(solution)/shard_map/jit(cholesky)/cholesky | solution.py:63
  14.4 0.6 compare_reduce_fusion
  15.0 0.7 fusion
  15.7 3.4 %custom-call.8 = f32[1,45,45]{1,2,0:T(8,128)S(1)} custom-call(f32[1,45,45]{2,1,0:T(8,128)S(1)} %fusion), custom_call_target="InvertDiagBlocksLowerTriangular" | custom-call | tf_op jit(solution)/shard_map/triangular_solve | solution.py:65
  19.5 0.3 fusion.5.matrix
  19.9 17.0 %shard_map.47 = (f32[8,96,128]{2,1,0:T(8,128)S(1)}, f32[8,96,128]{2,1,0:T(8,128)S(1)}, f32[2,1,8,96,128]{4,3,2,1,0:T(8,128)S(1)}) custom-call(s32[2]{0:T(128)S(1)} %pad_add_fusion.flags, f32[96,7]{1,0:T(8,128)S(1)} %bitcast.24, f32[96,96]{1,0:T(8,128)S(1)} %fusion.5.matrix, f32[8,96,128]{2,1,0:T(8,128)S(1)} %get-tuple-element.21.even_ref, ...), custom_call_target="tpu_custom_call" | custom-call | flops 26268736 | bytes 3283592 | tf_op jit(solution)/shard_map/pallas_call | solution.py:320
  36.9 4.9 %collective-permute-start.5 = (f32[8,96,128]{2,1,0:T(8,128)S(1)}, f32[8,96,128]{2,1,0:T(8,128)S(1)}, u32[]{:S(2)}, u32[]{:S(2)}) collective-permute-start(f32[8,96,128]{2,1,0:T(8,128)S(1)} %get-tuple-element.26.odd_ref), channel_id=1, source_target_pairs={{2,4},{4,2},{6,8},{8,6},{10,12},{12,10},{14,16},{16,14},{18,20},{2... | collective-permute-start | bytes 1179656 | tf_op jit(solution)/shard_map/ppermute | solution.py:78
  41.8 0.7 shard_map.48
  42.5 1.3 %collective-permute-done.3.refs_2_ = f32[2,96,128]{2,1,0:T(8,128)S(1)} collective-permute-done((f32[2,96,128]{2,1,0:T(8,128)S(1)}, f32[2,96,128]{2,1,0:T(8,128)S(1)}, u32[]{:S(2)}, u32[]{:S(2)}) %collective-permute-start.3) | collective-permute-done | bytes 98336 | tf_op jit(solution)/shard_map/ppermute | solution.py:76
  43.8 17.2 %shard_map.49 = (f32[8,96,128]{2,1,0:T(8,128)S(1)}, f32[8,96,128]{2,1,0:T(8,128)S(1)}, f32[2,1,8,96,128]{4,3,2,1,0:T(8,128)S(1)}) custom-call(s32[2]{0:T(128)S(1)} %pad_add_fusion.flags, f32[96,7]{1,0:T(8,128)S(1)} %bitcast.26, f32[96,96]{1,0:T(8,128)S(1)} %fusion.5.matrix, f32[8,96,128]{2,1,0:T(8,128)S(1)} %get-tuple-element.25.even_ref, ...), custom_call_target="tpu_custom_call" | custom-call | flops 32560192 | bytes 4070024 | tf_op jit(solution)/shard_map/pallas_call | solution.py:320
  61.0 4.9 %collective-permute-start.8 = (f32[8,96,128]{2,1,0:T(8,128)S(1)}, f32[8,96,128]{2,1,0:T(8,128)S(1)}, u32[]{:S(2)}, u32[]{:S(2)}) collective-permute-start(f32[8,96,128]{2,1,0:T(8,128)S(1)} %get-tuple-element.29.odd_ref), channel_id=1, source_target_pairs={{2,4},{4,2},{6,8},{8,6},{10,12},{12,10},{14,16},{16,14},{18,20},{2... | collective-permute-start | bytes 1179656 | tf_op jit(solution)/shard_map/ppermute | solution.py:78
  65.9 0.7 shard_map.50
  66.6 1.3 %collective-permute-done.6.refs_2_ = f32[2,96,128]{2,1,0:T(8,128)S(1)} collective-permute-done((f32[2,96,128]{2,1,0:T(8,128)S(1)}, f32[2,96,128]{2,1,0:T(8,128)S(1)}, u32[]{:S(2)}, u32[]{:S(2)}) %collective-permute-start.6) | collective-permute-done | bytes 98336 | tf_op jit(solution)/shard_map/ppermute | solution.py:76
  67.9 17.3 %shard_map.51 = (f32[8,96,128]{2,1,0:T(8,128)S(1)}, f32[8,96,128]{2,1,0:T(8,128)S(1)}, f32[2,1,8,96,128]{4,3,2,1,0:T(8,128)S(1)}) custom-call(s32[2]{0:T(128)S(1)} %pad_add_fusion.flags, f32[96,7]{1,0:T(8,128)S(1)} %bitcast.28, f32[96,96]{1,0:T(8,128)S(1)} %fusion.5.matrix, f32[8,96,128]{2,1,0:T(8,128)S(1)} %get-tuple-element.28.even_ref, ...), custom_call_target="tpu_custom_call" | custom-call | flops 32560192 | bytes 4070024 | tf_op jit(solution)/shard_map/pallas_call | solution.py:320
  85.2 4.9 %collective-permute-start.11 = (f32[8,96,128]{2,1,0:T(8,128)S(1)}, f32[8,96,128]{2,1,0:T(8,128)S(1)}, u32[]{:S(2)}, u32[]{:S(2)}) collective-permute-start(f32[8,96,128]{2,1,0:T(8,128)S(1)} %get-tuple-element.32.odd_ref), channel_id=1, source_target_pairs={{2,4},{4,2},{6,8},{8,6},{10,12},{12,10},{14,16},{16,14},{18,20},{2... | collective-permute-start | bytes 1179656 | tf_op jit(solution)/shard_map/ppermute | solution.py:78
  90.1 0.7 shard_map.52
  90.8 1.3 %collective-permute-done.9.refs_2_ = f32[2,96,128]{2,1,0:T(8,128)S(1)} collective-permute-done((f32[2,96,128]{2,1,0:T(8,128)S(1)}, f32[2,96,128]{2,1,0:T(8,128)S(1)}, u32[]{:S(2)}, u32[]{:S(2)}) %collective-permute-start.9) | collective-permute-done | bytes 98336 | tf_op jit(solution)/shard_map/ppermute | solution.py:76
  92.1 17.2 %shard_map.53 = (f32[8,96,128]{2,1,0:T(8,128)S(1)}, f32[8,96,128]{2,1,0:T(8,128)S(1)}, f32[2,1,8,96,128]{4,3,2,1,0:T(8,128)S(1)}) custom-call(s32[2]{0:T(128)S(1)} %pad_add_fusion.flags, f32[96,7]{1,0:T(8,128)S(1)} %bitcast.30, f32[96,96]{1,0:T(8,128)S(1)} %fusion.5.matrix, f32[8,96,128]{2,1,0:T(8,128)S(1)} %get-tuple-element.31.even_ref, ...), custom_call_target="tpu_custom_call" | custom-call | flops 32560192 | bytes 4070024 | tf_op jit(solution)/shard_map/pallas_call | solution.py:320
  109.3 2.7 %shard_map.54 = f32[3072,128]{1,0:T(8,128)} custom-call(s32[2]{0:T(128)S(1)} %pad_add_fusion.flags, f32[96,7]{1,0:T(8,128)S(1)} %bitcast.31, f32[8,96,128]{2,1,0:T(8,128)S(1)} %get-tuple-element.34.even_ref, f32[8,96,128]{2,1,0:T(8,128)S(1)} %get-tuple-element.35.odd_ref, f32[2,1,8,96,128]{4,3,2,1,0:T(8,128)S(1)} %get-tuple-element.36.rest_ref, ...), custom_call_target="tpu_custom_call" | custom-call | flops 31478848 | bytes 3934856 | tf_op jit(solution)/shard_map/pallas_call | solution.py:320
  (44 shorter events, 1.6 us)
Async XLA Ops:
  0.0 19.5 %copy-start.2 = (f32[45]{0:T(128)S(1)}, f32[45]{0:T(128)}, u32[]{:S(2)}) copy-start(f32[45]{0:T(128)} %constant.272) | copy-start | bytes 544
  0.0 9.6 %copy-start.1 = (f32[3,192]{1,0:T(4,128)S(1)}, f32[3,192]{1,0:T(4,128)}, u32[]{:S(2)}) copy-start(f32[3,192]{1,0:T(4,128)} %param.5) | copy-start | bytes 6916
  1.6 1.4 %copy-start = (f32[192,8,2,128]{3,2,1,0:T(2,128)S(1)}, f32[192,8,2,128]{3,2,1,0:T(2,128)}, u32[]{:S(2)}) copy-start(f32[192,8,2,128]{3,2,1,0:T(2,128)} %param.4) | copy-start | bytes 4718596
  4.6 15.3 %collective-permute-start = (f32[2,96,128]{2,1,0:T(8,128)S(1)}, f32[2,96,128]{2,1,0:T(8,128)S(1)}, u32[]{:S(2)}, u32[]{:S(2)}) collective-permute-start(f32[2,96,128]{2,1,0:T(8,128)S(1)} %get-tuple-element.24), channel_id=1, source_target_pairs={{0,1},{1,0},{2,3},{3,2},{4,5},{5,4},{6,7},{7,6},{8,9},{9,8},{10,11... | collective-permute-start | bytes 294920 | tf_op jit(solution)/shard_map/ppermute | solution.py:76
  4.7 37.1 %collective-permute-start.1 = (f32[8,96,128]{2,1,0:T(8,128)S(1)}, f32[8,96,128]{2,1,0:T(8,128)S(1)}, u32[]{:S(2)}, u32[]{:S(2)}) collective-permute-start(f32[8,96,128]{2,1,0:T(8,128)S(1)} %get-tuple-element.21.even_ref), channel_id=1, source_target_pairs={{0,2},{2,0},{4,6},{6,4},{8,10},{10,8},{12,14},{14,12},{16,18},{18,... | collective-permute-start | bytes 1179656 | tf_op jit(solution)/shard_map/ppermute | solution.py:76
  4.7 37.0 %collective-permute-start.2 = (f32[8,96,128]{2,1,0:T(8,128)S(1)}, f32[8,96,128]{2,1,0:T(8,128)S(1)}, u32[]{:S(2)}, u32[]{:S(2)}) collective-permute-start(f32[8,96,128]{2,1,0:T(8,128)S(1)} %get-tuple-element.22.odd_ref), channel_id=1, source_target_pairs={{2,4},{4,2},{6,8},{8,6},{10,12},{12,10},{14,16},{16,14},{18,20},{2... | collective-permute-start | bytes 1179656 | tf_op jit(solution)/shard_map/ppermute | solution.py:78
  36.8 29.0 %collective-permute-start.4 = (f32[8,96,128]{2,1,0:T(8,128)S(1)}, f32[8,96,128]{2,1,0:T(8,128)S(1)}, u32[]{:S(2)}, u32[]{:S(2)}) collective-permute-start(f32[8,96,128]{2,1,0:T(8,128)S(1)} %get-tuple-element.25.even_ref), channel_id=1, source_target_pairs={{0,2},{2,0},{4,6},{6,4},{8,10},{10,8},{12,14},{14,12},{16,18},{18,... | collective-permute-start | bytes 1179656 | tf_op jit(solution)/shard_map/ppermute | solution.py:76
  36.9 29.0 %collective-permute-start.5 = (f32[8,96,128]{2,1,0:T(8,128)S(1)}, f32[8,96,128]{2,1,0:T(8,128)S(1)}, u32[]{:S(2)}, u32[]{:S(2)}) collective-permute-start(f32[8,96,128]{2,1,0:T(8,128)S(1)} %get-tuple-element.26.odd_ref), channel_id=1, source_target_pairs={{2,4},{4,2},{6,8},{8,6},{10,12},{12,10},{14,16},{16,14},{18,20},{2... | collective-permute-start | bytes 1179656 | tf_op jit(solution)/shard_map/ppermute | solution.py:78
  42.4 1.4 %collective-permute-start.3 = (f32[2,96,128]{2,1,0:T(8,128)S(1)}, f32[2,96,128]{2,1,0:T(8,128)S(1)}, u32[]{:S(2)}, u32[]{:S(2)}) collective-permute-start(f32[2,96,128]{2,1,0:T(8,128)S(1)} %shard_map.48), channel_id=1, source_target_pairs={{0,1},{1,0},{2,3},{3,2},{4,5},{5,4},{6,7},{7,6},{8,9},{9,8},{10,11... | collective-permute-start | bytes 294920 | tf_op jit(solution)/shard_map/ppermute | solution.py:76
  61.0 29.1 %collective-permute-start.7 = (f32[8,96,128]{2,1,0:T(8,128)S(1)}, f32[8,96,128]{2,1,0:T(8,128)S(1)}, u32[]{:S(2)}, u32[]{:S(2)}) collective-permute-start(f32[8,96,128]{2,1,0:T(8,128)S(1)} %get-tuple-element.28.even_ref), channel_id=1, source_target_pairs={{0,2},{2,0},{4,6},{6,4},{8,10},{10,8},{12,14},{14,12},{16,18},{18,... | collective-permute-start | bytes 1179656 | tf_op jit(solution)/shard_map/ppermute | solution.py:76
  61.0 29.1 %collective-permute-start.8 = (f32[8,96,128]{2,1,0:T(8,128)S(1)}, f32[8,96,128]{2,1,0:T(8,128)S(1)}, u32[]{:S(2)}, u32[]{:S(2)}) collective-permute-start(f32[8,96,128]{2,1,0:T(8,128)S(1)} %get-tuple-element.29.odd_ref), channel_id=1, source_target_pairs={{2,4},{4,2},{6,8},{8,6},{10,12},{12,10},{14,16},{16,14},{18,20},{2... | collective-permute-start | bytes 1179656 | tf_op jit(solution)/shard_map/ppermute | solution.py:78
  66.5 1.4 %collective-permute-start.6 = (f32[2,96,128]{2,1,0:T(8,128)S(1)}, f32[2,96,128]{2,1,0:T(8,128)S(1)}, u32[]{:S(2)}, u32[]{:S(2)}) collective-permute-start(f32[2,96,128]{2,1,0:T(8,128)S(1)} %shard_map.50), channel_id=1, source_target_pairs={{0,1},{1,0},{2,3},{3,2},{4,5},{5,4},{6,7},{7,6},{8,9},{9,8},{10,11... | collective-permute-start | bytes 294920 | tf_op jit(solution)/shard_map/ppermute | solution.py:76
  85.2 24.1 %collective-permute-start.10 = (f32[8,96,128]{2,1,0:T(8,128)S(1)}, f32[8,96,128]{2,1,0:T(8,128)S(1)}, u32[]{:S(2)}, u32[]{:S(2)}) collective-permute-start(f32[8,96,128]{2,1,0:T(8,128)S(1)} %get-tuple-element.31.even_ref), channel_id=1, source_target_pairs={{0,2},{2,0},{4,6},{6,4},{8,10},{10,8},{12,14},{14,12},{16,18},{18,... | collective-permute-start | bytes 1179656 | tf_op jit(solution)/shard_map/ppermute | solution.py:76
  85.2 24.1 %collective-permute-start.11 = (f32[8,96,128]{2,1,0:T(8,128)S(1)}, f32[8,96,128]{2,1,0:T(8,128)S(1)}, u32[]{:S(2)}, u32[]{:S(2)}) collective-permute-start(f32[8,96,128]{2,1,0:T(8,128)S(1)} %get-tuple-element.32.odd_ref), channel_id=1, source_target_pairs={{2,4},{4,2},{6,8},{8,6},{10,12},{12,10},{14,16},{16,14},{18,20},{2... | collective-permute-start | bytes 1179656 | tf_op jit(solution)/shard_map/ppermute | solution.py:78
  90.8 1.4 %collective-permute-start.9 = (f32[2,96,128]{2,1,0:T(8,128)S(1)}, f32[2,96,128]{2,1,0:T(8,128)S(1)}, u32[]{:S(2)}, u32[]{:S(2)}) collective-permute-start(f32[2,96,128]{2,1,0:T(8,128)S(1)} %shard_map.52), channel_id=1, source_target_pairs={{0,1},{1,0},{2,3},{3,2},{4,5},{5,4},{6,7},{7,6},{8,9},{9,8},{10,11... | collective-permute-start | bytes 294920 | tf_op jit(solution)/shard_map/ppermute | solution.py:76
where the time goes:
time: 113 us; the launch traced here: 112 us
  Pallas kernels  74.7 us (66%)
  starting transfers between devices  19.9 us (18%)
  other arithmetic  10.5 us (9%)
  waiting for transfers between devices  3.89 us (3%)
  local copies, waits for them, and re-layouts  1.76 us (2%)
    pallas_call x9, Pallas kernels, call(): pl.pallas_call(body, out_shape=outs, in_specs=in_specs, out_specs=[pl.Blo...  74.7 us
    ppermute x4, starting transfers between devices, exchange(): got.append(lax.ppermute(odd_load, axis, second))  19.5 us
    another operation x3, other arithmetic, angular_matrix(): chol_lower = jnp.linalg.cholesky(gram)  4.78 us
    another operation x2, other arithmetic, angular_matrix(): lax.linalg.triangular_solve(chol_lower, partial_solve, left_side=True, lo...  4.1 us
    ppermute x8, waiting for transfers between devices, exchange(): got = [lax.ppermute(even_load, axis, first)]  3.88 us
  transfers between devices with their start and end apart: 12, of which 3 were waited for; matrix products, arithmetic and copies ran while one was open for 9% of the time, Pallas kernels for 63%

commit v1 on v0

--- a/solution.py
+++ b/solution.py
@@ -138,27 +138,13 @@
             if z > 0:
                 rest_ref[1, z - 1, y] = n
             if z == plan.nz - 1:
-
-                @pl.when(even)
-                def _():
-                    even_ref[y] = p
-
-                @pl.when(jnp.logical_not(even))
-                def _():
-                    odd_ref[y] = p
-
+                top = p
             if z == 0:
-
-                @pl.when(even)
-                def _():
-                    odd_ref[y] = n
-
-                @pl.when(jnp.logical_not(even))
-                def _():
-                    even_ref[y] = n
-
+                bottom = n
             if y in (0, plan.ny - 1):
                 kept[z, y] = (p, n)
+        even_ref[y] = jnp.where(even, top, bottom)
+        odd_ref[y] = jnp.where(even, bottom, top)
     write_edges(
         flags[1] == 0,
         rising_y,
@@ -201,57 +187,80 @@
     write_edges(flags[1] == 0, column(table, 5, shape) > 0, get_p, get_n, plan, edges)
 
 
+def split(value):
+    high = value.astype(jnp.bfloat16)
+    low = (value - high.astype(jnp.float32)).astype(jnp.bfloat16)
+    return high, low
+
+
 def step_body(plan, first, flags, table, matrix, even_ref, odd_ref, rest_ref, *refs):
     z_count = 0 if first else 1 + plan.z_two
     y_count = 1 + plan.y_two
     got = None if first else refs[:z_count]
     y_got = refs[z_count : z_count + y_count]
-    new_even, new_odd, new_rest, full, sums, turn = refs[z_count + y_count :]
+    new_even, new_odd, new_rest, full, highs, lows, turn = refs[z_count + y_count :]
     half, nx, ny, nz = plan.half, plan.nx, plan.ny, plan.nz
-    shape = (half, nx)
     even = flags[0] == 0
     y_even = flags[1] == 0
-    get_p, get_n = member_reader(
-        plan, even, (even_ref, odd_ref, rest_ref), got, column(table, 3, shape)
-    )
-    for z in range(nz):
-        low = from_below(y_even, [g[z] for g in y_got])
-        high = from_above(y_even, [g[z] for g in y_got])
-        full[0, z, 0] = low
-        full[1, z, 0] = low
-        full[0, z, ny + 1] = high
-        full[1, z, ny + 1] = high
+    for part in range(half // 16):
+        rows = pl.ds(part * 16, 16)
+        speed_z = column(table[rows, :], 3, (16, nx))
+        for z in range(nz):
+            low = from_below(y_even, [g[z, rows, :] for g in y_got])
+            high = from_above(y_even, [g[z, rows, :] for g in y_got])
+            full[0, z, 0, rows, :] = low
+            full[1, z, 0, rows, :] = low
+            full[0, z, ny + 1, rows, :] = high
+            full[1, z, ny + 1, rows, :] = high
         for y in range(ny):
-            p = get_p(z, y)
-            n = get_n(z, y)
-            full[0, z, y + 1] = p
-            full[1, z, y + 1] = n
-            row = z * ny + y
-            sums[:, row * nx : (row + 1) * nx] = p + n
-    turn[...] = jnp.dot(
-        matrix[...],
-        sums[...],
-        precision=lax.Precision.HIGHEST,
-        preferred_element_type=jnp.float32,
-    )
-    lane = lax.broadcasted_iota(jnp.int32, (8, nx), 1)
+            for z in range(nz):
+                if z == nz - 1:
+                    p = jnp.where(even, even_ref[y, rows, :], odd_ref[y, rows, :])
+                else:
+                    p = rest_ref[0, z, y, rows, :]
+                    if got is not None and z == 0:
+                        p = p + speed_z * from_below(even, [g[y, rows, :] for g in got])
+                if z == 0:
+                    n = jnp.where(even, odd_ref[y, rows, :], even_ref[y, rows, :])
+                else:
+                    n = rest_ref[1, z - 1, y, rows, :]
+                    if got is not None and z == nz - 1:
+                        n = n + speed_z * from_above(even, [g[y, rows, :] for g in got])
+                full[0, z, y + 1, rows, :] = p
+                full[1, z, y + 1, rows, :] = n
+                row = y * nz + z
+                high, low = split(p + n)
+                highs[rows, row * nx : (row + 1) * nx] = high
+                lows[rows, row * nx : (row + 1) * nx] = low
+    m_high, m_low = split(matrix[...])
+    width = nz * nx
+    for y in range(ny):
+        cols = slice(y * width, (y + 1) * width)
+        high = highs[:, cols]
+        turn[:, cols] = (
+            jnp.dot(m_high, high, preferred_element_type=jnp.float32)
+            + jnp.dot(m_low, high, preferred_element_type=jnp.float32)
+            + jnp.dot(m_high, lows[:, cols], preferred_element_type=jnp.float32)
+        )
+    tile = (8, nx)
+    lane = lax.broadcasted_iota(jnp.int32, tile, 1)
     first_lane = lane == 0
     last_lane = lane == nx - 1
     for part in range(half // 8):
         rows = pl.ds(part * 8, 8)
         tab = table[rows, :]
-        tile = (8, nx)
         rest_speed = column(tab, 0, tile)
         speed_x = column(tab, 1, tile)
         speed_y = column(tab, 2, tile)
         speed_z = column(tab, 3, tile)
         rising_x = column(tab, 4, tile) > 0
         rising_y = column(tab, 5, tile) > 0
-        for z in range(nz):
-            for y in range(ny):
-                row = z * ny + y
-                p = full[0, z, y + 1, rows, :]
-                n = full[1, z, y + 1, rows, :]
+        for y in range(ny):
+            ps = [full[0, z, y + 1, rows, :] for z in range(nz)]
+            ns = [full[1, z, y + 1, rows, :] for z in range(nz)]
+            for z in range(nz):
+                row = y * nz + z
+                p, n = ps[z], ns[z]
                 u = jnp.where(rising_x, p, n)
                 v = jnp.where(rising_x, n, p)
                 u = jnp.where(first_lane, 0.0, pltpu.roll(u, 1, 1))
@@ -266,34 +275,19 @@
                     rising_y, full[1, z, y + 2, rows, :], full[1, z, y, rows, :]
                 )
                 if z > 0:
-                    new_p = new_p + speed_z * full[0, z - 1, y + 1, rows, :]
+                    new_p = new_p + speed_z * ps[z - 1]
                 if z < nz - 1:
-                    new_n = new_n + speed_z * full[1, z + 1, y + 1, rows, :]
+                    new_n = new_n + speed_z * ns[z + 1]
                 if z < nz - 1:
                     new_rest[0, z, y, rows, :] = new_p
+                else:
+                    top = new_p
                 if z > 0:
                     new_rest[1, z - 1, y, rows, :] = new_n
-                if z == nz - 1:
-                    full_p = new_p
-
-                    @pl.when(even)
-                    def _():
-                        new_even[y, rows, :] = full_p
-
-                    @pl.when(jnp.logical_not(even))
-                    def _():
-                        new_odd[y, rows, :] = full_p
-
-                if z == 0:
-                    full_n = new_n
-
-                    @pl.when(even)
-                    def _():
-                        new_odd[y, rows, :] = full_n
-
-                    @pl.when(jnp.logical_not(even))
-                    def _():
-                        new_even[y, rows, :] = full_n
+                else:
+                    bottom = new_n
+            new_even[y, rows, :] = jnp.where(even, top, bottom)
+            new_odd[y, rows, :] = jnp.where(even, bottom, top)
 
 
 def close_body(plan, flags, table, even_ref, odd_ref, rest_ref, *refs):
@@ -361,7 +355,8 @@
             [flags, table, matrix, *state, *got, *y_got],
             [
                 VMEM((2, plan.nz, plan.ny + 2, half, plan.nx), jnp.float32),
-                VMEM((half, plan.rows * plan.nx), jnp.float32),
+                VMEM((half, plan.rows * plan.nx), jnp.bfloat16),
+                VMEM((half, plan.rows * plan.nx), jnp.bfloat16),
                 VMEM((half, plan.rows * plan.nx), jnp.float32),
             ],
         )

time: 113 us -> 78.8 us (0.70)
  Pallas kernels: 74.7 us -> 15.2 us
  waiting for transfers between devices: 3.89 us -> 32.8 us
  starting transfers between devices: 19.9 us -> 17.1 us
    pallas_call x9, Pallas kernels: 74.7 us -> 15.2 us  [call(): pl.pallas_call(body, out_shape=outs, in_specs=in_specs, out_specs=[pl.Blo...]
    ppermute x8, waiting for transfers between devices: 3.88 us -> 29.9 us  [exchange(): got = [lax.ppermute(even_load, axis, first)]]
    ppermute x4, starting transfers between devices: 19.5 us -> 16.5 us  [exchange(): got.append(lax.ppermute(odd_load, axis, second))]
    ppermute x4, waiting for transfers between devices: 0.01 us -> 2.87 us  [exchange(): got.append(lax.ppermute(odd_load, axis, second))]
  transfers between devices with their start and end apart: 12 -> 12, of which waited for: 3 -> 8; matrix products, arithmetic and copies ran while one was open for 9% -> 13% of each run, Pallas kernels for 63% -> 14%
where the time goes in v1:
time: 78.8 us; the launch traced here: 78.5 us
  waiting for transfers between devices  32.8 us (42%)
  starting transfers between devices  17.1 us (22%)
  Pallas kernels  15.2 us (19%)
  other arithmetic  10.5 us (13%)
  local copies, waits for them, and re-layouts  1.76 us (2%)
  matrix products  0.88 us (1%)
    ppermute x8, waiting for transfers between devices, exchange(): got = [lax.ppermute(even_load, axis, first)]  29.9 us
    ppermute x4, starting transfers between devices, exchange(): got.append(lax.ppermute(odd_load, axis, second))  16.5 us
    pallas_call x9, Pallas kernels, call(): pl.pallas_call(body, out_shape=outs, in_specs=in_specs, out_specs=[pl.Blo...  15.2 us
    another operation x3, other arithmetic, angular_matrix(): chol_lower = jnp.linalg.cholesky(gram)  4.78 us
    another operation x2, other arithmetic, angular_matrix(): lax.linalg.triangular_solve(chol_lower, partial_solve, left_side=True, lo...  4.1 us
    ppermute x4, waiting for transfers between devices, exchange(): got.append(lax.ppermute(odd_load, axis, second))  2.87 us
  transfers between devices with their start and end apart: 12, of which 8 were waited for; matrix products, arithmetic and copies ran while one was open for 13% of the time, Pallas kernels for 14%

profile of v1, /device:TPU:2, one launch (start us, length us, event | category | flops | bytes accessed | tf_op | source)
XLA Modules:
  0.0 78.5 jit_solution(2406335738838518901)
XLA Ops:
  0.0 0.7 slice_convert_fusion
  0.7 0.7 fusion.12
  1.6 1.4 %copy-done = f32[192,8,2,128]{3,2,1,0:T(2,128)S(1)} copy-done((f32[192,8,2,128]{3,2,1,0:T(2,128)S(1)}, f32[192,8,2,128]{3,2,1,0:T(2,128)}, u32[]{:S(2)}) %copy-start) | copy-done | bytes 1572888
  3.1 1.3 %shard_map.46 = (f32[8,96,128]{2,1,0:T(8,128)S(1)}, f32[8,96,128]{2,1,0:T(8,128)S(1)}, f32[2,1,8,96,128]{4,3,2,1,0:T(8,128)S(1)}, f32[2,96,128]{2,1,0:T(8,128)S(1)}) custom-call(s32[2]{0:T(128)S(1)} %pad_add_fusion.flags, f32[96,7]{1,0:T(8,128)S(1)} %bitcast.23, f32[3072,128]{1,0:T(8,128)S(1)} %bitcast.32), custom_call_target="tpu_custom_call" | custom-call | flops 25973824 | bytes 3246728 | tf_op jit(solution)/shard_map/pallas_call | solution.py:314
  4.5 4.9 %collective-permute-start.2 = (f32[8,96,128]{2,1,0:T(8,128)S(1)}, f32[8,96,128]{2,1,0:T(8,128)S(1)}, u32[]{:S(2)}, u32[]{:S(2)}) collective-permute-start(f32[8,96,128]{2,1,0:T(8,128)S(1)} %get-tuple-element.22.odd_ref), channel_id=1, source_target_pairs={{2,4},{4,2},{6,8},{8,6},{10,12},{12,10},{14,16},{16,14},{18,20},{2... | collective-permute-start | bytes 1179656 | tf_op jit(solution)/shard_map/ppermute | solution.py:78
  10.0 4.1 %cholesky.16 = f32[45,45]{1,0:T(8,128)S(1)} custom-call(f32[45,45]{1,0:T(8,128)S(1)} %bitcast_add_fusion), custom_call_target="Cholesky" | custom-call | tf_op jit(solution)/shard_map/jit(cholesky)/cholesky | solution.py:63
  15.4 3.4 %custom-call.8 = f32[1,45,45]{1,2,0:T(8,128)S(1)} custom-call(f32[1,45,45]{2,1,0:T(8,128)S(1)} %fusion), custom_call_target="InvertDiagBlocksLowerTriangular" | custom-call | tf_op jit(solution)/shard_map/triangular_solve | solution.py:65
  19.6 2.2 %shard_map.47 = (f32[8,96,128]{2,1,0:T(8,128)S(1)}, f32[8,96,128]{2,1,0:T(8,128)S(1)}, f32[2,1,8,96,128]{4,3,2,1,0:T(8,128)S(1)}) custom-call(s32[2]{0:T(128)S(1)} %pad_add_fusion.flags, f32[96,7]{1,0:T(8,128)S(1)} %bitcast.24, f32[96,96]{1,0:T(8,128)S(1)} %fusion.5.matrix, f32[8,96,128]{2,1,0:T(8,128)S(1)} %get-tuple-element.21.even_ref, ...), custom_call_target="tpu_custom_call" | custom-call | flops 26268736 | bytes 3283592 | tf_op jit(solution)/shard_map/pallas_call | solution.py:314
  21.9 4.9 %collective-permute-start.5 = (f32[8,96,128]{2,1,0:T(8,128)S(1)}, f32[8,96,128]{2,1,0:T(8,128)S(1)}, u32[]{:S(2)}, u32[]{:S(2)}) collective-permute-start(f32[8,96,128]{2,1,0:T(8,128)S(1)} %get-tuple-element.26.odd_ref), channel_id=1, source_target_pairs={{2,4},{4,2},{6,8},{8,6},{10,12},{12,10},{14,16},{16,14},{18,20},{2... | collective-permute-start | bytes 1179656 | tf_op jit(solution)/shard_map/ppermute | solution.py:78
  26.8 0.7 shard_map.48
  27.5 1.3 %collective-permute-done.3.refs_2_ = f32[2,96,128]{2,1,0:T(8,128)S(1)} collective-permute-done((f32[2,96,128]{2,1,0:T(8,128)S(1)}, f32[2,96,128]{2,1,0:T(8,128)S(1)}, u32[]{:S(2)}, u32[]{:S(2)}) %collective-permute-start.3) | collective-permute-done | bytes 98336 | tf_op jit(solution)/shard_map/ppermute | solution.py:76
  28.8 2.4 %shard_map.49 = (f32[8,96,128]{2,1,0:T(8,128)S(1)}, f32[8,96,128]{2,1,0:T(8,128)S(1)}, f32[2,1,8,96,128]{4,3,2,1,0:T(8,128)S(1)}) custom-call(s32[2]{0:T(128)S(1)} %pad_add_fusion.flags, f32[96,7]{1,0:T(8,128)S(1)} %bitcast.26, f32[96,96]{1,0:T(8,128)S(1)} %fusion.5.matrix, f32[8,96,128]{2,1,0:T(8,128)S(1)} %get-tuple-element.25.even_ref, ...), custom_call_target="tpu_custom_call" | custom-call | flops 32560192 | bytes 4070024 | tf_op jit(solution)/shard_map/pallas_call | solution.py:314
  31.3 4.9 %collective-permute-start.8 = (f32[8,96,128]{2,1,0:T(8,128)S(1)}, f32[8,96,128]{2,1,0:T(8,128)S(1)}, u32[]{:S(2)}, u32[]{:S(2)}) collective-permute-start(f32[8,96,128]{2,1,0:T(8,128)S(1)} %get-tuple-element.29.odd_ref), channel_id=1, source_target_pairs={{2,4},{4,2},{6,8},{8,6},{10,12},{12,10},{14,16},{16,14},{18,20},{2... | collective-permute-start | bytes 1179656 | tf_op jit(solution)/shard_map/ppermute | solution.py:78
  36.2 14.6 %collective-permute-done.4.refs_0_ = f32[8,96,128]{2,1,0:T(8,128)S(1)} collective-permute-done((f32[8,96,128]{2,1,0:T(8,128)S(1)}, f32[8,96,128]{2,1,0:T(8,128)S(1)}, u32[]{:S(2)}, u32[]{:S(2)}) %collective-permute-start.4) | collective-permute-done | bytes 393248 | tf_op jit(solution)/shard_map/ppermute | solution.py:76
  51.5 1.3 %collective-permute-done.6.refs_2_ = f32[2,96,128]{2,1,0:T(8,128)S(1)} collective-permute-done((f32[2,96,128]{2,1,0:T(8,128)S(1)}, f32[2,96,128]{2,1,0:T(8,128)S(1)}, u32[]{:S(2)}, u32[]{:S(2)}) %collective-permute-start.6) | collective-permute-done | bytes 98336 | tf_op jit(solution)/shard_map/ppermute | solution.py:76
  52.8 2.4 %shard_map.51 = (f32[8,96,128]{2,1,0:T(8,128)S(1)}, f32[8,96,128]{2,1,0:T(8,128)S(1)}, f32[2,1,8,96,128]{4,3,2,1,0:T(8,128)S(1)}) custom-call(s32[2]{0:T(128)S(1)} %pad_add_fusion.flags, f32[96,7]{1,0:T(8,128)S(1)} %bitcast.28, f32[96,96]{1,0:T(8,128)S(1)} %fusion.5.matrix, f32[8,96,128]{2,1,0:T(8,128)S(1)} %get-tuple-element.28.even_ref, ...), custom_call_target="tpu_custom_call" | custom-call | flops 32560192 | bytes 4070024 | tf_op jit(solution)/shard_map/pallas_call | solution.py:314
  55.2 1.9 %collective-permute-start.11 = (f32[8,96,128]{2,1,0:T(8,128)S(1)}, f32[8,96,128]{2,1,0:T(8,128)S(1)}, u32[]{:S(2)}, u32[]{:S(2)}) collective-permute-start(f32[8,96,128]{2,1,0:T(8,128)S(1)} %get-tuple-element.32.odd_ref), channel_id=1, source_target_pairs={{2,4},{4,2},{6,8},{8,6},{10,12},{12,10},{14,16},{16,14},{18,20},{2... | collective-permute-start | bytes 1179656 | tf_op jit(solution)/shard_map/ppermute | solution.py:78
  57.1 1.1 %collective-permute-done.7.refs_0_ = f32[8,96,128]{2,1,0:T(8,128)S(1)} collective-permute-done((f32[8,96,128]{2,1,0:T(8,128)S(1)}, f32[8,96,128]{2,1,0:T(8,128)S(1)}, u32[]{:S(2)}, u32[]{:S(2)}) %collective-permute-start.7) | collective-permute-done | bytes 393248 | tf_op jit(solution)/shard_map/ppermute | solution.py:76
  58.2 1.9 %collective-permute-done.8.refs_1_ = f32[8,96,128]{2,1,0:T(8,128)S(1)} collective-permute-done((f32[8,96,128]{2,1,0:T(8,128)S(1)}, f32[8,96,128]{2,1,0:T(8,128)S(1)}, u32[]{:S(2)}, u32[]{:S(2)}) %collective-permute-start.8) | collective-permute-done | bytes 393248 | tf_op jit(solution)/shard_map/ppermute | solution.py:78
  60.8 1.3 %collective-permute-done.9.refs_2_ = f32[2,96,128]{2,1,0:T(8,128)S(1)} collective-permute-done((f32[2,96,128]{2,1,0:T(8,128)S(1)}, f32[2,96,128]{2,1,0:T(8,128)S(1)}, u32[]{:S(2)}, u32[]{:S(2)}) %collective-permute-start.9) | collective-permute-done | bytes 98336 | tf_op jit(solution)/shard_map/ppermute | solution.py:76
  62.1 2.4 %shard_map.53 = (f32[8,96,128]{2,1,0:T(8,128)S(1)}, f32[8,96,128]{2,1,0:T(8,128)S(1)}, f32[2,1,8,96,128]{4,3,2,1,0:T(8,128)S(1)}) custom-call(s32[2]{0:T(128)S(1)} %pad_add_fusion.flags, f32[96,7]{1,0:T(8,128)S(1)} %bitcast.30, f32[96,96]{1,0:T(8,128)S(1)} %fusion.5.matrix, f32[8,96,128]{2,1,0:T(8,128)S(1)} %get-tuple-element.31.even_ref, ...), custom_call_target="tpu_custom_call" | custom-call | flops 32560192 | bytes 4070024 | tf_op jit(solution)/shard_map/pallas_call | solution.py:314
  64.5 10.4 %collective-permute-done.10.refs_0_ = f32[8,96,128]{2,1,0:T(8,128)S(1)} collective-permute-done((f32[8,96,128]{2,1,0:T(8,128)S(1)}, f32[8,96,128]{2,1,0:T(8,128)S(1)}, u32[]{:S(2)}, u32[]{:S(2)}) %collective-permute-start.10) | collective-permute-done | bytes 393248 | tf_op jit(solution)/shard_map/ppermute | solution.py:76
  74.9 1.0 %collective-permute-done.11.refs_1_ = f32[8,96,128]{2,1,0:T(8,128)S(1)} collective-permute-done((f32[8,96,128]{2,1,0:T(8,128)S(1)}, f32[8,96,128]{2,1,0:T(8,128)S(1)}, u32[]{:S(2)}, u32[]{:S(2)}) %collective-permute-start.11) | collective-permute-done | bytes 393248 | tf_op jit(solution)/shard_map/ppermute | solution.py:78
  75.9 2.7 %shard_map.54 = f32[3072,128]{1,0:T(8,128)} custom-call(s32[2]{0:T(128)S(1)} %pad_add_fusion.flags, f32[96,7]{1,0:T(8,128)S(1)} %bitcast.31, f32[8,96,128]{2,1,0:T(8,128)S(1)} %get-tuple-element.34.even_ref, f32[8,96,128]{2,1,0:T(8,128)S(1)} %get-tuple-element.35.odd_ref, f32[2,1,8,96,128]{4,3,2,1,0:T(8,128)S(1)} %get-tuple-element.36.rest_ref, ...), custom_call_target="tpu_custom_call" | custom-call | flops 31478848 | bytes 3934856 | tf_op jit(solution)/shard_map/pallas_call | solution.py:314
  (44 shorter events, 4.7 us)
Async XLA Ops:
  0.0 19.3 %copy-start.2 = (f32[45]{0:T(128)S(1)}, f32[45]{0:T(128)}, u32[]{:S(2)}) copy-start(f32[45]{0:T(128)} %constant.272) | copy-start | bytes 544
  0.0 9.4 %copy-start.1 = (f32[3,192]{1,0:T(4,128)S(1)}, f32[3,192]{1,0:T(4,128)}, u32[]{:S(2)}) copy-start(f32[3,192]{1,0:T(4,128)} %param.5) | copy-start | bytes 6916
  1.6 1.4 %copy-start = (f32[192,8,2,128]{3,2,1,0:T(2,128)S(1)}, f32[192,8,2,128]{3,2,1,0:T(2,128)}, u32[]{:S(2)}) copy-start(f32[192,8,2,128]{3,2,1,0:T(2,128)} %param.4) | copy-start | bytes 4718596
  4.3 15.3 %collective-permute-start = (f32[2,96,128]{2,1,0:T(8,128)S(1)}, f32[2,96,128]{2,1,0:T(8,128)S(1)}, u32[]{:S(2)}, u32[]{:S(2)}) collective-permute-start(f32[2,96,128]{2,1,0:T(8,128)S(1)} %get-tuple-element.24), channel_id=1, source_target_pairs={{0,1},{1,0},{2,3},{3,2},{4,5},{5,4},{6,7},{7,6},{8,9},{9,8},{10,11... | collective-permute-start | bytes 294920 | tf_op jit(solution)/shard_map/ppermute | solution.py:76
  4.4 22.4 %collective-permute-start.1 = (f32[8,96,128]{2,1,0:T(8,128)S(1)}, f32[8,96,128]{2,1,0:T(8,128)S(1)}, u32[]{:S(2)}, u32[]{:S(2)}) collective-permute-start(f32[8,96,128]{2,1,0:T(8,128)S(1)} %get-tuple-element.21.even_ref), channel_id=1, source_target_pairs={{0,2},{2,0},{4,6},{6,4},{8,10},{10,8},{12,14},{14,12},{16,18},{18,... | collective-permute-start | bytes 1179656 | tf_op jit(solution)/shard_map/ppermute | solution.py:76
  4.5 22.3 %collective-permute-start.2 = (f32[8,96,128]{2,1,0:T(8,128)S(1)}, f32[8,96,128]{2,1,0:T(8,128)S(1)}, u32[]{:S(2)}, u32[]{:S(2)}) collective-permute-start(f32[8,96,128]{2,1,0:T(8,128)S(1)} %get-tuple-element.22.odd_ref), channel_id=1, source_target_pairs={{2,4},{4,2},{6,8},{8,6},{10,12},{12,10},{14,16},{16,14},{18,20},{2... | collective-permute-start | bytes 1179656 | tf_op jit(solution)/shard_map/ppermute | solution.py:78
  21.8 28.9 %collective-permute-start.4 = (f32[8,96,128]{2,1,0:T(8,128)S(1)}, f32[8,96,128]{2,1,0:T(8,128)S(1)}, u32[]{:S(2)}, u32[]{:S(2)}) collective-permute-start(f32[8,96,128]{2,1,0:T(8,128)S(1)} %get-tuple-element.25.even_ref), channel_id=1, source_target_pairs={{0,2},{2,0},{4,6},{6,4},{8,10},{10,8},{12,14},{14,12},{16,18},{18,... | collective-permute-start | bytes 1179656 | tf_op jit(solution)/shard_map/ppermute | solution.py:76
  21.9 28.8 %collective-permute-start.5 = (f32[8,96,128]{2,1,0:T(8,128)S(1)}, f32[8,96,128]{2,1,0:T(8,128)S(1)}, u32[]{:S(2)}, u32[]{:S(2)}) collective-permute-start(f32[8,96,128]{2,1,0:T(8,128)S(1)} %get-tuple-element.26.odd_ref), channel_id=1, source_target_pairs={{2,4},{4,2},{6,8},{8,6},{10,12},{12,10},{14,16},{16,14},{18,20},{2... | collective-permute-start | bytes 1179656 | tf_op jit(solution)/shard_map/ppermute | solution.py:78
  27.5 1.4 %collective-permute-start.3 = (f32[2,96,128]{2,1,0:T(8,128)S(1)}, f32[2,96,128]{2,1,0:T(8,128)S(1)}, u32[]{:S(2)}, u32[]{:S(2)}) collective-permute-start(f32[2,96,128]{2,1,0:T(8,128)S(1)} %shard_map.48), channel_id=1, source_target_pairs={{0,1},{1,0},{2,3},{3,2},{4,5},{5,4},{6,7},{7,6},{8,9},{9,8},{10,11... | collective-permute-start | bytes 294920 | tf_op jit(solution)/shard_map/ppermute | solution.py:76
  31.2 27.0 %collective-permute-start.7 = (f32[8,96,128]{2,1,0:T(8,128)S(1)}, f32[8,96,128]{2,1,0:T(8,128)S(1)}, u32[]{:S(2)}, u32[]{:S(2)}) collective-permute-start(f32[8,96,128]{2,1,0:T(8,128)S(1)} %get-tuple-element.28.even_ref), channel_id=1, source_target_pairs={{0,2},{2,0},{4,6},{6,4},{8,10},{10,8},{12,14},{14,12},{16,18},{18,... | collective-permute-start | bytes 1179656 | tf_op jit(solution)/shard_map/ppermute | solution.py:76
  31.3 28.8 %collective-permute-start.8 = (f32[8,96,128]{2,1,0:T(8,128)S(1)}, f32[8,96,128]{2,1,0:T(8,128)S(1)}, u32[]{:S(2)}, u32[]{:S(2)}) collective-permute-start(f32[8,96,128]{2,1,0:T(8,128)S(1)} %get-tuple-element.29.odd_ref), channel_id=1, source_target_pairs={{2,4},{4,2},{6,8},{8,6},{10,12},{12,10},{14,16},{16,14},{18,20},{2... | collective-permute-start | bytes 1179656 | tf_op jit(solution)/shard_map/ppermute | solution.py:78
  51.4 1.4 %collective-permute-start.6 = (f32[2,96,128]{2,1,0:T(8,128)S(1)}, f32[2,96,128]{2,1,0:T(8,128)S(1)}, u32[]{:S(2)}, u32[]{:S(2)}) collective-permute-start(f32[2,96,128]{2,1,0:T(8,128)S(1)} %shard_map.50), channel_id=1, source_target_pairs={{0,1},{1,0},{2,3},{3,2},{4,5},{5,4},{6,7},{7,6},{8,9},{9,8},{10,11... | collective-permute-start | bytes 294920 | tf_op jit(solution)/shard_map/ppermute | solution.py:76
  55.1 19.8 %collective-permute-start.10 = (f32[8,96,128]{2,1,0:T(8,128)S(1)}, f32[8,96,128]{2,1,0:T(8,128)S(1)}, u32[]{:S(2)}, u32[]{:S(2)}) collective-permute-start(f32[8,96,128]{2,1,0:T(8,128)S(1)} %get-tuple-element.31.even_ref), channel_id=1, source_target_pairs={{0,2},{2,0},{4,6},{6,4},{8,10},{10,8},{12,14},{14,12},{16,18},{18,... | collective-permute-start | bytes 1179656 | tf_op jit(solution)/shard_map/ppermute | solution.py:76
  55.2 20.7 %collective-permute-start.11 = (f32[8,96,128]{2,1,0:T(8,128)S(1)}, f32[8,96,128]{2,1,0:T(8,128)S(1)}, u32[]{:S(2)}, u32[]{:S(2)}) collective-permute-start(f32[8,96,128]{2,1,0:T(8,128)S(1)} %get-tuple-element.32.odd_ref), channel_id=1, source_target_pairs={{2,4},{4,2},{6,8},{8,6},{10,12},{12,10},{14,16},{16,14},{18,20},{2... | collective-permute-start | bytes 1179656 | tf_op jit(solution)/shard_map/ppermute | solution.py:78
  60.8 1.4 %collective-permute-start.9 = (f32[2,96,128]{2,1,0:T(8,128)S(1)}, f32[2,96,128]{2,1,0:T(8,128)S(1)}, u32[]{:S(2)}, u32[]{:S(2)}) collective-permute-start(f32[2,96,128]{2,1,0:T(8,128)S(1)} %shard_map.52), channel_id=1, source_target_pairs={{0,1},{1,0},{2,3},{3,2},{4,5},{5,4},{6,7},{7,6},{8,9},{9,8},{10,11... | collective-permute-start | bytes 294920 | tf_op jit(solution)/shard_map/ppermute | solution.py:76

commit v2 on v1

--- a/solution.py
+++ b/solution.py
@@ -8,13 +8,13 @@
 from jax.experimental.pallas import tpu as pltpu
 from jax.sharding import PartitionSpec as P
 
+
 LMAX = 8
 ITERS = 4
 TIME_STEP = 0.5
 DIFFUSION = 0.02
 
 VMEM = pltpu.VMEM
-SMEM = pltpu.SMEM
 
 
 def double_factorial(value):
@@ -29,7 +29,7 @@
     along_x, along_y, along_z = (directions[0], directions[1], directions[2])
     cosines = [jnp.ones_like(along_x)]
     sines = [jnp.zeros_like(along_x)]
-    for order in range(1, LMAX + 1):
+    for _ in range(1, LMAX + 1):
         cosines.append(cosines[-1] * along_x - sines[-1] * along_y)
         sines.append(cosines[-2] * along_y + sines[-1] * along_x)
     legendre = {}
@@ -84,12 +84,17 @@
         self.kk, self.ny, self.nz, self.nx = shape
         self.half = self.kk // 2
         self.rows = self.ny * self.nz
+        self.chunks = 3
         self.z_two = z_peers > 2
         self.y_two = y_peers > 2
         self.layer = jax.ShapeDtypeStruct((self.ny, self.half, self.nx), jnp.float32)
         self.rest = jax.ShapeDtypeStruct((2, self.nz - 1, self.ny, self.half, self.nx), jnp.float32)
         self.edge = jax.ShapeDtypeStruct((self.nz, self.half, self.nx), jnp.float32)
         self.field = jax.ShapeDtypeStruct((self.kk * self.rows, self.nx), jnp.float32)
+
+
+def is_even(axis):
+    return lax.rem(lax.axis_index(axis), 2) == 0
 
 
 def column(table, index, shape):
@@ -120,33 +125,84 @@
             outs[1][z] = jnp.where(even, down, up)
 
 
-def open_body(plan, flags, table, field, even_ref, odd_ref, rest_ref, *edges):
+def row_to_column(row, size):
+    square = jnp.broadcast_to(row, (size, size))
+    same = lax.broadcasted_iota(jnp.int32, (size, size), 0) == lax.broadcasted_iota(
+        jnp.int32, (size, size), 1
+    )
+    return jnp.sum(jnp.where(same, square, 0.0), axis=1, keepdims=True)
+
+
+def field_copies(plan, source, target, sems):
+    copies = []
+    depth = plan.half // plan.chunks * plan.rows
+    for chunk in range(plan.chunks):
+        for member in range(2):
+            where = pl.ds((member * plan.chunks + chunk) * depth, depth)
+            copies.append(
+                pltpu.make_async_copy(source.at[where], target.at[where], sems.at[chunk, member])
+            )
+    return copies
+
+
+def load_pair(plan, held, start, size, row):
+    pair = []
+    for member in range(2):
+        base = (member * plan.half + start) * plan.rows + row
+        pair.append(held[pl.ds(base, size, stride=plan.rows), :])
+    return pair
+
+
+def send_body(plan, signs_raw, field_raw, even_ref, odd_ref, signs, field, sems, small):
+    fetch = pltpu.make_async_copy(signs_raw, signs, small)
+    fetch.start()
+    copies = field_copies(plan, field_raw, field, sems)
+    for copy in copies:
+        copy.start()
+    fetch.wait()
+    even = is_even("gz")
+    signs_z = signs[2:3, : plan.half].astype(jnp.float32)
+    turn = jnp.broadcast_to(row_to_column(signs_z, plan.half), (plan.half, plan.nx))
+    size = plan.half // plan.chunks
+    for chunk in range(plan.chunks):
+        copies[2 * chunk].wait()
+        copies[2 * chunk + 1].wait()
+        start = chunk * size
+        rising_z = turn[start : start + size] > 0
+        rows = pl.ds(start, size)
+        for y in range(plan.ny):
+            a, b = load_pair(plan, field, start, size, y * plan.nz + plan.nz - 1)
+            top = jnp.where(rising_z, a, b)
+            a, b = load_pair(plan, field, start, size, y * plan.nz)
+            bottom = jnp.where(rising_z, b, a)
+            even_ref[y, rows, :] = jnp.where(even, top, bottom)
+            odd_ref[y, rows, :] = jnp.where(even, bottom, top)
+
+
+def open_body(plan, table, field_raw, rest_ref, *refs):
+    edges, (field, sems) = refs[:-2], refs[-2:]
+    copies = field_copies(plan, field_raw, field, sems)
+    for copy in copies:
+        copy.start()
+    for copy in copies:
+        copy.wait()
     shape = (plan.half, plan.nx)
-    even = flags[0] == 0
     rising_z = column(table, 6, shape) > 0
     rising_y = column(table, 5, shape) > 0
     kept = {}
     for y in range(plan.ny):
         for z in range(plan.nz):
-            row = y * plan.nz + z
-            a = field[pl.ds(row, plan.half, stride=plan.rows), :]
-            b = field[pl.ds(row + plan.half * plan.rows, plan.half, stride=plan.rows), :]
+            a, b = load_pair(plan, field, 0, plan.half, y * plan.nz + z)
             p = jnp.where(rising_z, a, b)
             n = jnp.where(rising_z, b, a)
             if z < plan.nz - 1:
                 rest_ref[0, z, y] = p
             if z > 0:
                 rest_ref[1, z - 1, y] = n
-            if z == plan.nz - 1:
-                top = p
-            if z == 0:
-                bottom = n
             if y in (0, plan.ny - 1):
                 kept[z, y] = (p, n)
-        even_ref[y] = jnp.where(even, top, bottom)
-        odd_ref[y] = jnp.where(even, bottom, top)
     write_edges(
-        flags[1] == 0,
+        is_even("gy"),
         rising_y,
         lambda z, y: kept[z, y][0],
         lambda z, y: kept[z, y][1],
@@ -177,14 +233,14 @@
     return get_p, get_n
 
 
-def edge_body(plan, flags, table, even_ref, odd_ref, rest_ref, *refs):
+def edge_body(plan, table, even_ref, odd_ref, rest_ref, *refs):
     count = 1 + plan.z_two
     got, edges = refs[:count], refs[count:]
     shape = (plan.half, plan.nx)
     get_p, get_n = member_reader(
-        plan, flags[0] == 0, (even_ref, odd_ref, rest_ref), got, column(table, 3, shape)
-    )
-    write_edges(flags[1] == 0, column(table, 5, shape) > 0, get_p, get_n, plan, edges)
+        plan, is_even("gz"), (even_ref, odd_ref, rest_ref), got, column(table, 3, shape)
+    )
+    write_edges(is_even("gy"), column(table, 5, shape) > 0, get_p, get_n, plan, edges)
 
 
 def split(value):
@@ -193,15 +249,15 @@
     return high, low
 
 
-def step_body(plan, first, flags, table, matrix, even_ref, odd_ref, rest_ref, *refs):
+def step_body(plan, first, table, matrix, even_ref, odd_ref, rest_ref, *refs):
     z_count = 0 if first else 1 + plan.z_two
     y_count = 1 + plan.y_two
     got = None if first else refs[:z_count]
     y_got = refs[z_count : z_count + y_count]
     new_even, new_odd, new_rest, full, highs, lows, turn = refs[z_count + y_count :]
     half, nx, ny, nz = plan.half, plan.nx, plan.ny, plan.nz
-    even = flags[0] == 0
-    y_even = flags[1] == 0
+    even = is_even("gz")
+    y_even = is_even("gy")
     for part in range(half // 16):
         rows = pl.ds(part * 16, 16)
         speed_z = column(table[rows, :], 3, (16, nx))
@@ -290,32 +346,60 @@
             new_odd[y, rows, :] = jnp.where(even, bottom, top)
 
 
-def close_body(plan, flags, table, even_ref, odd_ref, rest_ref, *refs):
-    got, field = refs[:-1], refs[-1]
-    shape = (plan.half, plan.nx)
-    rising_z = column(table, 6, shape) > 0
-    get_p, get_n = member_reader(
-        plan, flags[0] == 0, (even_ref, odd_ref, rest_ref), got, column(table, 3, shape)
-    )
-    for y in range(plan.ny):
-        for z in range(plan.nz):
-            row = y * plan.nz + z
-            p = get_p(z, y)
-            n = get_n(z, y)
-            field[pl.ds(row, plan.half, stride=plan.rows), :] = jnp.where(rising_z, p, n)
-            field[pl.ds(row + plan.half * plan.rows, plan.half, stride=plan.rows), :] = jnp.where(
-                rising_z, n, p
-            )
-
-
-def call(body, outs, args, scratch=()):
-    in_specs = [pl.BlockSpec(memory_space=SMEM)] + [pl.BlockSpec(memory_space=VMEM)] * (len(args) - 1)
+def close_body(plan, table, even_ref, odd_ref, rest_ref, *refs):
+    got, (field, held, sems) = refs[:-3], refs[-3:]
+    copies = field_copies(plan, held, field, sems)
+    even = is_even("gz")
+    nz = plan.nz
+    size = plan.half // plan.chunks
+    for chunk in range(plan.chunks):
+        start = chunk * size
+        rows = pl.ds(start, size)
+        tab = table[rows, :]
+        rising_z = column(tab, 6, (size, plan.nx)) > 0
+        speed_z = column(tab, 3, (size, plan.nx))
+        for y in range(plan.ny):
+            arrived = [g[y, rows, :] for g in got]
+            low = speed_z * from_below(even, arrived)
+            high = speed_z * from_above(even, arrived)
+            one, two = even_ref[y, rows, :], odd_ref[y, rows, :]
+            for z in range(nz):
+                if z == nz - 1:
+                    p = jnp.where(even, one, two)
+                else:
+                    p = rest_ref[0, z, y, rows, :]
+                if z == 0:
+                    n = jnp.where(even, two, one)
+                else:
+                    n = rest_ref[1, z - 1, y, rows, :]
+                if z == 0:
+                    p = p + low
+                if z == nz - 1:
+                    n = n + high
+                base = start * plan.rows + y * nz + z
+                held[pl.ds(base, size, stride=plan.rows), :] = jnp.where(rising_z, p, n)
+                base = base + plan.half * plan.rows
+                held[pl.ds(base, size, stride=plan.rows), :] = jnp.where(rising_z, n, p)
+        copies[2 * chunk].start()
+        copies[2 * chunk + 1].start()
+    for copy in copies:
+        copy.wait()
+
+
+def stay(value):
+    return pltpu.with_memory_space_constraint(value, pltpu.HBM)
+
+
+def call(body, outs, args, scratch=(), raw_in=(), raw_out=False):
+    in_specs = []
+    for i in range(len(args)):
+        in_specs.append(pl.BlockSpec(memory_space=pltpu.HBM if i in raw_in else VMEM))
     moved = sum(math.prod(a.shape) * 4 for a in list(args) + list(outs))
     return pl.pallas_call(
         body,
         out_shape=outs,
         in_specs=in_specs,
-        out_specs=[pl.BlockSpec(memory_space=VMEM)] * len(outs),
+        out_specs=[pl.BlockSpec(memory_space=pltpu.HBM if raw_out else VMEM)] * len(outs),
         scratch_shapes=list(scratch),
         cost_estimate=pl.CostEstimate(flops=8 * moved, bytes_accessed=moved, transcendentals=0),
         compiler_params=pltpu.CompilerParams(vmem_limit_bytes=32 << 20),
@@ -325,7 +409,23 @@
 def shards(fodf, directions, signs):
     plan = Plan(fodf.shape, lax.axis_size("gz"), lax.axis_size("gy"))
     half = plan.half
-    flags = jnp.stack([lax.axis_index("gz") % 2, lax.axis_index("gy") % 2]).astype(jnp.int32)
+    field = fodf.reshape(plan.field.shape)
+    edge_outs = [plan.edge] * (1 + plan.y_two)
+    state_outs = [plan.layer, plan.layer, plan.rest]
+    streamed = [
+        VMEM(plan.field.shape, jnp.float32),
+        pltpu.SemaphoreType.DMA((plan.chunks, 2)),
+    ]
+    first, second = call(
+        functools.partial(send_body, plan),
+        [plan.layer, plan.layer],
+        [stay(signs), stay(field)],
+        [VMEM(signs.shape, signs.dtype), *streamed, pltpu.SemaphoreType.DMA],
+        raw_in=(0, 1),
+    )
+    later, signs, directions, first, second = lax.optimization_barrier(
+        (field, signs, directions, first, second)
+    )
     near = directions[:, :half]
     turn = signs[:, :half].astype(jnp.float32)
     speeds = TIME_STEP * jnp.abs(near)
@@ -333,26 +433,27 @@
         [1.0 - jnp.sum(speeds, 0, keepdims=True), speeds, turn[:2] * turn[2:], turn[2:]], 0
     )
     table = columns.T
-    field = fodf.reshape(plan.field.shape)
-    edge_outs = [plan.edge] * (1 + plan.y_two)
-    state_outs = [plan.layer, plan.layer, plan.rest]
     opened = call(
-        functools.partial(open_body, plan), state_outs + edge_outs, [flags, table, field]
-    )
-    state, edges = opened[:3], opened[3:]
+        functools.partial(open_body, plan),
+        [plan.rest] + edge_outs,
+        [table, stay(later)],
+        streamed,
+        raw_in=(1,),
+    )
+    state, edges = [first, second, opened[0]], opened[1:]
     matrix = angular_matrix(near)
     got = []
     for step in range(ITERS):
         if step > 0:
             edges = call(
-                functools.partial(edge_body, plan), edge_outs, [flags, table, *state, *got]
+                functools.partial(edge_body, plan), edge_outs, [table, *state, *got]
             )
         arriving = exchange(state[0], state[1], "gz")
         y_got = exchange(edges[0], edges[-1], "gy")
         state = call(
             functools.partial(step_body, plan, step == 0),
             state_outs,
-            [flags, table, matrix, *state, *got, *y_got],
+            [table, matrix, *state, *got, *y_got],
             [
                 VMEM((2, plan.nz, plan.ny + 2, half, plan.nx), jnp.float32),
                 VMEM((half, plan.rows * plan.nx), jnp.bfloat16),
@@ -362,7 +463,11 @@
         )
         got = arriving
     field = call(
-        functools.partial(close_body, plan), [plan.field], [flags, table, *state, *got]
+        functools.partial(close_body, plan),
+        [plan.field],
+        [table, *state, *got],
+        streamed,
+        raw_out=True,
     )[0]
     return field.reshape(fodf.shape)
 

time: 78.8 us -> 77.2 us (0.980)
  waiting for transfers between devices: 32.8 us -> 36.6 us
  Pallas kernels: 15.2 us -> 12.7 us
  other arithmetic: 10.5 us -> 9.07 us
  local copies, waits for them, and re-layouts: 1.76 us -> 0.36 us
    ppermute x8, waiting for transfers between devices: 29.9 us -> 34.7 us  [exchange(): got = [lax.ppermute(even_load, axis, first)]]
    pallas_call x9 -> x10, Pallas kernels: 15.2 us -> 12.7 us  [call(): pl.pallas_call(body, out_shape=outs, in_specs=in_specs, out_specs=[pl.Blo...]
    unnamed x6, local copies, waits for them, and re-layouts: 1.42 us -> 0.02 us
    ppermute x4, waiting for transfers between devices: 2.87 us -> 1.91 us  [exchange(): got.append(lax.ppermute(odd_load, axis, second))]
  transfers between devices with their start and end apart: 12 -> 12, of which waited for: 8 -> 8; matrix products, arithmetic and copies ran while one was open for 13% -> 13% of each run, Pallas kernels for 14% -> 10%
where the time goes in v2:
time: 77.2 us; the launch traced here: 77 us
  waiting for transfers between devices  36.6 us (47%)
  starting transfers between devices  17.1 us (22%)
  Pallas kernels  12.7 us (16%)
  other arithmetic  9.07 us (12%)
  matrix products  0.88 us (1%)
    ppermute x8, waiting for transfers between devices, exchange(): got = [lax.ppermute(even_load, axis, first)]  34.7 us
    ppermute x4, starting transfers between devices, exchange(): got.append(lax.ppermute(odd_load, axis, second))  16.5 us
    pallas_call x10, Pallas kernels, call(): pl.pallas_call(body, out_shape=outs, in_specs=in_specs, out_specs=[pl.Blo...  12.7 us
    another operation x3, other arithmetic, angular_matrix(): chol_lower = jnp.linalg.cholesky(gram)  4.78 us
    another operation x2, other arithmetic, angular_matrix(): lax.linalg.triangular_solve(chol_lower, partial_solve, left_side=True, lo...  4.1 us
    ppermute x4, waiting for transfers between devices, exchange(): got.append(lax.ppermute(odd_load, axis, second))  1.91 us
  transfers between devices with their start and end apart: 12, of which 8 were waited for; matrix products, arithmetic and copies ran while one was open for 13% of the time, Pallas kernels for 10%

profile of v2, /device:TPU:2, one launch (start us, length us, event | category | flops | bytes accessed | tf_op | source)
XLA Modules:
  0.0 77.0 jit_solution(10458571203378750912)
XLA Ops:
  0.0 1.8 %shard_map.46 = (f32[8,96,128]{2,1,0:T(8,128)S(1)}, f32[8,96,128]{2,1,0:T(8,128)S(1)}) custom-call(s32[3,192]{1,0:T(4,128)} %signs_raw.1, f32[3072,128]{1,0:T(8,128)} %bitcast.30), custom_call_target="tpu_custom_call" | custom-call | flops 18892800 | bytes 2361600 | tf_op jit(solution)/shard_map/pallas_call | solution.py:398
  2.0 1.9 %shard_map.47 = (f32[2,1,8,96,128]{4,3,2,1,0:T(8,128)S(1)}, f32[2,96,128]{2,1,0:T(8,128)S(1)}) custom-call(f32[96,7]{1,0:T(8,128)S(1)} %bitcast.21, f32[3072,128]{1,0:T(8,128)} %bitcast.31), custom_call_target="tpu_custom_call" | custom-call | flops 19682304 | bytes 2460288 | tf_op jit(solution)/shard_map/pallas_call | solution.py:398
  4.0 4.9 %collective-permute-start.2 = (f32[8,96,128]{2,1,0:T(8,128)S(1)}, f32[8,96,128]{2,1,0:T(8,128)S(1)}, u32[]{:S(2)}, u32[]{:S(2)}) collective-permute-start(f32[8,96,128]{2,1,0:T(8,128)S(1)} %get-tuple-element.31.odd_ref), channel_id=1, source_target_pairs={{2,4},{4,2},{6,8},{8,6},{10,12},{12,10},{14,16},{16,14},{18,20},{2... | collective-permute-start | bytes 1179656 | tf_op jit(solution)/shard_map/ppermute | solution.py:78
  9.5 4.1 %cholesky.16 = f32[45,45]{1,0:T(8,128)S(1)} custom-call(f32[45,45]{1,0:T(8,128)S(1)} %bitcast_add_fusion), custom_call_target="Cholesky" | custom-call | tf_op jit(solution)/shard_map/jit(cholesky)/cholesky | solution.py:63
  13.7 0.6 compare_reduce_fusion
  14.3 0.7 fusion
  15.0 3.4 %custom-call.8 = f32[1,45,45]{1,2,0:T(8,128)S(1)} custom-call(f32[1,45,45]{2,1,0:T(8,128)S(1)} %fusion), custom_call_target="InvertDiagBlocksLowerTriangular" | custom-call | tf_op jit(solution)/shard_map/triangular_solve | solution.py:65
  18.8 0.3 fusion.5.matrix
  19.2 1.7 %shard_map.48 = (f32[8,96,128]{2,1,0:T(8,128)S(1)}, f32[8,96,128]{2,1,0:T(8,128)S(1)}, f32[2,1,8,96,128]{4,3,2,1,0:T(8,128)S(1)}) custom-call(f32[96,7]{1,0:T(8,128)S(1)} %bitcast.22, f32[96,96]{1,0:T(8,128)S(1)} %fusion.5.matrix, f32[8,96,128]{2,1,0:T(8,128)S(1)} %get-tuple-element.30.even_ref, f32[8,96,128]{2,1,0:T(8,128)S(1)} %get-tuple-element.31.odd_ref, ...), custom_call_target="tpu_custom_call" | custom-call | flops 26268672 | bytes 3283584 | tf_op jit(solution)/shard_map/pallas_call | solution.py:398
  20.9 4.9 %collective-permute-start.5 = (f32[8,96,128]{2,1,0:T(8,128)S(1)}, f32[8,96,128]{2,1,0:T(8,128)S(1)}, u32[]{:S(2)}, u32[]{:S(2)}) collective-permute-start(f32[8,96,128]{2,1,0:T(8,128)S(1)} %get-tuple-element.36.odd_ref), channel_id=1, source_target_pairs={{2,4},{4,2},{6,8},{8,6},{10,12},{12,10},{14,16},{16,14},{18,20},{2... | collective-permute-start | bytes 1179656 | tf_op jit(solution)/shard_map/ppermute | solution.py:78
  26.0 1.3 %collective-permute-done.3.refs_2_ = f32[2,96,128]{2,1,0:T(8,128)S(1)} collective-permute-done((f32[2,96,128]{2,1,0:T(8,128)S(1)}, f32[2,96,128]{2,1,0:T(8,128)S(1)}, u32[]{:S(2)}, u32[]{:S(2)}) %collective-permute-start.3) | collective-permute-done | bytes 98336 | tf_op jit(solution)/shard_map/ppermute | solution.py:76
  27.3 1.8 %shard_map.50 = (f32[8,96,128]{2,1,0:T(8,128)S(1)}, f32[8,96,128]{2,1,0:T(8,128)S(1)}, f32[2,1,8,96,128]{4,3,2,1,0:T(8,128)S(1)}) custom-call(f32[96,7]{1,0:T(8,128)S(1)} %bitcast.24, f32[96,96]{1,0:T(8,128)S(1)} %fusion.5.matrix, f32[8,96,128]{2,1,0:T(8,128)S(1)} %get-tuple-element.35.even_ref, f32[8,96,128]{2,1,0:T(8,128)S(1)} %get-tuple-element.36.odd_ref, ...), custom_call_target="tpu_custom_call" | custom-call | flops 32560128 | bytes 4070016 | tf_op jit(solution)/shard_map/pallas_call | solution.py:398
  29.2 4.9 %collective-permute-start.8 = (f32[8,96,128]{2,1,0:T(8,128)S(1)}, f32[8,96,128]{2,1,0:T(8,128)S(1)}, u32[]{:S(2)}, u32[]{:S(2)}) collective-permute-start(f32[8,96,128]{2,1,0:T(8,128)S(1)} %get-tuple-element.39.odd_ref), channel_id=1, source_target_pairs={{2,4},{4,2},{6,8},{8,6},{10,12},{12,10},{14,16},{16,14},{18,20},{2... | collective-permute-start | bytes 1179656 | tf_op jit(solution)/shard_map/ppermute | solution.py:78
  34.1 15.7 %collective-permute-done.4.refs_0_ = f32[8,96,128]{2,1,0:T(8,128)S(1)} collective-permute-done((f32[8,96,128]{2,1,0:T(8,128)S(1)}, f32[8,96,128]{2,1,0:T(8,128)S(1)}, u32[]{:S(2)}, u32[]{:S(2)}) %collective-permute-start.4) | collective-permute-done | bytes 393248 | tf_op jit(solution)/shard_map/ppermute | solution.py:76
  49.9 1.3 %collective-permute-done.6.refs_2_ = f32[2,96,128]{2,1,0:T(8,128)S(1)} collective-permute-done((f32[2,96,128]{2,1,0:T(8,128)S(1)}, f32[2,96,128]{2,1,0:T(8,128)S(1)}, u32[]{:S(2)}, u32[]{:S(2)}) %collective-permute-start.6) | collective-permute-done | bytes 98336 | tf_op jit(solution)/shard_map/ppermute | solution.py:76
  51.2 1.8 %shard_map.52 = (f32[8,96,128]{2,1,0:T(8,128)S(1)}, f32[8,96,128]{2,1,0:T(8,128)S(1)}, f32[2,1,8,96,128]{4,3,2,1,0:T(8,128)S(1)}) custom-call(f32[96,7]{1,0:T(8,128)S(1)} %bitcast.26, f32[96,96]{1,0:T(8,128)S(1)} %fusion.5.matrix, f32[8,96,128]{2,1,0:T(8,128)S(1)} %get-tuple-element.38.even_ref, f32[8,96,128]{2,1,0:T(8,128)S(1)} %get-tuple-element.39.odd_ref, ...), custom_call_target="tpu_custom_call" | custom-call | flops 32560128 | bytes 4070016 | tf_op jit(solution)/shard_map/pallas_call | solution.py:398
  53.1 1.9 %collective-permute-start.11 = (f32[8,96,128]{2,1,0:T(8,128)S(1)}, f32[8,96,128]{2,1,0:T(8,128)S(1)}, u32[]{:S(2)}, u32[]{:S(2)}) collective-permute-start(f32[8,96,128]{2,1,0:T(8,128)S(1)} %get-tuple-element.42.odd_ref), channel_id=1, source_target_pairs={{2,4},{4,2},{6,8},{8,6},{10,12},{12,10},{14,16},{16,14},{18,20},{2... | collective-permute-start | bytes 1179656 | tf_op jit(solution)/shard_map/ppermute | solution.py:78
  55.1 3.1 %collective-permute-done.7.refs_0_ = f32[8,96,128]{2,1,0:T(8,128)S(1)} collective-permute-done((f32[8,96,128]{2,1,0:T(8,128)S(1)}, f32[8,96,128]{2,1,0:T(8,128)S(1)}, u32[]{:S(2)}, u32[]{:S(2)}) %collective-permute-start.7) | collective-permute-done | bytes 393248 | tf_op jit(solution)/shard_map/ppermute | solution.py:76
  58.2 1.0 %collective-permute-done.8.refs_1_ = f32[8,96,128]{2,1,0:T(8,128)S(1)} collective-permute-done((f32[8,96,128]{2,1,0:T(8,128)S(1)}, f32[8,96,128]{2,1,0:T(8,128)S(1)}, u32[]{:S(2)}, u32[]{:S(2)}) %collective-permute-start.8) | collective-permute-done | bytes 393248 | tf_op jit(solution)/shard_map/ppermute | solution.py:78
  59.3 1.3 %collective-permute-done.9.refs_2_ = f32[2,96,128]{2,1,0:T(8,128)S(1)} collective-permute-done((f32[2,96,128]{2,1,0:T(8,128)S(1)}, f32[2,96,128]{2,1,0:T(8,128)S(1)}, u32[]{:S(2)}, u32[]{:S(2)}) %collective-permute-start.9) | collective-permute-done | bytes 98336 | tf_op jit(solution)/shard_map/ppermute | solution.py:76
  60.6 1.8 %shard_map.54 = (f32[8,96,128]{2,1,0:T(8,128)S(1)}, f32[8,96,128]{2,1,0:T(8,128)S(1)}, f32[2,1,8,96,128]{4,3,2,1,0:T(8,128)S(1)}) custom-call(f32[96,7]{1,0:T(8,128)S(1)} %bitcast.28, f32[96,96]{1,0:T(8,128)S(1)} %fusion.5.matrix, f32[8,96,128]{2,1,0:T(8,128)S(1)} %get-tuple-element.41.even_ref, f32[8,96,128]{2,1,0:T(8,128)S(1)} %get-tuple-element.42.odd_ref, ...), custom_call_target="tpu_custom_call" | custom-call | flops 32560128 | bytes 4070016 | tf_op jit(solution)/shard_map/pallas_call | solution.py:398
  62.4 12.0 %collective-permute-done.10.refs_0_ = f32[8,96,128]{2,1,0:T(8,128)S(1)} collective-permute-done((f32[8,96,128]{2,1,0:T(8,128)S(1)}, f32[8,96,128]{2,1,0:T(8,128)S(1)}, u32[]{:S(2)}, u32[]{:S(2)}) %collective-permute-start.10) | collective-permute-done | bytes 393248 | tf_op jit(solution)/shard_map/ppermute | solution.py:76
  74.5 1.0 %collective-permute-done.11.refs_1_ = f32[8,96,128]{2,1,0:T(8,128)S(1)} collective-permute-done((f32[8,96,128]{2,1,0:T(8,128)S(1)}, f32[8,96,128]{2,1,0:T(8,128)S(1)}, u32[]{:S(2)}, u32[]{:S(2)}) %collective-permute-start.11) | collective-permute-done | bytes 393248 | tf_op jit(solution)/shard_map/ppermute | solution.py:78
  75.4 1.6 %shard_map.55 = f32[3072,128]{1,0:T(8,128)} custom-call(f32[96,7]{1,0:T(8,128)S(1)} %bitcast.29, f32[8,96,128]{2,1,0:T(8,128)S(1)} %get-tuple-element.44.even_ref, f32[8,96,128]{2,1,0:T(8,128)S(1)} %get-tuple-element.45.odd_ref, f32[2,1,8,96,128]{4,3,2,1,0:T(8,128)S(1)} %get-tuple-element.46.rest_ref, f32[8,96,128]{2,1,0:T(8,128)S(1)} %collective-permute-done.10.refs_0_, ...), custom_call_target="tpu_custom_call" | custom-call | flops 31478784 | bytes 3934848 | tf_op jit(solution)/shard_map/pallas_call | solution.py:398
  (44 shorter events, 2.0 us)
Async XLA Ops:
  0.0 1.8 %copy-start.1 = (s32[3,192]{1,0:T(4,128)S(1)}, s32[3,192]{1,0:T(4,128)}, u32[]{:S(2)}) copy-start(s32[3,192]{1,0:T(4,128)} %signs_raw.1) | copy-start | bytes 6916
  0.0 1.8 %copy-start = (f32[3,192]{1,0:T(4,128)S(1)}, f32[3,192]{1,0:T(4,128)}, u32[]{:S(2)}) copy-start(f32[3,192]{1,0:T(4,128)} %param.5) | copy-start | bytes 6916
  1.8 17.0 %copy-start.2 = (f32[45]{0:T(128)S(1)}, f32[45]{0:T(128)}, u32[]{:S(2)}) copy-start(f32[45]{0:T(128)} %constant.247) | copy-start | bytes 544
  3.9 15.3 %collective-permute-start = (f32[2,96,128]{2,1,0:T(8,128)S(1)}, f32[2,96,128]{2,1,0:T(8,128)S(1)}, u32[]{:S(2)}, u32[]{:S(2)}) collective-permute-start(f32[2,96,128]{2,1,0:T(8,128)S(1)} %get-tuple-element.34), channel_id=1, source_target_pairs={{0,1},{1,0},{2,3},{3,2},{4,5},{5,4},{6,7},{7,6},{8,9},{9,8},{10,11... | collective-permute-start | bytes 294920 | tf_op jit(solution)/shard_map/ppermute | solution.py:76
  4.0 21.8 %collective-permute-start.1 = (f32[8,96,128]{2,1,0:T(8,128)S(1)}, f32[8,96,128]{2,1,0:T(8,128)S(1)}, u32[]{:S(2)}, u32[]{:S(2)}) collective-permute-start(f32[8,96,128]{2,1,0:T(8,128)S(1)} %get-tuple-element.30.even_ref), channel_id=1, source_target_pairs={{0,2},{2,0},{4,6},{6,4},{8,10},{10,8},{12,14},{14,12},{16,18},{18,... | collective-permute-start | bytes 1179656 | tf_op jit(solution)/shard_map/ppermute | solution.py:76
  4.0 21.7 %collective-permute-start.2 = (f32[8,96,128]{2,1,0:T(8,128)S(1)}, f32[8,96,128]{2,1,0:T(8,128)S(1)}, u32[]{:S(2)}, u32[]{:S(2)}) collective-permute-start(f32[8,96,128]{2,1,0:T(8,128)S(1)} %get-tuple-element.31.odd_ref), channel_id=1, source_target_pairs={{2,4},{4,2},{6,8},{8,6},{10,12},{12,10},{14,16},{16,14},{18,20},{2... | collective-permute-start | bytes 1179656 | tf_op jit(solution)/shard_map/ppermute | solution.py:78
  20.8 28.9 %collective-permute-start.4 = (f32[8,96,128]{2,1,0:T(8,128)S(1)}, f32[8,96,128]{2,1,0:T(8,128)S(1)}, u32[]{:S(2)}, u32[]{:S(2)}) collective-permute-start(f32[8,96,128]{2,1,0:T(8,128)S(1)} %get-tuple-element.35.even_ref), channel_id=1, source_target_pairs={{0,2},{2,0},{4,6},{6,4},{8,10},{10,8},{12,14},{14,12},{16,18},{18,... | collective-permute-start | bytes 1179656 | tf_op jit(solution)/shard_map/ppermute | solution.py:76
  20.9 28.8 %collective-permute-start.5 = (f32[8,96,128]{2,1,0:T(8,128)S(1)}, f32[8,96,128]{2,1,0:T(8,128)S(1)}, u32[]{:S(2)}, u32[]{:S(2)}) collective-permute-start(f32[8,96,128]{2,1,0:T(8,128)S(1)} %get-tuple-element.36.odd_ref), channel_id=1, source_target_pairs={{2,4},{4,2},{6,8},{8,6},{10,12},{12,10},{14,16},{16,14},{18,20},{2... | collective-permute-start | bytes 1179656 | tf_op jit(solution)/shard_map/ppermute | solution.py:78
  25.9 1.4 %collective-permute-start.3 = (f32[2,96,128]{2,1,0:T(8,128)S(1)}, f32[2,96,128]{2,1,0:T(8,128)S(1)}, u32[]{:S(2)}, u32[]{:S(2)}) collective-permute-start(f32[2,96,128]{2,1,0:T(8,128)S(1)} %shard_map.49), channel_id=1, source_target_pairs={{0,1},{1,0},{2,3},{3,2},{4,5},{5,4},{6,7},{7,6},{8,9},{9,8},{10,11... | collective-permute-start | bytes 294920 | tf_op jit(solution)/shard_map/ppermute | solution.py:76
  29.1 29.0 %collective-permute-start.7 = (f32[8,96,128]{2,1,0:T(8,128)S(1)}, f32[8,96,128]{2,1,0:T(8,128)S(1)}, u32[]{:S(2)}, u32[]{:S(2)}) collective-permute-start(f32[8,96,128]{2,1,0:T(8,128)S(1)} %get-tuple-element.38.even_ref), channel_id=1, source_target_pairs={{0,2},{2,0},{4,6},{6,4},{8,10},{10,8},{12,14},{14,12},{16,18},{18,... | collective-permute-start | bytes 1179656 | tf_op jit(solution)/shard_map/ppermute | solution.py:76
  29.2 29.9 %collective-permute-start.8 = (f32[8,96,128]{2,1,0:T(8,128)S(1)}, f32[8,96,128]{2,1,0:T(8,128)S(1)}, u32[]{:S(2)}, u32[]{:S(2)}) collective-permute-start(f32[8,96,128]{2,1,0:T(8,128)S(1)} %get-tuple-element.39.odd_ref), channel_id=1, source_target_pairs={{2,4},{4,2},{6,8},{8,6},{10,12},{12,10},{14,16},{16,14},{18,20},{2... | collective-permute-start | bytes 1179656 | tf_op jit(solution)/shard_map/ppermute | solution.py:78
  49.8 1.4 %collective-permute-start.6 = (f32[2,96,128]{2,1,0:T(8,128)S(1)}, f32[2,96,128]{2,1,0:T(8,128)S(1)}, u32[]{:S(2)}, u32[]{:S(2)}) collective-permute-start(f32[2,96,128]{2,1,0:T(8,128)S(1)} %shard_map.51), channel_id=1, source_target_pairs={{0,1},{1,0},{2,3},{3,2},{4,5},{5,4},{6,7},{7,6},{8,9},{9,8},{10,11... | collective-permute-start | bytes 294920 | tf_op jit(solution)/shard_map/ppermute | solution.py:76
  53.0 21.4 %collective-permute-start.10 = (f32[8,96,128]{2,1,0:T(8,128)S(1)}, f32[8,96,128]{2,1,0:T(8,128)S(1)}, u32[]{:S(2)}, u32[]{:S(2)}) collective-permute-start(f32[8,96,128]{2,1,0:T(8,128)S(1)} %get-tuple-element.41.even_ref), channel_id=1, source_target_pairs={{0,2},{2,0},{4,6},{6,4},{8,10},{10,8},{12,14},{14,12},{16,18},{18,... | collective-permute-start | bytes 1179656 | tf_op jit(solution)/shard_map/ppermute | solution.py:76
  53.1 22.3 %collective-permute-start.11 = (f32[8,96,128]{2,1,0:T(8,128)S(1)}, f32[8,96,128]{2,1,0:T(8,128)S(1)}, u32[]{:S(2)}, u32[]{:S(2)}) collective-permute-start(f32[8,96,128]{2,1,0:T(8,128)S(1)} %get-tuple-element.42.odd_ref), channel_id=1, source_target_pairs={{2,4},{4,2},{6,8},{8,6},{10,12},{12,10},{14,16},{16,14},{18,20},{2... | collective-permute-start | bytes 1179656 | tf_op jit(solution)/shard_map/ppermute | solution.py:78
  59.2 1.4 %collective-permute-start.9 = (f32[2,96,128]{2,1,0:T(8,128)S(1)}, f32[2,96,128]{2,1,0:T(8,128)S(1)}, u32[]{:S(2)}, u32[]{:S(2)}) collective-permute-start(f32[2,96,128]{2,1,0:T(8,128)S(1)} %shard_map.53), channel_id=1, source_target_pairs={{0,1},{1,0},{2,3},{3,2},{4,5},{5,4},{6,7},{7,6},{8,9},{9,8},{10,11... | collective-permute-start | bytes 294920 | tf_op jit(solution)/shard_map/ppermute | solution.py:76

commit v3 on v2

--- a/solution.py
+++ b/solution.py
@@ -153,7 +153,7 @@
     return pair
 
 
-def send_body(plan, signs_raw, field_raw, even_ref, odd_ref, signs, field, sems, small):
+def send_body(plan, signs_raw, field_raw, even_ref, odd_ref, rest_ref, signs, field, sems, small):
     fetch = pltpu.make_async_copy(signs_raw, signs, small)
     fetch.start()
     copies = field_copies(plan, field_raw, field, sems)
@@ -171,44 +171,20 @@
         rising_z = turn[start : start + size] > 0
         rows = pl.ds(start, size)
         for y in range(plan.ny):
-            a, b = load_pair(plan, field, start, size, y * plan.nz + plan.nz - 1)
-            top = jnp.where(rising_z, a, b)
-            a, b = load_pair(plan, field, start, size, y * plan.nz)
-            bottom = jnp.where(rising_z, b, a)
+            for z in range(plan.nz):
+                a, b = load_pair(plan, field, start, size, y * plan.nz + z)
+                p = jnp.where(rising_z, a, b)
+                n = jnp.where(rising_z, b, a)
+                if z < plan.nz - 1:
+                    rest_ref[0, z, y, rows, :] = p
+                else:
+                    top = p
+                if z > 0:
+                    rest_ref[1, z - 1, y, rows, :] = n
+                else:
+                    bottom = n
             even_ref[y, rows, :] = jnp.where(even, top, bottom)
             odd_ref[y, rows, :] = jnp.where(even, bottom, top)
-
-
-def open_body(plan, table, field_raw, rest_ref, *refs):
-    edges, (field, sems) = refs[:-2], refs[-2:]
-    copies = field_copies(plan, field_raw, field, sems)
-    for copy in copies:
-        copy.start()
-    for copy in copies:
-        copy.wait()
-    shape = (plan.half, plan.nx)
-    rising_z = column(table, 6, shape) > 0
-    rising_y = column(table, 5, shape) > 0
-    kept = {}
-    for y in range(plan.ny):
-        for z in range(plan.nz):
-            a, b = load_pair(plan, field, 0, plan.half, y * plan.nz + z)
-            p = jnp.where(rising_z, a, b)
-            n = jnp.where(rising_z, b, a)
-            if z < plan.nz - 1:
-                rest_ref[0, z, y] = p
-            if z > 0:
-                rest_ref[1, z - 1, y] = n
-            if y in (0, plan.ny - 1):
-                kept[z, y] = (p, n)
-    write_edges(
-        is_even("gy"),
-        rising_y,
-        lambda z, y: kept[z, y][0],
-        lambda z, y: kept[z, y][1],
-        plan,
-        edges,
-    )
 
 
 def member_reader(plan, even, state, got, speed_z):
@@ -233,9 +209,9 @@
     return get_p, get_n
 
 
-def edge_body(plan, table, even_ref, odd_ref, rest_ref, *refs):
-    count = 1 + plan.z_two
-    got, edges = refs[:count], refs[count:]
+def edge_body(plan, first, table, even_ref, odd_ref, rest_ref, *refs):
+    count = 0 if first else 1 + plan.z_two
+    got, edges = refs[:count] or None, refs[count:]
     shape = (plan.half, plan.nx)
     get_p, get_n = member_reader(
         plan, is_even("gz"), (even_ref, odd_ref, rest_ref), got, column(table, 3, shape)
@@ -416,16 +392,14 @@
         VMEM(plan.field.shape, jnp.float32),
         pltpu.SemaphoreType.DMA((plan.chunks, 2)),
     ]
-    first, second = call(
+    state = call(
         functools.partial(send_body, plan),
-        [plan.layer, plan.layer],
+        [plan.layer, plan.layer, plan.rest],
         [stay(signs), stay(field)],
         [VMEM(signs.shape, signs.dtype), *streamed, pltpu.SemaphoreType.DMA],
         raw_in=(0, 1),
     )
-    later, signs, directions, first, second = lax.optimization_barrier(
-        (field, signs, directions, first, second)
-    )
+    signs, directions, *state = lax.optimization_barrier((signs, directions, *state))
     near = directions[:, :half]
     turn = signs[:, :half].astype(jnp.float32)
     speeds = TIME_STEP * jnp.abs(near)
@@ -433,21 +407,12 @@
         [1.0 - jnp.sum(speeds, 0, keepdims=True), speeds, turn[:2] * turn[2:], turn[2:]], 0
     )
     table = columns.T
-    opened = call(
-        functools.partial(open_body, plan),
-        [plan.rest] + edge_outs,
-        [table, stay(later)],
-        streamed,
-        raw_in=(1,),
-    )
-    state, edges = [first, second, opened[0]], opened[1:]
     matrix = angular_matrix(near)
     got = []
     for step in range(ITERS):
-        if step > 0:
-            edges = call(
-                functools.partial(edge_body, plan), edge_outs, [table, *state, *got]
-            )
+        edges = call(
+            functools.partial(edge_body, plan, step == 0), edge_outs, [table, *state, *got]
+        )
         arriving = exchange(state[0], state[1], "gz")
         y_got = exchange(edges[0], edges[-1], "gy")
         state = call(

time: 77.2 us -> 75.5 us (0.978)
  Pallas kernels: 12.7 us -> 10.9 us
    pallas_call x10, Pallas kernels: 12.7 us -> 10.9 us  [call(): pl.pallas_call(body, out_shape=outs, in_specs=in_specs, out_specs=[pl.Blo...]
  transfers between devices with their start and end apart: 12 -> 12, of which waited for: 8 -> 8; matrix products, arithmetic and copies ran while one was open for 13% -> 14% of each run, Pallas kernels for 10% -> 10%
where the time goes in v3:
time: 75.5 us; the launch traced here: 75.3 us
  waiting for transfers between devices  36.7 us (49%)
  starting transfers between devices  17.1 us (23%)
  Pallas kernels  10.9 us (14%)
  other arithmetic  9.07 us (12%)
  matrix products  0.88 us (1%)
    ppermute x8, waiting for transfers between devices, exchange(): got = [lax.ppermute(even_load, axis, first)]  34.7 us
    ppermute x4, starting transfers between devices, exchange(): got.append(lax.ppermute(odd_load, axis, second))  16.5 us
    pallas_call x10, Pallas kernels, call(): pl.pallas_call(body, out_shape=outs, in_specs=in_specs, out_specs=[pl.Blo...  10.9 us
    another operation x3, other arithmetic, angular_matrix(): chol_lower = jnp.linalg.cholesky(gram)  4.78 us
    another operation x2, other arithmetic, angular_matrix(): lax.linalg.triangular_solve(chol_lower, partial_solve, left_side=True, lo...  4.1 us
    ppermute x4, waiting for transfers between devices, exchange(): got.append(lax.ppermute(odd_load, axis, second))  1.91 us
  transfers between devices with their start and end apart: 12, of which 8 were waited for; matrix products, arithmetic and copies ran while one was open for 14% of the time, Pallas kernels for 10%

profile of v3, /device:TPU:2, one launch (start us, length us, event | category | flops | bytes accessed | tf_op | source)
XLA Modules:
  0.0 75.3 jit_solution(16556244255557145402)
XLA Ops:
  0.0 1.8 %shard_map.46 = (f32[8,96,128]{2,1,0:T(8,128)S(1)}, f32[8,96,128]{2,1,0:T(8,128)S(1)}, f32[2,1,8,96,128]{4,3,2,1,0:T(8,128)S(1)}) custom-call(s32[3,192]{1,0:T(4,128)} %signs_raw.1, f32[3072,128]{1,0:T(8,128)} %bitcast.30), custom_call_target="tpu_custom_call" | custom-call | flops 25184256 | bytes 3148032 | tf_op jit(solution)/shard_map/pallas_call | solution.py:374
  1.9 4.9 %collective-permute-start.2 = (f32[8,96,128]{2,1,0:T(8,128)S(1)}, f32[8,96,128]{2,1,0:T(8,128)S(1)}, u32[]{:S(2)}, u32[]{:S(2)}) collective-permute-start(f32[8,96,128]{2,1,0:T(8,128)S(1)} %get-tuple-element.31.odd_ref), channel_id=1, source_target_pairs={{2,4},{4,2},{6,8},{8,6},{10,12},{12,10},{14,16},{16,14},{18,20},{2... | collective-permute-start | bytes 1179656 | tf_op jit(solution)/shard_map/ppermute | solution.py:78
  7.8 4.1 %cholesky.16 = f32[45,45]{1,0:T(8,128)S(1)} custom-call(f32[45,45]{1,0:T(8,128)S(1)} %bitcast_add_fusion), custom_call_target="Cholesky" | custom-call | tf_op jit(solution)/shard_map/jit(cholesky)/cholesky | solution.py:63
  11.9 0.6 compare_reduce_fusion
  12.6 0.7 fusion
  13.2 3.4 %custom-call.8 = f32[1,45,45]{1,2,0:T(8,128)S(1)} custom-call(f32[1,45,45]{2,1,0:T(8,128)S(1)} %fusion), custom_call_target="InvertDiagBlocksLowerTriangular" | custom-call | tf_op jit(solution)/shard_map/triangular_solve | solution.py:65
  16.7 0.2 fusion.3
  17.1 0.3 fusion.5.matrix
  17.4 1.7 %shard_map.48 = (f32[8,96,128]{2,1,0:T(8,128)S(1)}, f32[8,96,128]{2,1,0:T(8,128)S(1)}, f32[2,1,8,96,128]{4,3,2,1,0:T(8,128)S(1)}) custom-call(f32[96,7]{1,0:T(8,128)S(1)} %bitcast.22, f32[96,96]{1,0:T(8,128)S(1)} %fusion.5.matrix, f32[8,96,128]{2,1,0:T(8,128)S(1)} %get-tuple-element.30.even_ref, f32[8,96,128]{2,1,0:T(8,128)S(1)} %get-tuple-element.31.odd_ref, ...), custom_call_target="tpu_custom_call" | custom-call | flops 26268672 | bytes 3283584 | tf_op jit(solution)/shard_map/pallas_call | solution.py:374
  19.2 4.9 %collective-permute-start.5 = (f32[8,96,128]{2,1,0:T(8,128)S(1)}, f32[8,96,128]{2,1,0:T(8,128)S(1)}, u32[]{:S(2)}, u32[]{:S(2)}) collective-permute-start(f32[8,96,128]{2,1,0:T(8,128)S(1)} %get-tuple-element.34.odd_ref), channel_id=1, source_target_pairs={{2,4},{4,2},{6,8},{8,6},{10,12},{12,10},{14,16},{16,14},{18,20},{2... | collective-permute-start | bytes 1179656 | tf_op jit(solution)/shard_map/ppermute | solution.py:78
  24.3 1.3 %collective-permute-done.3.refs_2_ = f32[2,96,128]{2,1,0:T(8,128)S(1)} collective-permute-done((f32[2,96,128]{2,1,0:T(8,128)S(1)}, f32[2,96,128]{2,1,0:T(8,128)S(1)}, u32[]{:S(2)}, u32[]{:S(2)}) %collective-permute-start.3) | collective-permute-done | bytes 98336 | tf_op jit(solution)/shard_map/ppermute | solution.py:76
  25.5 1.8 %shard_map.50 = (f32[8,96,128]{2,1,0:T(8,128)S(1)}, f32[8,96,128]{2,1,0:T(8,128)S(1)}, f32[2,1,8,96,128]{4,3,2,1,0:T(8,128)S(1)}) custom-call(f32[96,7]{1,0:T(8,128)S(1)} %bitcast.24, f32[96,96]{1,0:T(8,128)S(1)} %fusion.5.matrix, f32[8,96,128]{2,1,0:T(8,128)S(1)} %get-tuple-element.33.even_ref, f32[8,96,128]{2,1,0:T(8,128)S(1)} %get-tuple-element.34.odd_ref, ...), custom_call_target="tpu_custom_call" | custom-call | flops 32560128 | bytes 4070016 | tf_op jit(solution)/shard_map/pallas_call | solution.py:374
  27.5 4.9 %collective-permute-start.8 = (f32[8,96,128]{2,1,0:T(8,128)S(1)}, f32[8,96,128]{2,1,0:T(8,128)S(1)}, u32[]{:S(2)}, u32[]{:S(2)}) collective-permute-start(f32[8,96,128]{2,1,0:T(8,128)S(1)} %get-tuple-element.37.odd_ref), channel_id=1, source_target_pairs={{2,4},{4,2},{6,8},{8,6},{10,12},{12,10},{14,16},{16,14},{18,20},{2... | collective-permute-start | bytes 1179656 | tf_op jit(solution)/shard_map/ppermute | solution.py:78
  32.3 15.7 %collective-permute-done.4.refs_0_ = f32[8,96,128]{2,1,0:T(8,128)S(1)} collective-permute-done((f32[8,96,128]{2,1,0:T(8,128)S(1)}, f32[8,96,128]{2,1,0:T(8,128)S(1)}, u32[]{:S(2)}, u32[]{:S(2)}) %collective-permute-start.4) | collective-permute-done | bytes 393248 | tf_op jit(solution)/shard_map/ppermute | solution.py:76
  48.2 1.3 %collective-permute-done.6.refs_2_ = f32[2,96,128]{2,1,0:T(8,128)S(1)} collective-permute-done((f32[2,96,128]{2,1,0:T(8,128)S(1)}, f32[2,96,128]{2,1,0:T(8,128)S(1)}, u32[]{:S(2)}, u32[]{:S(2)}) %collective-permute-start.6) | collective-permute-done | bytes 98336 | tf_op jit(solution)/shard_map/ppermute | solution.py:76
  49.5 1.8 %shard_map.52 = (f32[8,96,128]{2,1,0:T(8,128)S(1)}, f32[8,96,128]{2,1,0:T(8,128)S(1)}, f32[2,1,8,96,128]{4,3,2,1,0:T(8,128)S(1)}) custom-call(f32[96,7]{1,0:T(8,128)S(1)} %bitcast.26, f32[96,96]{1,0:T(8,128)S(1)} %fusion.5.matrix, f32[8,96,128]{2,1,0:T(8,128)S(1)} %get-tuple-element.36.even_ref, f32[8,96,128]{2,1,0:T(8,128)S(1)} %get-tuple-element.37.odd_ref, ...), custom_call_target="tpu_custom_call" | custom-call | flops 32560128 | bytes 4070016 | tf_op jit(solution)/shard_map/pallas_call | solution.py:374
  51.4 1.9 %collective-permute-start.11 = (f32[8,96,128]{2,1,0:T(8,128)S(1)}, f32[8,96,128]{2,1,0:T(8,128)S(1)}, u32[]{:S(2)}, u32[]{:S(2)}) collective-permute-start(f32[8,96,128]{2,1,0:T(8,128)S(1)} %get-tuple-element.40.odd_ref), channel_id=1, source_target_pairs={{2,4},{4,2},{6,8},{8,6},{10,12},{12,10},{14,16},{16,14},{18,20},{2... | collective-permute-start | bytes 1179656 | tf_op jit(solution)/shard_map/ppermute | solution.py:78
  53.3 3.1 %collective-permute-done.7.refs_0_ = f32[8,96,128]{2,1,0:T(8,128)S(1)} collective-permute-done((f32[8,96,128]{2,1,0:T(8,128)S(1)}, f32[8,96,128]{2,1,0:T(8,128)S(1)}, u32[]{:S(2)}, u32[]{:S(2)}) %collective-permute-start.7) | collective-permute-done | bytes 393248 | tf_op jit(solution)/shard_map/ppermute | solution.py:76
  56.4 1.0 %collective-permute-done.8.refs_1_ = f32[8,96,128]{2,1,0:T(8,128)S(1)} collective-permute-done((f32[8,96,128]{2,1,0:T(8,128)S(1)}, f32[8,96,128]{2,1,0:T(8,128)S(1)}, u32[]{:S(2)}, u32[]{:S(2)}) %collective-permute-start.8) | collective-permute-done | bytes 393248 | tf_op jit(solution)/shard_map/ppermute | solution.py:78
  57.6 1.3 %collective-permute-done.9.refs_2_ = f32[2,96,128]{2,1,0:T(8,128)S(1)} collective-permute-done((f32[2,96,128]{2,1,0:T(8,128)S(1)}, f32[2,96,128]{2,1,0:T(8,128)S(1)}, u32[]{:S(2)}, u32[]{:S(2)}) %collective-permute-start.9) | collective-permute-done | bytes 98336 | tf_op jit(solution)/shard_map/ppermute | solution.py:76
  58.9 1.8 %shard_map.54 = (f32[8,96,128]{2,1,0:T(8,128)S(1)}, f32[8,96,128]{2,1,0:T(8,128)S(1)}, f32[2,1,8,96,128]{4,3,2,1,0:T(8,128)S(1)}) custom-call(f32[96,7]{1,0:T(8,128)S(1)} %bitcast.28, f32[96,96]{1,0:T(8,128)S(1)} %fusion.5.matrix, f32[8,96,128]{2,1,0:T(8,128)S(1)} %get-tuple-element.39.even_ref, f32[8,96,128]{2,1,0:T(8,128)S(1)} %get-tuple-element.40.odd_ref, ...), custom_call_target="tpu_custom_call" | custom-call | flops 32560128 | bytes 4070016 | tf_op jit(solution)/shard_map/pallas_call | solution.py:374
  60.7 12.1 %collective-permute-done.10.refs_0_ = f32[8,96,128]{2,1,0:T(8,128)S(1)} collective-permute-done((f32[8,96,128]{2,1,0:T(8,128)S(1)}, f32[8,96,128]{2,1,0:T(8,128)S(1)}, u32[]{:S(2)}, u32[]{:S(2)}) %collective-permute-start.10) | collective-permute-done | bytes 393248 | tf_op jit(solution)/shard_map/ppermute | solution.py:76
  72.8 1.0 %collective-permute-done.11.refs_1_ = f32[8,96,128]{2,1,0:T(8,128)S(1)} collective-permute-done((f32[8,96,128]{2,1,0:T(8,128)S(1)}, f32[8,96,128]{2,1,0:T(8,128)S(1)}, u32[]{:S(2)}, u32[]{:S(2)}) %collective-permute-start.11) | collective-permute-done | bytes 393248 | tf_op jit(solution)/shard_map/ppermute | solution.py:78
  73.8 1.6 %shard_map.55 = f32[3072,128]{1,0:T(8,128)} custom-call(f32[96,7]{1,0:T(8,128)S(1)} %bitcast.29, f32[8,96,128]{2,1,0:T(8,128)S(1)} %get-tuple-element.42.even_ref, f32[8,96,128]{2,1,0:T(8,128)S(1)} %get-tuple-element.43.odd_ref, f32[2,1,8,96,128]{4,3,2,1,0:T(8,128)S(1)} %get-tuple-element.44.rest_ref, f32[8,96,128]{2,1,0:T(8,128)S(1)} %collective-permute-done.10.refs_0_, ...), custom_call_target="tpu_custom_call" | custom-call | flops 31478784 | bytes 3934848 | tf_op jit(solution)/shard_map/pallas_call | solution.py:374
  (44 shorter events, 1.9 us)
Async XLA Ops:
  0.0 6.8 %copy-start.1 = (s32[3,192]{1,0:T(4,128)S(1)}, s32[3,192]{1,0:T(4,128)}, u32[]{:S(2)}) copy-start(s32[3,192]{1,0:T(4,128)} %signs_raw.1) | copy-start | bytes 6916
  0.0 6.8 %copy-start = (f32[3,192]{1,0:T(4,128)S(1)}, f32[3,192]{1,0:T(4,128)}, u32[]{:S(2)}) copy-start(f32[3,192]{1,0:T(4,128)} %param.5) | copy-start | bytes 6916
  1.8 15.2 %copy-start.2 = (f32[45]{0:T(128)S(1)}, f32[45]{0:T(128)}, u32[]{:S(2)}) copy-start(f32[45]{0:T(128)} %constant.247) | copy-start | bytes 544
  1.9 22.2 %collective-permute-start.1 = (f32[8,96,128]{2,1,0:T(8,128)S(1)}, f32[8,96,128]{2,1,0:T(8,128)S(1)}, u32[]{:S(2)}, u32[]{:S(2)}) collective-permute-start(f32[8,96,128]{2,1,0:T(8,128)S(1)} %get-tuple-element.30.even_ref), channel_id=1, source_target_pairs={{0,2},{2,0},{4,6},{6,4},{8,10},{10,8},{12,14},{14,12},{16,18},{18,... | collective-permute-start | bytes 1179656 | tf_op jit(solution)/shard_map/ppermute | solution.py:76
  1.9 22.1 %collective-permute-start.2 = (f32[8,96,128]{2,1,0:T(8,128)S(1)}, f32[8,96,128]{2,1,0:T(8,128)S(1)}, u32[]{:S(2)}, u32[]{:S(2)}) collective-permute-start(f32[8,96,128]{2,1,0:T(8,128)S(1)} %get-tuple-element.31.odd_ref), channel_id=1, source_target_pairs={{2,4},{4,2},{6,8},{8,6},{10,12},{12,10},{14,16},{16,14},{18,20},{2... | collective-permute-start | bytes 1179656 | tf_op jit(solution)/shard_map/ppermute | solution.py:78
  7.1 10.3 %collective-permute-start = (f32[2,96,128]{2,1,0:T(8,128)S(1)}, f32[2,96,128]{2,1,0:T(8,128)S(1)}, u32[]{:S(2)}, u32[]{:S(2)}) collective-permute-start(f32[2,96,128]{2,1,0:T(8,128)S(1)} %shard_map.47), channel_id=1, source_target_pairs={{0,1},{1,0},{2,3},{3,2},{4,5},{5,4},{6,7},{7,6},{8,9},{9,8},{10,11... | collective-permute-start | bytes 294920 | tf_op jit(solution)/shard_map/ppermute | solution.py:76
  19.1 28.9 %collective-permute-start.4 = (f32[8,96,128]{2,1,0:T(8,128)S(1)}, f32[8,96,128]{2,1,0:T(8,128)S(1)}, u32[]{:S(2)}, u32[]{:S(2)}) collective-permute-start(f32[8,96,128]{2,1,0:T(8,128)S(1)} %get-tuple-element.33.even_ref), channel_id=1, source_target_pairs={{0,2},{2,0},{4,6},{6,4},{8,10},{10,8},{12,14},{14,12},{16,18},{18,... | collective-permute-start | bytes 1179656 | tf_op jit(solution)/shard_map/ppermute | solution.py:76
  19.2 28.8 %collective-permute-start.5 = (f32[8,96,128]{2,1,0:T(8,128)S(1)}, f32[8,96,128]{2,1,0:T(8,128)S(1)}, u32[]{:S(2)}, u32[]{:S(2)}) collective-permute-start(f32[8,96,128]{2,1,0:T(8,128)S(1)} %get-tuple-element.34.odd_ref), channel_id=1, source_target_pairs={{2,4},{4,2},{6,8},{8,6},{10,12},{12,10},{14,16},{16,14},{18,20},{2... | collective-permute-start | bytes 1179656 | tf_op jit(solution)/shard_map/ppermute | solution.py:78
  24.2 1.4 %collective-permute-start.3 = (f32[2,96,128]{2,1,0:T(8,128)S(1)}, f32[2,96,128]{2,1,0:T(8,128)S(1)}, u32[]{:S(2)}, u32[]{:S(2)}) collective-permute-start(f32[2,96,128]{2,1,0:T(8,128)S(1)} %shard_map.49), channel_id=1, source_target_pairs={{0,1},{1,0},{2,3},{3,2},{4,5},{5,4},{6,7},{7,6},{8,9},{9,8},{10,11... | collective-permute-start | bytes 294920 | tf_op jit(solution)/shard_map/ppermute | solution.py:76
  27.4 29.0 %collective-permute-start.7 = (f32[8,96,128]{2,1,0:T(8,128)S(1)}, f32[8,96,128]{2,1,0:T(8,128)S(1)}, u32[]{:S(2)}, u32[]{:S(2)}) collective-permute-start(f32[8,96,128]{2,1,0:T(8,128)S(1)} %get-tuple-element.36.even_ref), channel_id=1, source_target_pairs={{0,2},{2,0},{4,6},{6,4},{8,10},{10,8},{12,14},{14,12},{16,18},{18,... | collective-permute-start | bytes 1179656 | tf_op jit(solution)/shard_map/ppermute | solution.py:76
  27.5 29.9 %collective-permute-start.8 = (f32[8,96,128]{2,1,0:T(8,128)S(1)}, f32[8,96,128]{2,1,0:T(8,128)S(1)}, u32[]{:S(2)}, u32[]{:S(2)}) collective-permute-start(f32[8,96,128]{2,1,0:T(8,128)S(1)} %get-tuple-element.37.odd_ref), channel_id=1, source_target_pairs={{2,4},{4,2},{6,8},{8,6},{10,12},{12,10},{14,16},{16,14},{18,20},{2... | collective-permute-start | bytes 1179656 | tf_op jit(solution)/shard_map/ppermute | solution.py:78
  48.1 1.4 %collective-permute-start.6 = (f32[2,96,128]{2,1,0:T(8,128)S(1)}, f32[2,96,128]{2,1,0:T(8,128)S(1)}, u32[]{:S(2)}, u32[]{:S(2)}) collective-permute-start(f32[2,96,128]{2,1,0:T(8,128)S(1)} %shard_map.51), channel_id=1, source_target_pairs={{0,1},{1,0},{2,3},{3,2},{4,5},{5,4},{6,7},{7,6},{8,9},{9,8},{10,11... | collective-permute-start | bytes 294920 | tf_op jit(solution)/shard_map/ppermute | solution.py:76
  51.3 21.5 %collective-permute-start.10 = (f32[8,96,128]{2,1,0:T(8,128)S(1)}, f32[8,96,128]{2,1,0:T(8,128)S(1)}, u32[]{:S(2)}, u32[]{:S(2)}) collective-permute-start(f32[8,96,128]{2,1,0:T(8,128)S(1)} %get-tuple-element.39.even_ref), channel_id=1, source_target_pairs={{0,2},{2,0},{4,6},{6,4},{8,10},{10,8},{12,14},{14,12},{16,18},{18,... | collective-permute-start | bytes 1179656 | tf_op jit(solution)/shard_map/ppermute | solution.py:76
  51.4 22.4 %collective-permute-start.11 = (f32[8,96,128]{2,1,0:T(8,128)S(1)}, f32[8,96,128]{2,1,0:T(8,128)S(1)}, u32[]{:S(2)}, u32[]{:S(2)}) collective-permute-start(f32[8,96,128]{2,1,0:T(8,128)S(1)} %get-tuple-element.40.odd_ref), channel_id=1, source_target_pairs={{2,4},{4,2},{6,8},{8,6},{10,12},{12,10},{14,16},{16,14},{18,20},{2... | collective-permute-start | bytes 1179656 | tf_op jit(solution)/shard_map/ppermute | solution.py:78
  57.5 1.4 %collective-permute-start.9 = (f32[2,96,128]{2,1,0:T(8,128)S(1)}, f32[2,96,128]{2,1,0:T(8,128)S(1)}, u32[]{:S(2)}, u32[]{:S(2)}) collective-permute-start(f32[2,96,128]{2,1,0:T(8,128)S(1)} %shard_map.53), channel_id=1, source_target_pairs={{0,1},{1,0},{2,3},{3,2},{4,5},{5,4},{6,7},{7,6},{8,9},{9,8},{10,11... | collective-permute-start | bytes 294920 | tf_op jit(solution)/shard_map/ppermute | solution.py:76

commit v4 on v3

--- a/solution.py
+++ b/solution.py
@@ -60,13 +60,13 @@
 def angular_matrix(half):
     basis, eigen_values = harmonic_rows(half)
     gram = 2.0 * jnp.dot(basis, basis.T, precision=lax.Precision.HIGHEST)
-    chol_lower = jnp.linalg.cholesky(gram)
-    partial_solve = lax.linalg.triangular_solve(chol_lower, basis, left_side=True, lower=True)
-    analysis = lax.linalg.triangular_solve(
-        chol_lower, partial_solve, left_side=True, lower=True, transpose_a=True
-    )
-    synthesis = basis.T * (TIME_STEP * DIFFUSION * eigen_values)[None, :]
-    return jnp.dot(synthesis, analysis, precision=lax.Precision.HIGHEST)
+    chol_lower = lax.linalg.cholesky(gram, symmetrize_input=False)
+    scaled = (TIME_STEP * DIFFUSION * eigen_values)[:, None] * basis
+    solved = lax.linalg.triangular_solve(
+        chol_lower, jnp.concatenate([basis, scaled], 1), left_side=True, lower=True
+    )
+    size = basis.shape[1]
+    return jnp.dot(solved[:, size:].T, solved[:, :size], precision=lax.Precision.HIGHEST)
 
 
 def exchange(even_load, odd_load, axis):

time: 75.5 us -> 75.4 us (level)
  no operation moved by 1% of the time
where the time goes in v4:
time: 75.4 us; the launch traced here: 75.2 us
  waiting for transfers between devices  36.7 us (49%)
  starting transfers between devices  17.1 us (23%)
  Pallas kernels  10.9 us (14%)
  other arithmetic  9.14 us (12%)
  matrix products  0.78 us (1%)
    ppermute x8, waiting for transfers between devices, exchange(): got = [lax.ppermute(even_load, axis, first)]  34.7 us
    ppermute x4, starting transfers between devices, exchange(): got.append(lax.ppermute(odd_load, axis, second))  16.5 us
    pallas_call x10, Pallas kernels, call(): pl.pallas_call(body, out_shape=outs, in_specs=in_specs, out_specs=[pl.Blo...  10.9 us
    another operation x3, other arithmetic, angular_matrix(): chol_lower = lax.linalg.cholesky(gram, symmetrize_input=False)  4.77 us
    another operation x2, other arithmetic, angular_matrix(): lax.linalg.triangular_solve(chol_lower, jnp.concatenate([basis, scaled],...  4.1 us
    ppermute x4, waiting for transfers between devices, exchange(): got.append(lax.ppermute(odd_load, axis, second))  1.92 us
  transfers between devices with their start and end apart: 12, of which 8 were waited for; matrix products, arithmetic and copies ran while one was open for 14% of the time, Pallas kernels for 10%

profile of v4, /device:TPU:2, one launch (start us, length us, event | category | flops | bytes accessed | tf_op | source)
XLA Modules:
  0.0 75.2 jit_solution(2605062689118019200)
XLA Ops:
  0.0 1.8 %shard_map.46 = (f32[8,96,128]{2,1,0:T(8,128)S(1)}, f32[8,96,128]{2,1,0:T(8,128)S(1)}, f32[2,1,8,96,128]{4,3,2,1,0:T(8,128)S(1)}) custom-call(s32[3,192]{1,0:T(4,128)} %signs_raw.1, f32[3072,128]{1,0:T(8,128)} %bitcast.23), custom_call_target="tpu_custom_call" | custom-call | flops 25184256 | bytes 3148032 | tf_op jit(solution)/shard_map/pallas_call | solution.py:374
  1.9 4.9 %collective-permute-start.2 = (f32[8,96,128]{2,1,0:T(8,128)S(1)}, f32[8,96,128]{2,1,0:T(8,128)S(1)}, u32[]{:S(2)}, u32[]{:S(2)}) collective-permute-start(f32[8,96,128]{2,1,0:T(8,128)S(1)} %get-tuple-element.31.odd_ref), channel_id=1, source_target_pairs={{2,4},{4,2},{6,8},{8,6},{10,12},{12,10},{14,16},{16,14},{18,20},{2... | collective-permute-start | bytes 1179656 | tf_op jit(solution)/shard_map/ppermute | solution.py:78
  7.7 4.1 %cholesky.16 = f32[45,45]{1,0:T(8,128)S(1)} custom-call(f32[45,45]{1,0:T(8,128)S(1)} %convolution_multiply_fusion), custom_call_target="Cholesky" | custom-call | tf_op jit(solution)/shard_map/cholesky | solution.py:63
  11.8 0.6 compare_reduce_fusion
  12.5 0.7 fusion.4
  13.1 3.4 %custom-call.5 = f32[1,45,45]{1,2,0:T(8,128)S(1)} custom-call(f32[1,45,45]{2,1,0:T(8,128)S(1)} %fusion.4), custom_call_target="InvertDiagBlocksLowerTriangular" | custom-call | tf_op jit(solution)/shard_map/triangular_solve | solution.py:65
  16.6 0.3 fusion
  16.9 0.3 fusion.5.matrix
  17.3 1.7 %shard_map.48 = (f32[8,96,128]{2,1,0:T(8,128)S(1)}, f32[8,96,128]{2,1,0:T(8,128)S(1)}, f32[2,1,8,96,128]{4,3,2,1,0:T(8,128)S(1)}) custom-call(f32[96,7]{1,0:T(8,128)S(1)} %bitcast.15, f32[96,96]{1,0:T(8,128)S(1)} %fusion.5.matrix, f32[8,96,128]{2,1,0:T(8,128)S(1)} %get-tuple-element.30.even_ref, f32[8,96,128]{2,1,0:T(8,128)S(1)} %get-tuple-element.31.odd_ref, ...), custom_call_target="tpu_custom_call" | custom-call | flops 26268672 | bytes 3283584 | tf_op jit(solution)/shard_map/pallas_call | solution.py:374
  19.0 4.9 %collective-permute-start.5 = (f32[8,96,128]{2,1,0:T(8,128)S(1)}, f32[8,96,128]{2,1,0:T(8,128)S(1)}, u32[]{:S(2)}, u32[]{:S(2)}) collective-permute-start(f32[8,96,128]{2,1,0:T(8,128)S(1)} %get-tuple-element.34.odd_ref), channel_id=1, source_target_pairs={{2,4},{4,2},{6,8},{8,6},{10,12},{12,10},{14,16},{16,14},{18,20},{2... | collective-permute-start | bytes 1179656 | tf_op jit(solution)/shard_map/ppermute | solution.py:78
  24.1 1.3 %collective-permute-done.3.refs_2_ = f32[2,96,128]{2,1,0:T(8,128)S(1)} collective-permute-done((f32[2,96,128]{2,1,0:T(8,128)S(1)}, f32[2,96,128]{2,1,0:T(8,128)S(1)}, u32[]{:S(2)}, u32[]{:S(2)}) %collective-permute-start.3) | collective-permute-done | bytes 98336 | tf_op jit(solution)/shard_map/ppermute | solution.py:76
  25.4 1.8 %shard_map.50 = (f32[8,96,128]{2,1,0:T(8,128)S(1)}, f32[8,96,128]{2,1,0:T(8,128)S(1)}, f32[2,1,8,96,128]{4,3,2,1,0:T(8,128)S(1)}) custom-call(f32[96,7]{1,0:T(8,128)S(1)} %bitcast.17, f32[96,96]{1,0:T(8,128)S(1)} %fusion.5.matrix, f32[8,96,128]{2,1,0:T(8,128)S(1)} %get-tuple-element.33.even_ref, f32[8,96,128]{2,1,0:T(8,128)S(1)} %get-tuple-element.34.odd_ref, ...), custom_call_target="tpu_custom_call" | custom-call | flops 32560128 | bytes 4070016 | tf_op jit(solution)/shard_map/pallas_call | solution.py:374
  27.3 4.9 %collective-permute-start.8 = (f32[8,96,128]{2,1,0:T(8,128)S(1)}, f32[8,96,128]{2,1,0:T(8,128)S(1)}, u32[]{:S(2)}, u32[]{:S(2)}) collective-permute-start(f32[8,96,128]{2,1,0:T(8,128)S(1)} %get-tuple-element.37.odd_ref), channel_id=1, source_target_pairs={{2,4},{4,2},{6,8},{8,6},{10,12},{12,10},{14,16},{16,14},{18,20},{2... | collective-permute-start | bytes 1179656 | tf_op jit(solution)/shard_map/ppermute | solution.py:78
  32.2 15.7 %collective-permute-done.4.refs_0_ = f32[8,96,128]{2,1,0:T(8,128)S(1)} collective-permute-done((f32[8,96,128]{2,1,0:T(8,128)S(1)}, f32[8,96,128]{2,1,0:T(8,128)S(1)}, u32[]{:S(2)}, u32[]{:S(2)}) %collective-permute-start.4) | collective-permute-done | bytes 393248 | tf_op jit(solution)/shard_map/ppermute | solution.py:76
  48.0 1.3 %collective-permute-done.6.refs_2_ = f32[2,96,128]{2,1,0:T(8,128)S(1)} collective-permute-done((f32[2,96,128]{2,1,0:T(8,128)S(1)}, f32[2,96,128]{2,1,0:T(8,128)S(1)}, u32[]{:S(2)}, u32[]{:S(2)}) %collective-permute-start.6) | collective-permute-done | bytes 98336 | tf_op jit(solution)/shard_map/ppermute | solution.py:76
  49.3 1.8 %shard_map.52 = (f32[8,96,128]{2,1,0:T(8,128)S(1)}, f32[8,96,128]{2,1,0:T(8,128)S(1)}, f32[2,1,8,96,128]{4,3,2,1,0:T(8,128)S(1)}) custom-call(f32[96,7]{1,0:T(8,128)S(1)} %bitcast.19, f32[96,96]{1,0:T(8,128)S(1)} %fusion.5.matrix, f32[8,96,128]{2,1,0:T(8,128)S(1)} %get-tuple-element.36.even_ref, f32[8,96,128]{2,1,0:T(8,128)S(1)} %get-tuple-element.37.odd_ref, ...), custom_call_target="tpu_custom_call" | custom-call | flops 32560128 | bytes 4070016 | tf_op jit(solution)/shard_map/pallas_call | solution.py:374
  51.2 1.9 %collective-permute-start.11 = (f32[8,96,128]{2,1,0:T(8,128)S(1)}, f32[8,96,128]{2,1,0:T(8,128)S(1)}, u32[]{:S(2)}, u32[]{:S(2)}) collective-permute-start(f32[8,96,128]{2,1,0:T(8,128)S(1)} %get-tuple-element.40.odd_ref), channel_id=1, source_target_pairs={{2,4},{4,2},{6,8},{8,6},{10,12},{12,10},{14,16},{16,14},{18,20},{2... | collective-permute-start | bytes 1179656 | tf_op jit(solution)/shard_map/ppermute | solution.py:78
  53.2 3.1 %collective-permute-done.7.refs_0_ = f32[8,96,128]{2,1,0:T(8,128)S(1)} collective-permute-done((f32[8,96,128]{2,1,0:T(8,128)S(1)}, f32[8,96,128]{2,1,0:T(8,128)S(1)}, u32[]{:S(2)}, u32[]{:S(2)}) %collective-permute-start.7) | collective-permute-done | bytes 393248 | tf_op jit(solution)/shard_map/ppermute | solution.py:76
  56.3 1.0 %collective-permute-done.8.refs_1_ = f32[8,96,128]{2,1,0:T(8,128)S(1)} collective-permute-done((f32[8,96,128]{2,1,0:T(8,128)S(1)}, f32[8,96,128]{2,1,0:T(8,128)S(1)}, u32[]{:S(2)}, u32[]{:S(2)}) %collective-permute-start.8) | collective-permute-done | bytes 393248 | tf_op jit(solution)/shard_map/ppermute | solution.py:78
  57.4 1.3 %collective-permute-done.9.refs_2_ = f32[2,96,128]{2,1,0:T(8,128)S(1)} collective-permute-done((f32[2,96,128]{2,1,0:T(8,128)S(1)}, f32[2,96,128]{2,1,0:T(8,128)S(1)}, u32[]{:S(2)}, u32[]{:S(2)}) %collective-permute-start.9) | collective-permute-done | bytes 98336 | tf_op jit(solution)/shard_map/ppermute | solution.py:76
  58.7 1.8 %shard_map.54 = (f32[8,96,128]{2,1,0:T(8,128)S(1)}, f32[8,96,128]{2,1,0:T(8,128)S(1)}, f32[2,1,8,96,128]{4,3,2,1,0:T(8,128)S(1)}) custom-call(f32[96,7]{1,0:T(8,128)S(1)} %bitcast.21, f32[96,96]{1,0:T(8,128)S(1)} %fusion.5.matrix, f32[8,96,128]{2,1,0:T(8,128)S(1)} %get-tuple-element.39.even_ref, f32[8,96,128]{2,1,0:T(8,128)S(1)} %get-tuple-element.40.odd_ref, ...), custom_call_target="tpu_custom_call" | custom-call | flops 32560128 | bytes 4070016 | tf_op jit(solution)/shard_map/pallas_call | solution.py:374
  60.5 12.1 %collective-permute-done.10.refs_0_ = f32[8,96,128]{2,1,0:T(8,128)S(1)} collective-permute-done((f32[8,96,128]{2,1,0:T(8,128)S(1)}, f32[8,96,128]{2,1,0:T(8,128)S(1)}, u32[]{:S(2)}, u32[]{:S(2)}) %collective-permute-start.10) | collective-permute-done | bytes 393248 | tf_op jit(solution)/shard_map/ppermute | solution.py:76
  72.7 1.0 %collective-permute-done.11.refs_1_ = f32[8,96,128]{2,1,0:T(8,128)S(1)} collective-permute-done((f32[8,96,128]{2,1,0:T(8,128)S(1)}, f32[8,96,128]{2,1,0:T(8,128)S(1)}, u32[]{:S(2)}, u32[]{:S(2)}) %collective-permute-start.11) | collective-permute-done | bytes 393248 | tf_op jit(solution)/shard_map/ppermute | solution.py:78
  73.6 1.6 %shard_map.55 = f32[3072,128]{1,0:T(8,128)} custom-call(f32[96,7]{1,0:T(8,128)S(1)} %bitcast.22, f32[8,96,128]{2,1,0:T(8,128)S(1)} %get-tuple-element.42.even_ref, f32[8,96,128]{2,1,0:T(8,128)S(1)} %get-tuple-element.43.odd_ref, f32[2,1,8,96,128]{4,3,2,1,0:T(8,128)S(1)} %get-tuple-element.44.rest_ref, f32[8,96,128]{2,1,0:T(8,128)S(1)} %collective-permute-done.10.refs_0_, ...), custom_call_target="tpu_custom_call" | custom-call | flops 31478784 | bytes 3934848 | tf_op jit(solution)/shard_map/pallas_call | solution.py:374
  (42 shorter events, 1.7 us)
Async XLA Ops:
  0.0 6.8 %copy-start.1 = (s32[3,192]{1,0:T(4,128)S(1)}, s32[3,192]{1,0:T(4,128)}, u32[]{:S(2)}) copy-start(s32[3,192]{1,0:T(4,128)} %signs_raw.1) | copy-start | bytes 6916
  0.0 6.8 %copy-start = (f32[3,192]{1,0:T(4,128)S(1)}, f32[3,192]{1,0:T(4,128)}, u32[]{:S(2)}) copy-start(f32[3,192]{1,0:T(4,128)} %param.5) | copy-start | bytes 6916
  0.0 16.6 %copy-start.2 = (f32[45]{0:T(128)S(1)}, f32[45]{0:T(128)}, u32[]{:S(2)}) copy-start(f32[45]{0:T(128)} %constant.229) | copy-start | bytes 544
  1.8 22.0 %collective-permute-start.1 = (f32[8,96,128]{2,1,0:T(8,128)S(1)}, f32[8,96,128]{2,1,0:T(8,128)S(1)}, u32[]{:S(2)}, u32[]{:S(2)}) collective-permute-start(f32[8,96,128]{2,1,0:T(8,128)S(1)} %get-tuple-element.30.even_ref), channel_id=1, source_target_pairs={{0,2},{2,0},{4,6},{6,4},{8,10},{10,8},{12,14},{14,12},{16,18},{18,... | collective-permute-start | bytes 1179656 | tf_op jit(solution)/shard_map/ppermute | solution.py:76
  1.9 22.0 %collective-permute-start.2 = (f32[8,96,128]{2,1,0:T(8,128)S(1)}, f32[8,96,128]{2,1,0:T(8,128)S(1)}, u32[]{:S(2)}, u32[]{:S(2)}) collective-permute-start(f32[8,96,128]{2,1,0:T(8,128)S(1)} %get-tuple-element.31.odd_ref), channel_id=1, source_target_pairs={{2,4},{4,2},{6,8},{8,6},{10,12},{12,10},{14,16},{16,14},{18,20},{2... | collective-permute-start | bytes 1179656 | tf_op jit(solution)/shard_map/ppermute | solution.py:78
  7.1 10.2 %collective-permute-start = (f32[2,96,128]{2,1,0:T(8,128)S(1)}, f32[2,96,128]{2,1,0:T(8,128)S(1)}, u32[]{:S(2)}, u32[]{:S(2)}) collective-permute-start(f32[2,96,128]{2,1,0:T(8,128)S(1)} %shard_map.47), channel_id=1, source_target_pairs={{0,1},{1,0},{2,3},{3,2},{4,5},{5,4},{6,7},{7,6},{8,9},{9,8},{10,11... | collective-permute-start | bytes 294920 | tf_op jit(solution)/shard_map/ppermute | solution.py:76
  18.9 28.9 %collective-permute-start.4 = (f32[8,96,128]{2,1,0:T(8,128)S(1)}, f32[8,96,128]{2,1,0:T(8,128)S(1)}, u32[]{:S(2)}, u32[]{:S(2)}) collective-permute-start(f32[8,96,128]{2,1,0:T(8,128)S(1)} %get-tuple-element.33.even_ref), channel_id=1, source_target_pairs={{0,2},{2,0},{4,6},{6,4},{8,10},{10,8},{12,14},{14,12},{16,18},{18,... | collective-permute-start | bytes 1179656 | tf_op jit(solution)/shard_map/ppermute | solution.py:76
  19.0 28.8 %collective-permute-start.5 = (f32[8,96,128]{2,1,0:T(8,128)S(1)}, f32[8,96,128]{2,1,0:T(8,128)S(1)}, u32[]{:S(2)}, u32[]{:S(2)}) collective-permute-start(f32[8,96,128]{2,1,0:T(8,128)S(1)} %get-tuple-element.34.odd_ref), channel_id=1, source_target_pairs={{2,4},{4,2},{6,8},{8,6},{10,12},{12,10},{14,16},{16,14},{18,20},{2... | collective-permute-start | bytes 1179656 | tf_op jit(solution)/shard_map/ppermute | solution.py:78
  24.0 1.4 %collective-permute-start.3 = (f32[2,96,128]{2,1,0:T(8,128)S(1)}, f32[2,96,128]{2,1,0:T(8,128)S(1)}, u32[]{:S(2)}, u32[]{:S(2)}) collective-permute-start(f32[2,96,128]{2,1,0:T(8,128)S(1)} %shard_map.49), channel_id=1, source_target_pairs={{0,1},{1,0},{2,3},{3,2},{4,5},{5,4},{6,7},{7,6},{8,9},{9,8},{10,11... | collective-permute-start | bytes 294920 | tf_op jit(solution)/shard_map/ppermute | solution.py:76
  27.2 29.0 %collective-permute-start.7 = (f32[8,96,128]{2,1,0:T(8,128)S(1)}, f32[8,96,128]{2,1,0:T(8,128)S(1)}, u32[]{:S(2)}, u32[]{:S(2)}) collective-permute-start(f32[8,96,128]{2,1,0:T(8,128)S(1)} %get-tuple-element.36.even_ref), channel_id=1, source_target_pairs={{0,2},{2,0},{4,6},{6,4},{8,10},{10,8},{12,14},{14,12},{16,18},{18,... | collective-permute-start | bytes 1179656 | tf_op jit(solution)/shard_map/ppermute | solution.py:76
  27.3 29.9 %collective-permute-start.8 = (f32[8,96,128]{2,1,0:T(8,128)S(1)}, f32[8,96,128]{2,1,0:T(8,128)S(1)}, u32[]{:S(2)}, u32[]{:S(2)}) collective-permute-start(f32[8,96,128]{2,1,0:T(8,128)S(1)} %get-tuple-element.37.odd_ref), channel_id=1, source_target_pairs={{2,4},{4,2},{6,8},{8,6},{10,12},{12,10},{14,16},{16,14},{18,20},{2... | collective-permute-start | bytes 1179656 | tf_op jit(solution)/shard_map/ppermute | solution.py:78
  48.0 1.4 %collective-permute-start.6 = (f32[2,96,128]{2,1,0:T(8,128)S(1)}, f32[2,96,128]{2,1,0:T(8,128)S(1)}, u32[]{:S(2)}, u32[]{:S(2)}) collective-permute-start(f32[2,96,128]{2,1,0:T(8,128)S(1)} %shard_map.51), channel_id=1, source_target_pairs={{0,1},{1,0},{2,3},{3,2},{4,5},{5,4},{6,7},{7,6},{8,9},{9,8},{10,11... | collective-permute-start | bytes 294920 | tf_op jit(solution)/shard_map/ppermute | solution.py:76
  51.2 21.5 %collective-permute-start.10 = (f32[8,96,128]{2,1,0:T(8,128)S(1)}, f32[8,96,128]{2,1,0:T(8,128)S(1)}, u32[]{:S(2)}, u32[]{:S(2)}) collective-permute-start(f32[8,96,128]{2,1,0:T(8,128)S(1)} %get-tuple-element.39.even_ref), channel_id=1, source_target_pairs={{0,2},{2,0},{4,6},{6,4},{8,10},{10,8},{12,14},{14,12},{16,18},{18,... | collective-permute-start | bytes 1179656 | tf_op jit(solution)/shard_map/ppermute | solution.py:76
  51.2 22.4 %collective-permute-start.11 = (f32[8,96,128]{2,1,0:T(8,128)S(1)}, f32[8,96,128]{2,1,0:T(8,128)S(1)}, u32[]{:S(2)}, u32[]{:S(2)}) collective-permute-start(f32[8,96,128]{2,1,0:T(8,128)S(1)} %get-tuple-element.40.odd_ref), channel_id=1, source_target_pairs={{2,4},{4,2},{6,8},{8,6},{10,12},{12,10},{14,16},{16,14},{18,20},{2... | collective-permute-start | bytes 1179656 | tf_op jit(solution)/shard_map/ppermute | solution.py:78
  57.3 1.4 %collective-permute-start.9 = (f32[2,96,128]{2,1,0:T(8,128)S(1)}, f32[2,96,128]{2,1,0:T(8,128)S(1)}, u32[]{:S(2)}, u32[]{:S(2)}) collective-permute-start(f32[2,96,128]{2,1,0:T(8,128)S(1)} %shard_map.53), channel_id=1, source_target_pairs={{0,1},{1,0},{2,3},{3,2},{4,5},{5,4},{6,7},{7,6},{8,9},{9,8},{10,11... | collective-permute-start | bytes 294920 | tf_op jit(solution)/shard_map/ppermute | solution.py:76

commit v5 on v4

--- a/solution.py
+++ b/solution.py
@@ -62,11 +62,45 @@
     gram = 2.0 * jnp.dot(basis, basis.T, precision=lax.Precision.HIGHEST)
     chol_lower = lax.linalg.cholesky(gram, symmetrize_input=False)
     scaled = (TIME_STEP * DIFFUSION * eigen_values)[:, None] * basis
-    solved = lax.linalg.triangular_solve(
-        chol_lower, jnp.concatenate([basis, scaled], 1), left_side=True, lower=True
-    )
-    size = basis.shape[1]
-    return jnp.dot(solved[:, size:].T, solved[:, :size], precision=lax.Precision.HIGHEST)
+    return call(
+        functools.partial(solve_body, basis.shape[0]),
+        [jax.ShapeDtypeStruct((basis.shape[1],) * 2, jnp.float32)],
+        [padded(chol_lower), padded(scaled), padded(basis)],
+    )[0]
+
+
+def padded(value):
+    return jnp.pad(value, ((0, -value.shape[0] % 8), (0, 0)))
+
+
+def solve_body(count, chol, left, right, out):
+    size, width = left.shape
+    factor = chol[...]
+    row = lax.broadcasted_iota(jnp.int32, factor.shape, 0)
+    col = lax.broadcasted_iota(jnp.int32, factor.shape, 1)
+    diagonal = jnp.where(row == col, factor, 0.0)
+    by_lane = jnp.sum(diagonal, axis=0, keepdims=True)
+    factor = jnp.where(row > col, factor / by_lane, 0.0)
+    weight = jnp.sum(diagonal, axis=1, keepdims=True)
+    weight = jnp.where(weight == 0.0, 1.0, weight)
+    blocks = [
+        [ref[8 * block : 8 * block + 8, :] for block in range(size // 8)] for ref in (left, right)
+    ]
+    for j in range(count):
+        home, place = divmod(j, 8)
+        pivots = [jnp.broadcast_to(side[home][place : place + 1, :], (8, width)) for side in blocks]
+        for block in range(home, size // 8):
+            ratio = jnp.broadcast_to(factor[8 * block : 8 * block + 8, j : j + 1], (8, width))
+            for side, pivot in zip(blocks, pivots):
+                side[block] = side[block] - ratio * pivot
+    first, second = (jnp.concatenate(side, 0) for side in blocks)
+    out[...] = lax.dot_general(
+        first,
+        second / (weight * weight),
+        (((0,), (0,)), ((), ())),
+        precision=lax.Precision.HIGHEST,
+        preferred_element_type=jnp.float32,
+    )
 
 
 def exchange(even_load, odd_load, axis):

time: 75.4 us -> 74.5 us (0.988)
  waiting for transfers between devices: 36.7 us -> 41.9 us
  other arithmetic: 9.14 us -> 5.69 us
  starting transfers between devices: 17.1 us -> 14.3 us
    ppermute x8, waiting for transfers between devices: 34.7 us -> 39.1 us  [exchange(): got = [lax.ppermute(even_load, axis, first)]]
    another operation x2 -> x0, other arithmetic: 4.1 us -> none  [angular_matrix(): lax.linalg.triangular_solve(chol_lower, jnp.concatenate([basis, scaled],...]
    ppermute x4, starting transfers between devices: 16.5 us -> 13.7 us  [exchange(): got.append(lax.ppermute(odd_load, axis, second))]
    ppermute x4, waiting for transfers between devices: 1.92 us -> 2.87 us  [exchange(): got.append(lax.ppermute(odd_load, axis, second))]
    pallas_call x10 -> x11, Pallas kernels: 10.9 us -> 11.6 us  [call(): pl.pallas_call(body, out_shape=outs, in_specs=in_specs, out_specs=[pl.Blo...]
  transfers between devices with their start and end apart: 12 -> 12, of which waited for: 8 -> 10; matrix products, arithmetic and copies ran while one was open for 14% -> 8% of each run, Pallas kernels for 10% -> 11%
where the time goes in v5:
time: 74.5 us; the launch traced here: 74.3 us
  waiting for transfers between devices  41.9 us (56%)
  starting transfers between devices  14.3 us (19%)
  Pallas kernels  11.6 us (16%)
  other arithmetic  5.69 us (8%)
    ppermute x8, waiting for transfers between devices, exchange(): got = [lax.ppermute(even_load, axis, first)]  39.1 us
    ppermute x4, starting transfers between devices, exchange(): got.append(lax.ppermute(odd_load, axis, second))  13.7 us
    pallas_call x11, Pallas kernels, call(): pl.pallas_call(body, out_shape=outs, in_specs=in_specs, out_specs=[pl.Blo...  11.6 us
    another operation x3, other arithmetic, angular_matrix(): chol_lower = lax.linalg.cholesky(gram, symmetrize_input=False)  4.77 us
    ppermute x4, waiting for transfers between devices, exchange(): got.append(lax.ppermute(odd_load, axis, second))  2.87 us
  transfers between devices with their start and end apart: 12, of which 10 were waited for; matrix products, arithmetic and copies ran while one was open for 8% of the time, Pallas kernels for 11%

profile of v5, /device:TPU:2, one launch (start us, length us, event | category | flops | bytes accessed | tf_op | source)
XLA Modules:
  0.0 74.3 jit_solution(4539582964356711669)
XLA Ops:
  0.0 1.8 %shard_map.46 = (f32[8,96,128]{2,1,0:T(8,128)S(1)}, f32[8,96,128]{2,1,0:T(8,128)S(1)}, f32[2,1,8,96,128]{4,3,2,1,0:T(8,128)S(1)}) custom-call(s32[3,192]{1,0:T(4,128)} %signs_raw.1, f32[3072,128]{1,0:T(8,128)} %bitcast.18), custom_call_target="tpu_custom_call" | custom-call | flops 25184256 | bytes 3148032 | tf_op jit(solution)/shard_map/pallas_call | solution.py:408
  1.9 4.9 %collective-permute-start.2 = (f32[8,96,128]{2,1,0:T(8,128)S(1)}, f32[8,96,128]{2,1,0:T(8,128)S(1)}, u32[]{:S(2)}, u32[]{:S(2)}) collective-permute-start(f32[8,96,128]{2,1,0:T(8,128)S(1)} %get-tuple-element.31.odd_ref), channel_id=1, source_target_pairs={{2,4},{4,2},{6,8},{8,6},{10,12},{12,10},{14,16},{16,14},{18,20},{2... | collective-permute-start | bytes 1179656 | tf_op jit(solution)/shard_map/ppermute | solution.py:112
  7.7 4.1 %cholesky.18 = f32[45,45]{1,0:T(8,128)S(1)} custom-call(f32[45,45]{1,0:T(8,128)S(1)} %convolution_multiply_fusion), custom_call_target="Cholesky" | custom-call | tf_op jit(solution)/shard_map/cholesky | solution.py:63
  11.8 0.6 compare_reduce_fusion
  12.5 0.7 select_select_fusion
  13.2 0.6 shard_map.47.matrix
  13.9 1.7 %shard_map.49 = (f32[8,96,128]{2,1,0:T(8,128)S(1)}, f32[8,96,128]{2,1,0:T(8,128)S(1)}, f32[2,1,8,96,128]{4,3,2,1,0:T(8,128)S(1)}) custom-call(f32[96,7]{1,0:T(8,128)S(1)} %bitcast.10, f32[96,96]{1,0:T(8,128)S(1)} %shard_map.47.matrix, f32[8,96,128]{2,1,0:T(8,128)S(1)} %get-tuple-element.30.even_ref, f32[8,96,128]{2,1,0:T(8,128)S(1)} %get-tuple-element.31.odd_ref, ...), custom_call_target="tpu_custom_call" | custom-call | flops 26268672 | bytes 3283584 | tf_op jit(solution)/shard_map/pallas_call | solution.py:408
  15.6 4.9 %collective-permute-start.5 = (f32[8,96,128]{2,1,0:T(8,128)S(1)}, f32[8,96,128]{2,1,0:T(8,128)S(1)}, u32[]{:S(2)}, u32[]{:S(2)}) collective-permute-start(f32[8,96,128]{2,1,0:T(8,128)S(1)} %get-tuple-element.34.odd_ref), channel_id=1, source_target_pairs={{2,4},{4,2},{6,8},{8,6},{10,12},{12,10},{14,16},{16,14},{18,20},{2... | collective-permute-start | bytes 1179656 | tf_op jit(solution)/shard_map/ppermute | solution.py:112
  20.5 1.8 %collective-permute-done.1.refs_0_ = f32[8,96,128]{2,1,0:T(8,128)S(1)} collective-permute-done((f32[8,96,128]{2,1,0:T(8,128)S(1)}, f32[8,96,128]{2,1,0:T(8,128)S(1)}, u32[]{:S(2)}, u32[]{:S(2)}) %collective-permute-start.1) | collective-permute-done | bytes 393248 | tf_op jit(solution)/shard_map/ppermute | solution.py:110
  22.3 1.0 %collective-permute-done.2.refs_1_ = f32[8,96,128]{2,1,0:T(8,128)S(1)} collective-permute-done((f32[8,96,128]{2,1,0:T(8,128)S(1)}, f32[8,96,128]{2,1,0:T(8,128)S(1)}, u32[]{:S(2)}, u32[]{:S(2)}) %collective-permute-start.2) | collective-permute-done | bytes 393248 | tf_op jit(solution)/shard_map/ppermute | solution.py:112
  23.5 1.3 %collective-permute-done.3.refs_2_ = f32[2,96,128]{2,1,0:T(8,128)S(1)} collective-permute-done((f32[2,96,128]{2,1,0:T(8,128)S(1)}, f32[2,96,128]{2,1,0:T(8,128)S(1)}, u32[]{:S(2)}, u32[]{:S(2)}) %collective-permute-start.3) | collective-permute-done | bytes 98336 | tf_op jit(solution)/shard_map/ppermute | solution.py:110
  24.8 1.8 %shard_map.51 = (f32[8,96,128]{2,1,0:T(8,128)S(1)}, f32[8,96,128]{2,1,0:T(8,128)S(1)}, f32[2,1,8,96,128]{4,3,2,1,0:T(8,128)S(1)}) custom-call(f32[96,7]{1,0:T(8,128)S(1)} %bitcast.12, f32[96,96]{1,0:T(8,128)S(1)} %shard_map.47.matrix, f32[8,96,128]{2,1,0:T(8,128)S(1)} %get-tuple-element.33.even_ref, f32[8,96,128]{2,1,0:T(8,128)S(1)} %get-tuple-element.34.odd_ref, ...), custom_call_target="tpu_custom_call" | custom-call | flops 32560128 | bytes 4070016 | tf_op jit(solution)/shard_map/pallas_call | solution.py:408
  26.7 2.1 %collective-permute-start.8 = (f32[8,96,128]{2,1,0:T(8,128)S(1)}, f32[8,96,128]{2,1,0:T(8,128)S(1)}, u32[]{:S(2)}, u32[]{:S(2)}) collective-permute-start(f32[8,96,128]{2,1,0:T(8,128)S(1)} %get-tuple-element.37.odd_ref), channel_id=1, source_target_pairs={{2,4},{4,2},{6,8},{8,6},{10,12},{12,10},{14,16},{16,14},{18,20},{2... | collective-permute-start | bytes 1179656 | tf_op jit(solution)/shard_map/ppermute | solution.py:112
  28.8 18.8 %collective-permute-done.4.refs_0_ = f32[8,96,128]{2,1,0:T(8,128)S(1)} collective-permute-done((f32[8,96,128]{2,1,0:T(8,128)S(1)}, f32[8,96,128]{2,1,0:T(8,128)S(1)}, u32[]{:S(2)}, u32[]{:S(2)}) %collective-permute-start.4) | collective-permute-done | bytes 393248 | tf_op jit(solution)/shard_map/ppermute | solution.py:110
  47.8 1.3 %collective-permute-done.6.refs_2_ = f32[2,96,128]{2,1,0:T(8,128)S(1)} collective-permute-done((f32[2,96,128]{2,1,0:T(8,128)S(1)}, f32[2,96,128]{2,1,0:T(8,128)S(1)}, u32[]{:S(2)}, u32[]{:S(2)}) %collective-permute-start.6) | collective-permute-done | bytes 98336 | tf_op jit(solution)/shard_map/ppermute | solution.py:110
  49.1 1.8 %shard_map.53 = (f32[8,96,128]{2,1,0:T(8,128)S(1)}, f32[8,96,128]{2,1,0:T(8,128)S(1)}, f32[2,1,8,96,128]{4,3,2,1,0:T(8,128)S(1)}) custom-call(f32[96,7]{1,0:T(8,128)S(1)} %bitcast.14, f32[96,96]{1,0:T(8,128)S(1)} %shard_map.47.matrix, f32[8,96,128]{2,1,0:T(8,128)S(1)} %get-tuple-element.36.even_ref, f32[8,96,128]{2,1,0:T(8,128)S(1)} %get-tuple-element.37.odd_ref, ...), custom_call_target="tpu_custom_call" | custom-call | flops 32560128 | bytes 4070016 | tf_op jit(solution)/shard_map/pallas_call | solution.py:408
  51.0 1.9 %collective-permute-start.11 = (f32[8,96,128]{2,1,0:T(8,128)S(1)}, f32[8,96,128]{2,1,0:T(8,128)S(1)}, u32[]{:S(2)}, u32[]{:S(2)}) collective-permute-start(f32[8,96,128]{2,1,0:T(8,128)S(1)} %get-tuple-element.40.odd_ref), channel_id=1, source_target_pairs={{2,4},{4,2},{6,8},{8,6},{10,12},{12,10},{14,16},{16,14},{18,20},{2... | collective-permute-start | bytes 1179656 | tf_op jit(solution)/shard_map/ppermute | solution.py:112
  52.9 3.1 %collective-permute-done.7.refs_0_ = f32[8,96,128]{2,1,0:T(8,128)S(1)} collective-permute-done((f32[8,96,128]{2,1,0:T(8,128)S(1)}, f32[8,96,128]{2,1,0:T(8,128)S(1)}, u32[]{:S(2)}, u32[]{:S(2)}) %collective-permute-start.7) | collective-permute-done | bytes 393248 | tf_op jit(solution)/shard_map/ppermute | solution.py:110
  56.0 1.0 %collective-permute-done.8.refs_1_ = f32[8,96,128]{2,1,0:T(8,128)S(1)} collective-permute-done((f32[8,96,128]{2,1,0:T(8,128)S(1)}, f32[8,96,128]{2,1,0:T(8,128)S(1)}, u32[]{:S(2)}, u32[]{:S(2)}) %collective-permute-start.8) | collective-permute-done | bytes 393248 | tf_op jit(solution)/shard_map/ppermute | solution.py:112
  57.2 1.3 %collective-permute-done.9.refs_2_ = f32[2,96,128]{2,1,0:T(8,128)S(1)} collective-permute-done((f32[2,96,128]{2,1,0:T(8,128)S(1)}, f32[2,96,128]{2,1,0:T(8,128)S(1)}, u32[]{:S(2)}, u32[]{:S(2)}) %collective-permute-start.9) | collective-permute-done | bytes 98336 | tf_op jit(solution)/shard_map/ppermute | solution.py:110
  58.5 1.8 %shard_map.55 = (f32[8,96,128]{2,1,0:T(8,128)S(1)}, f32[8,96,128]{2,1,0:T(8,128)S(1)}, f32[2,1,8,96,128]{4,3,2,1,0:T(8,128)S(1)}) custom-call(f32[96,7]{1,0:T(8,128)S(1)} %bitcast.16, f32[96,96]{1,0:T(8,128)S(1)} %shard_map.47.matrix, f32[8,96,128]{2,1,0:T(8,128)S(1)} %get-tuple-element.39.even_ref, f32[8,96,128]{2,1,0:T(8,128)S(1)} %get-tuple-element.40.odd_ref, ...), custom_call_target="tpu_custom_call" | custom-call | flops 32560128 | bytes 4070016 | tf_op jit(solution)/shard_map/pallas_call | solution.py:408
  60.3 11.4 %collective-permute-done.10.refs_0_ = f32[8,96,128]{2,1,0:T(8,128)S(1)} collective-permute-done((f32[8,96,128]{2,1,0:T(8,128)S(1)}, f32[8,96,128]{2,1,0:T(8,128)S(1)}, u32[]{:S(2)}, u32[]{:S(2)}) %collective-permute-start.10) | collective-permute-done | bytes 393248 | tf_op jit(solution)/shard_map/ppermute | solution.py:110
  71.8 1.0 %collective-permute-done.11.refs_1_ = f32[8,96,128]{2,1,0:T(8,128)S(1)} collective-permute-done((f32[8,96,128]{2,1,0:T(8,128)S(1)}, f32[8,96,128]{2,1,0:T(8,128)S(1)}, u32[]{:S(2)}, u32[]{:S(2)}) %collective-permute-start.11) | collective-permute-done | bytes 393248 | tf_op jit(solution)/shard_map/ppermute | solution.py:112
  72.7 1.6 %shard_map.56 = f32[3072,128]{1,0:T(8,128)} custom-call(f32[96,7]{1,0:T(8,128)S(1)} %bitcast.17, f32[8,96,128]{2,1,0:T(8,128)S(1)} %get-tuple-element.42.even_ref, f32[8,96,128]{2,1,0:T(8,128)S(1)} %get-tuple-element.43.odd_ref, f32[2,1,8,96,128]{4,3,2,1,0:T(8,128)S(1)} %get-tuple-element.44.rest_ref, f32[8,96,128]{2,1,0:T(8,128)S(1)} %collective-permute-done.10.refs_0_, ...), custom_call_target="tpu_custom_call" | custom-call | flops 31478784 | bytes 3934848 | tf_op jit(solution)/shard_map/pallas_call | solution.py:408
  (43 shorter events, 1.7 us)
Async XLA Ops:
  0.0 6.8 %copy-start.1 = (s32[3,192]{1,0:T(4,128)S(1)}, s32[3,192]{1,0:T(4,128)}, u32[]{:S(2)}) copy-start(s32[3,192]{1,0:T(4,128)} %signs_raw.1) | copy-start | bytes 6916
  0.0 6.8 %copy-start = (f32[3,192]{1,0:T(4,128)S(1)}, f32[3,192]{1,0:T(4,128)}, u32[]{:S(2)}) copy-start(f32[3,192]{1,0:T(4,128)} %param.5) | copy-start | bytes 6916
  0.0 12.5 %copy-start.2 = (f32[45]{0:T(128)S(1)}, f32[45]{0:T(128)}, u32[]{:S(2)}) copy-start(f32[45]{0:T(128)} %constant.233) | copy-start | bytes 544
  1.8 20.5 %collective-permute-start.1 = (f32[8,96,128]{2,1,0:T(8,128)S(1)}, f32[8,96,128]{2,1,0:T(8,128)S(1)}, u32[]{:S(2)}, u32[]{:S(2)}) collective-permute-start(f32[8,96,128]{2,1,0:T(8,128)S(1)} %get-tuple-element.30.even_ref), channel_id=1, source_target_pairs={{0,2},{2,0},{4,6},{6,4},{8,10},{10,8},{12,14},{14,12},{16,18},{18,... | collective-permute-start | bytes 1179656 | tf_op jit(solution)/shard_map/ppermute | solution.py:110
  1.9 21.4 %collective-permute-start.2 = (f32[8,96,128]{2,1,0:T(8,128)S(1)}, f32[8,96,128]{2,1,0:T(8,128)S(1)}, u32[]{:S(2)}, u32[]{:S(2)}) collective-permute-start(f32[8,96,128]{2,1,0:T(8,128)S(1)} %get-tuple-element.31.odd_ref), channel_id=1, source_target_pairs={{2,4},{4,2},{6,8},{8,6},{10,12},{12,10},{14,16},{16,14},{18,20},{2... | collective-permute-start | bytes 1179656 | tf_op jit(solution)/shard_map/ppermute | solution.py:112
  7.1 6.8 %collective-permute-start = (f32[2,96,128]{2,1,0:T(8,128)S(1)}, f32[2,96,128]{2,1,0:T(8,128)S(1)}, u32[]{:S(2)}, u32[]{:S(2)}) collective-permute-start(f32[2,96,128]{2,1,0:T(8,128)S(1)} %shard_map.48), channel_id=1, source_target_pairs={{0,1},{1,0},{2,3},{3,2},{4,5},{5,4},{6,7},{7,6},{8,9},{9,8},{10,11... | collective-permute-start | bytes 294920 | tf_op jit(solution)/shard_map/ppermute | solution.py:110
  15.5 32.1 %collective-permute-start.4 = (f32[8,96,128]{2,1,0:T(8,128)S(1)}, f32[8,96,128]{2,1,0:T(8,128)S(1)}, u32[]{:S(2)}, u32[]{:S(2)}) collective-permute-start(f32[8,96,128]{2,1,0:T(8,128)S(1)} %get-tuple-element.33.even_ref), channel_id=1, source_target_pairs={{0,2},{2,0},{4,6},{6,4},{8,10},{10,8},{12,14},{14,12},{16,18},{18,... | collective-permute-start | bytes 1179656 | tf_op jit(solution)/shard_map/ppermute | solution.py:110
  15.6 32.0 %collective-permute-start.5 = (f32[8,96,128]{2,1,0:T(8,128)S(1)}, f32[8,96,128]{2,1,0:T(8,128)S(1)}, u32[]{:S(2)}, u32[]{:S(2)}) collective-permute-start(f32[8,96,128]{2,1,0:T(8,128)S(1)} %get-tuple-element.34.odd_ref), channel_id=1, source_target_pairs={{2,4},{4,2},{6,8},{8,6},{10,12},{12,10},{14,16},{16,14},{18,20},{2... | collective-permute-start | bytes 1179656 | tf_op jit(solution)/shard_map/ppermute | solution.py:112
  23.4 1.4 %collective-permute-start.3 = (f32[2,96,128]{2,1,0:T(8,128)S(1)}, f32[2,96,128]{2,1,0:T(8,128)S(1)}, u32[]{:S(2)}, u32[]{:S(2)}) collective-permute-start(f32[2,96,128]{2,1,0:T(8,128)S(1)} %shard_map.50), channel_id=1, source_target_pairs={{0,1},{1,0},{2,3},{3,2},{4,5},{5,4},{6,7},{7,6},{8,9},{9,8},{10,11... | collective-permute-start | bytes 294920 | tf_op jit(solution)/shard_map/ppermute | solution.py:110
  26.6 29.4 %collective-permute-start.7 = (f32[8,96,128]{2,1,0:T(8,128)S(1)}, f32[8,96,128]{2,1,0:T(8,128)S(1)}, u32[]{:S(2)}, u32[]{:S(2)}) collective-permute-start(f32[8,96,128]{2,1,0:T(8,128)S(1)} %get-tuple-element.36.even_ref), channel_id=1, source_target_pairs={{0,2},{2,0},{4,6},{6,4},{8,10},{10,8},{12,14},{14,12},{16,18},{18,... | collective-permute-start | bytes 1179656 | tf_op jit(solution)/shard_map/ppermute | solution.py:110
  26.7 30.3 %collective-permute-start.8 = (f32[8,96,128]{2,1,0:T(8,128)S(1)}, f32[8,96,128]{2,1,0:T(8,128)S(1)}, u32[]{:S(2)}, u32[]{:S(2)}) collective-permute-start(f32[8,96,128]{2,1,0:T(8,128)S(1)} %get-tuple-element.37.odd_ref), channel_id=1, source_target_pairs={{2,4},{4,2},{6,8},{8,6},{10,12},{12,10},{14,16},{16,14},{18,20},{2... | collective-permute-start | bytes 1179656 | tf_op jit(solution)/shard_map/ppermute | solution.py:112
  47.7 1.4 %collective-permute-start.6 = (f32[2,96,128]{2,1,0:T(8,128)S(1)}, f32[2,96,128]{2,1,0:T(8,128)S(1)}, u32[]{:S(2)}, u32[]{:S(2)}) collective-permute-start(f32[2,96,128]{2,1,0:T(8,128)S(1)} %shard_map.52), channel_id=1, source_target_pairs={{0,1},{1,0},{2,3},{3,2},{4,5},{5,4},{6,7},{7,6},{8,9},{9,8},{10,11... | collective-permute-start | bytes 294920 | tf_op jit(solution)/shard_map/ppermute | solution.py:110
  50.9 20.8 %collective-permute-start.10 = (f32[8,96,128]{2,1,0:T(8,128)S(1)}, f32[8,96,128]{2,1,0:T(8,128)S(1)}, u32[]{:S(2)}, u32[]{:S(2)}) collective-permute-start(f32[8,96,128]{2,1,0:T(8,128)S(1)} %get-tuple-element.39.even_ref), channel_id=1, source_target_pairs={{0,2},{2,0},{4,6},{6,4},{8,10},{10,8},{12,14},{14,12},{16,18},{18,... | collective-permute-start | bytes 1179656 | tf_op jit(solution)/shard_map/ppermute | solution.py:110
  51.0 21.7 %collective-permute-start.11 = (f32[8,96,128]{2,1,0:T(8,128)S(1)}, f32[8,96,128]{2,1,0:T(8,128)S(1)}, u32[]{:S(2)}, u32[]{:S(2)}) collective-permute-start(f32[8,96,128]{2,1,0:T(8,128)S(1)} %get-tuple-element.40.odd_ref), channel_id=1, source_target_pairs={{2,4},{4,2},{6,8},{8,6},{10,12},{12,10},{14,16},{16,14},{18,20},{2... | collective-permute-start | bytes 1179656 | tf_op jit(solution)/shard_map/ppermute | solution.py:112
  57.1 1.4 %collective-permute-start.9 = (f32[2,96,128]{2,1,0:T(8,128)S(1)}, f32[2,96,128]{2,1,0:T(8,128)S(1)}, u32[]{:S(2)}, u32[]{:S(2)}) collective-permute-start(f32[2,96,128]{2,1,0:T(8,128)S(1)} %shard_map.54), channel_id=1, source_target_pairs={{0,1},{1,0},{2,3},{3,2},{4,5},{5,4},{6,7},{7,6},{8,9},{9,8},{10,11... | collective-permute-start | bytes 294920 | tf_op jit(solution)/shard_map/ppermute | solution.py:110

commit v6 on v5

--- a/solution.py
+++ b/solution.py
@@ -14,6 +14,7 @@
 TIME_STEP = 0.5
 DIFFUSION = 0.02
 
+PIECES = 2
 VMEM = pltpu.VMEM
 
 
@@ -119,6 +120,7 @@
         self.half = self.kk // 2
         self.rows = self.ny * self.nz
         self.chunks = 3
+        self.piece = jax.ShapeDtypeStruct((self.ny, self.half // PIECES, self.nx), jnp.float32)
         self.z_two = z_peers > 2
         self.y_two = y_peers > 2
         self.layer = jax.ShapeDtypeStruct((self.ny, self.half, self.nx), jnp.float32)
@@ -167,12 +169,14 @@
     return jnp.sum(jnp.where(same, square, 0.0), axis=1, keepdims=True)
 
 
-def field_copies(plan, source, target, sems):
+def field_copies(plan, source, target, sems, start=0, length=None):
     copies = []
-    depth = plan.half // plan.chunks * plan.rows
+    size = (length or plan.half) // plan.chunks
+    depth = size * plan.rows
     for chunk in range(plan.chunks):
         for member in range(2):
-            where = pl.ds((member * plan.chunks + chunk) * depth, depth)
+            first = member * plan.half + start + chunk * size
+            where = pl.ds(first * plan.rows, depth)
             copies.append(
                 pltpu.make_async_copy(source.at[where], target.at[where], sems.at[chunk, member])
             )
@@ -221,12 +225,26 @@
             odd_ref[y, rows, :] = jnp.where(even, bottom, top)
 
 
+def state_refs(refs, pieces):
+    loads, rest = refs[: 2 * pieces], refs[2 * pieces]
+    return loads[0::2], loads[1::2], rest, refs[2 * pieces + 1 :]
+
+
+def take(refs, y, start, size, half):
+    piece, inner = divmod(start, half // len(refs))
+    return refs[piece][y, pl.ds(inner, size), :]
+
+
+def whole(refs, y):
+    return jnp.concatenate([ref[y] for ref in refs], 0) if len(refs) > 1 else refs[0][y]
+
+
 def member_reader(plan, even, state, got, speed_z):
-    even_ref, odd_ref, rest_ref = state
+    evens, odds, rest_ref = state
 
     def get_p(z, y):
         if z == plan.nz - 1:
-            return jnp.where(even, even_ref[y], odd_ref[y])
+            return jnp.where(even, whole(evens, y), whole(odds, y))
         value = rest_ref[0, z, y]
         if got is not None and z == 0:
             value = value + speed_z * from_below(even, [g[y] for g in got])
@@ -234,7 +252,7 @@
 
     def get_n(z, y):
         if z == 0:
-            return jnp.where(even, odd_ref[y], even_ref[y])
+            return jnp.where(even, whole(odds, y), whole(evens, y))
         value = rest_ref[1, z - 1, y]
         if got is not None and z == plan.nz - 1:
             value = value + speed_z * from_above(even, [g[y] for g in got])
@@ -243,12 +261,13 @@
     return get_p, get_n
 
 
-def edge_body(plan, first, table, even_ref, odd_ref, rest_ref, *refs):
+def edge_body(plan, first, split_in, table, *refs):
+    evens, odds, rest_ref, refs = state_refs(refs, split_in)
     count = 0 if first else 1 + plan.z_two
     got, edges = refs[:count] or None, refs[count:]
     shape = (plan.half, plan.nx)
     get_p, get_n = member_reader(
-        plan, is_even("gz"), (even_ref, odd_ref, rest_ref), got, column(table, 3, shape)
+        plan, is_even("gz"), (evens, odds, rest_ref), got, column(table, 3, shape)
     )
     write_edges(is_even("gy"), column(table, 5, shape) > 0, get_p, get_n, plan, edges)
 
@@ -259,12 +278,14 @@
     return high, low
 
 
-def step_body(plan, first, table, matrix, even_ref, odd_ref, rest_ref, *refs):
+def step_body(plan, first, split_in, pieces, table, matrix, *refs):
+    evens, odds, rest_ref, refs = state_refs(refs, split_in)
     z_count = 0 if first else 1 + plan.z_two
     y_count = 1 + plan.y_two
     got = None if first else refs[:z_count]
     y_got = refs[z_count : z_count + y_count]
-    new_even, new_odd, new_rest, full, highs, lows, turn = refs[z_count + y_count :]
+    outs = refs[z_count + y_count :]
+    loads, (new_rest, full, highs, lows, turn) = outs[: 2 * pieces], outs[2 * pieces :]
     half, nx, ny, nz = plan.half, plan.nx, plan.ny, plan.nz
     even = is_even("gz")
     y_even = is_even("gy")
@@ -281,13 +302,13 @@
         for y in range(ny):
             for z in range(nz):
                 if z == nz - 1:
-                    p = jnp.where(even, even_ref[y, rows, :], odd_ref[y, rows, :])
+                    p = jnp.where(even, take(evens, y, part * 16, 16, half), take(odds, y, part * 16, 16, half))
                 else:
                     p = rest_ref[0, z, y, rows, :]
                     if got is not None and z == 0:
                         p = p + speed_z * from_below(even, [g[y, rows, :] for g in got])
                 if z == 0:
-                    n = jnp.where(even, odd_ref[y, rows, :], even_ref[y, rows, :])
+                    n = jnp.where(even, take(odds, y, part * 16, 16, half), take(evens, y, part * 16, 16, half))
                 else:
                     n = rest_ref[1, z - 1, y, rows, :]
                     if got is not None and z == nz - 1:
@@ -352,24 +373,29 @@
                     new_rest[1, z - 1, y, rows, :] = new_n
                 else:
                     bottom = new_n
-            new_even[y, rows, :] = jnp.where(even, top, bottom)
-            new_odd[y, rows, :] = jnp.where(even, bottom, top)
-
-
-def close_body(plan, table, even_ref, odd_ref, rest_ref, *refs):
-    got, (field, held, sems) = refs[:-3], refs[-3:]
-    copies = field_copies(plan, held, field, sems)
+            piece, inner = divmod(part * 8, half // pieces)
+            loads[2 * piece][y, pl.ds(inner, 8), :] = jnp.where(even, top, bottom)
+            loads[2 * piece + 1][y, pl.ds(inner, 8), :] = jnp.where(even, bottom, top)
+
+
+def close_body(plan, piece, table, even_ref, odd_ref, rest_ref, *refs):
+    count = 1 + plan.z_two
+    got, (field, held, sems) = refs[:count], refs[-3:]
+    length = plan.half // PIECES
+    offset = piece * length
+    copies = field_copies(plan, held, field, sems, offset, length)
     even = is_even("gz")
     nz = plan.nz
-    size = plan.half // plan.chunks
+    size = length // plan.chunks
     for chunk in range(plan.chunks):
-        start = chunk * size
+        inner = pl.ds(chunk * size, size)
+        start = offset + chunk * size
         rows = pl.ds(start, size)
         tab = table[rows, :]
         rising_z = column(tab, 6, (size, plan.nx)) > 0
         speed_z = column(tab, 3, (size, plan.nx))
         for y in range(plan.ny):
-            arrived = [g[y, rows, :] for g in got]
+            arrived = [g[y, inner, :] for g in got]
             low = speed_z * from_below(even, arrived)
             high = speed_z * from_above(even, arrived)
             one, two = even_ref[y, rows, :], odd_ref[y, rows, :]
@@ -400,7 +426,7 @@
     return pltpu.with_memory_space_constraint(value, pltpu.HBM)
 
 
-def call(body, outs, args, scratch=(), raw_in=(), raw_out=False):
+def call(body, outs, args, scratch=(), raw_in=(), raw_out=False, aliases=None):
     in_specs = []
     for i in range(len(args)):
         in_specs.append(pl.BlockSpec(memory_space=pltpu.HBM if i in raw_in else VMEM))
@@ -411,6 +437,7 @@
         in_specs=in_specs,
         out_specs=[pl.BlockSpec(memory_space=pltpu.HBM if raw_out else VMEM)] * len(outs),
         scratch_shapes=list(scratch),
+        input_output_aliases=aliases or {},
         cost_estimate=pl.CostEstimate(flops=8 * moved, bytes_accessed=moved, transcendentals=0),
         compiler_params=pltpu.CompilerParams(vmem_limit_bytes=32 << 20),
     )(*args)
@@ -421,7 +448,6 @@
     half = plan.half
     field = fodf.reshape(plan.field.shape)
     edge_outs = [plan.edge] * (1 + plan.y_two)
-    state_outs = [plan.layer, plan.layer, plan.rest]
     streamed = [
         VMEM(plan.field.shape, jnp.float32),
         pltpu.SemaphoreType.DMA((plan.chunks, 2)),
@@ -442,17 +468,25 @@
     )
     table = columns.T
     matrix = angular_matrix(near)
+    *loads, rest = state
     got = []
     for step in range(ITERS):
+        split_in = len(loads) // 2
+        split_out = PIECES if step == ITERS - 2 else 1
         edges = call(
-            functools.partial(edge_body, plan, step == 0), edge_outs, [table, *state, *got]
+            functools.partial(edge_body, plan, step == 0, split_in),
+            edge_outs,
+            [table, *loads, rest, *got],
         )
-        arriving = exchange(state[0], state[1], "gz")
+        arriving = [
+            exchange(loads[2 * piece], loads[2 * piece + 1], "gz") for piece in range(split_in)
+        ]
         y_got = exchange(edges[0], edges[-1], "gy")
-        state = call(
-            functools.partial(step_body, plan, step == 0),
-            state_outs,
-            [table, matrix, *state, *got, *y_got],
+        load_outs = [plan.layer] * 2 if split_out == 1 else [plan.piece] * (2 * split_out)
+        *loads, rest = call(
+            functools.partial(step_body, plan, step == 0, split_in, split_out),
+            [*load_outs, plan.rest],
+            [table, matrix, *loads, rest, *got, *y_got],
             [
                 VMEM((2, plan.nz, plan.ny + 2, half, plan.nx), jnp.float32),
                 VMEM((half, plan.rows * plan.nx), jnp.bfloat16),
@@ -460,14 +494,20 @@
                 VMEM((half, plan.rows * plan.nx), jnp.float32),
             ],
         )
-        got = arriving
-    field = call(
-        functools.partial(close_body, plan),
-        [plan.field],
-        [table, *state, *got],
-        streamed,
-        raw_out=True,
-    )[0]
+        got = arriving[0]
+    written = []
+    for piece in range(PIECES):
+        args = [table, *loads, rest, *arriving[piece], *written]
+        written = call(
+            functools.partial(close_body, plan, piece),
+            [plan.field],
+            args,
+            streamed,
+            raw_in=(len(args) - 1,) if written else (),
+            raw_out=True,
+            aliases={len(args) - 1: 0} if written else None,
+        )
+    field = written[0]
     return field.reshape(fodf.shape)
 
 

time: 74.5 us -> 74 us (level)
  waiting for transfers between devices: 41.9 us -> 35.2 us
  starting transfers between devices: 14.3 us -> 19.9 us
    ppermute x8 -> x9, waiting for transfers between devices: 39.1 us -> 33.3 us  [exchange(): got = [lax.ppermute(even_load, axis, first)]]
    ppermute x4 -> x5, starting transfers between devices: 13.7 us -> 18.5 us  [exchange(): got.append(lax.ppermute(odd_load, axis, second))]
    ppermute x4 -> x5, waiting for transfers between devices: 2.87 us -> 1.92 us  [exchange(): got.append(lax.ppermute(odd_load, axis, second))]
    ppermute x8 -> x9, starting transfers between devices: 0.57 us -> 1.39 us  [exchange(): got = [lax.ppermute(even_load, axis, first)]]
    pallas_call x11 -> x12, Pallas kernels: 11.6 us -> 12.2 us  [call(): pl.pallas_call(body, out_shape=outs, in_specs=in_specs, out_specs=[pl.Blo...]
  transfers between devices with their start and end apart: 12 -> 14, of which waited for: 10 -> 10; matrix products, arithmetic and copies ran while one was open for 8% -> 8% of each run, Pallas kernels for 11% -> 13%
where the time goes in v6:
time: 74 us; the launch traced here: 73.8 us
  waiting for transfers between devices  35.2 us (48%)
  starting transfers between devices  19.9 us (27%)
  Pallas kernels  12.2 us (16%)
  other arithmetic  5.69 us (8%)
    ppermute x9, waiting for transfers between devices, exchange(): got = [lax.ppermute(even_load, axis, first)]  33.3 us
    ppermute x5, starting transfers between devices, exchange(): got.append(lax.ppermute(odd_load, axis, second))  18.5 us
    pallas_call x12, Pallas kernels, call(): pl.pallas_call(body, out_shape=outs, in_specs=in_specs, out_specs=[pl.Blo...  12.2 us
    another operation x3, other arithmetic, angular_matrix(): chol_lower = lax.linalg.cholesky(gram, symmetrize_input=False)  4.78 us
    ppermute x5, waiting for transfers between devices, exchange(): got.append(lax.ppermute(odd_load, axis, second))  1.92 us
  transfers between devices with their start and end apart: 14, of which 10 were waited for; matrix products, arithmetic and copies ran while one was open for 8% of the time, Pallas kernels for 13%

profile of v6, /device:TPU:2, one launch (start us, length us, event | category | flops | bytes accessed | tf_op | source)
XLA Modules:
  0.0 73.8 jit_solution(8905217769410753526)
XLA Ops:
  0.0 1.8 %shard_map.46 = (f32[8,96,128]{2,1,0:T(8,128)S(1)}, f32[8,96,128]{2,1,0:T(8,128)S(1)}, f32[2,1,8,96,128]{4,3,2,1,0:T(8,128)S(1)}) custom-call(s32[3,192]{1,0:T(4,128)} %signs_raw.1, f32[3072,128]{1,0:T(8,128)} %bitcast.19), custom_call_target="tpu_custom_call" | custom-call | flops 25184256 | bytes 3148032 | tf_op jit(solution)/shard_map/pallas_call | solution.py:434
  1.9 4.9 %collective-permute-start.2 = (f32[8,96,128]{2,1,0:T(8,128)S(1)}, f32[8,96,128]{2,1,0:T(8,128)S(1)}, u32[]{:S(2)}, u32[]{:S(2)}) collective-permute-start(f32[8,96,128]{2,1,0:T(8,128)S(1)} %get-tuple-element.33.refs_1_), channel_id=1, source_target_pairs={{2,4},{4,2},{6,8},{8,6},{10,12},{12,10},{14,16},{16,14},{18,20},{2... | collective-permute-start | bytes 1179656 | tf_op jit(solution)/shard_map/ppermute | solution.py:113
  7.8 4.1 %cholesky.18 = f32[45,45]{1,0:T(8,128)S(1)} custom-call(f32[45,45]{1,0:T(8,128)S(1)} %convolution_multiply_fusion), custom_call_target="Cholesky" | custom-call | tf_op jit(solution)/shard_map/cholesky | solution.py:64
  13.9 1.7 %shard_map.49 = (f32[8,96,128]{2,1,0:T(8,128)S(1)}, f32[8,96,128]{2,1,0:T(8,128)S(1)}, f32[2,1,8,96,128]{4,3,2,1,0:T(8,128)S(1)}) custom-call(f32[96,7]{1,0:T(8,128)S(1)} %bitcast.10, f32[96,96]{1,0:T(8,128)S(1)} %shard_map.47.matrix, f32[8,96,128]{2,1,0:T(8,128)S(1)} %get-tuple-element.32.refs_0_, f32[8,96,128]{2,1,0:T(8,128)S(1)} %get-tuple-element.33.refs_1_, ...), custom_call_target="tpu_custom_call" | custom-call | flops 26268672 | bytes 3283584 | tf_op jit(solution)/shard_map/pallas_call | solution.py:434
  15.6 4.9 %collective-permute-start.5 = (f32[8,96,128]{2,1,0:T(8,128)S(1)}, f32[8,96,128]{2,1,0:T(8,128)S(1)}, u32[]{:S(2)}, u32[]{:S(2)}) collective-permute-start(f32[8,96,128]{2,1,0:T(8,128)S(1)} %get-tuple-element.36.refs_1_), channel_id=1, source_target_pairs={{2,4},{4,2},{6,8},{8,6},{10,12},{12,10},{14,16},{16,14},{18,20},{2... | collective-permute-start | bytes 1179656 | tf_op jit(solution)/shard_map/ppermute | solution.py:113
  20.5 1.8 %collective-permute-done.1.refs_3_ = f32[8,96,128]{2,1,0:T(8,128)S(1)} collective-permute-done((f32[8,96,128]{2,1,0:T(8,128)S(1)}, f32[8,96,128]{2,1,0:T(8,128)S(1)}, u32[]{:S(2)}, u32[]{:S(2)}) %collective-permute-start.1) | collective-permute-done | bytes 393248 | tf_op jit(solution)/shard_map/ppermute | solution.py:111
  22.3 1.0 %collective-permute-done.2.refs_4_ = f32[8,96,128]{2,1,0:T(8,128)S(1)} collective-permute-done((f32[8,96,128]{2,1,0:T(8,128)S(1)}, f32[8,96,128]{2,1,0:T(8,128)S(1)}, u32[]{:S(2)}, u32[]{:S(2)}) %collective-permute-start.2) | collective-permute-done | bytes 393248 | tf_op jit(solution)/shard_map/ppermute | solution.py:113
  23.5 1.3 %collective-permute-done.3.refs_5_ = f32[2,96,128]{2,1,0:T(8,128)S(1)} collective-permute-done((f32[2,96,128]{2,1,0:T(8,128)S(1)}, f32[2,96,128]{2,1,0:T(8,128)S(1)}, u32[]{:S(2)}, u32[]{:S(2)}) %collective-permute-start.3) | collective-permute-done | bytes 98336 | tf_op jit(solution)/shard_map/ppermute | solution.py:111
  24.8 1.8 %shard_map.51 = (f32[8,96,128]{2,1,0:T(8,128)S(1)}, f32[8,96,128]{2,1,0:T(8,128)S(1)}, f32[2,1,8,96,128]{4,3,2,1,0:T(8,128)S(1)}) custom-call(f32[96,7]{1,0:T(8,128)S(1)} %bitcast.12, f32[96,96]{1,0:T(8,128)S(1)} %shard_map.47.matrix, f32[8,96,128]{2,1,0:T(8,128)S(1)} %get-tuple-element.35.refs_0_, f32[8,96,128]{2,1,0:T(8,128)S(1)} %get-tuple-element.36.refs_1_, ...), custom_call_target="tpu_custom_call" | custom-call | flops 32560128 | bytes 4070016 | tf_op jit(solution)/shard_map/pallas_call | solution.py:434
  26.7 2.1 %collective-permute-start.8 = (f32[8,96,128]{2,1,0:T(8,128)S(1)}, f32[8,96,128]{2,1,0:T(8,128)S(1)}, u32[]{:S(2)}, u32[]{:S(2)}) collective-permute-start(f32[8,96,128]{2,1,0:T(8,128)S(1)} %get-tuple-element.39.refs_1_), channel_id=1, source_target_pairs={{2,4},{4,2},{6,8},{8,6},{10,12},{12,10},{14,16},{16,14},{18,20},{2... | collective-permute-start | bytes 1179656 | tf_op jit(solution)/shard_map/ppermute | solution.py:113
  28.8 18.8 %collective-permute-done.4.refs_3_ = f32[8,96,128]{2,1,0:T(8,128)S(1)} collective-permute-done((f32[8,96,128]{2,1,0:T(8,128)S(1)}, f32[8,96,128]{2,1,0:T(8,128)S(1)}, u32[]{:S(2)}, u32[]{:S(2)}) %collective-permute-start.4) | collective-permute-done | bytes 393248 | tf_op jit(solution)/shard_map/ppermute | solution.py:111
  47.8 1.3 %collective-permute-done.6.refs_5_ = f32[2,96,128]{2,1,0:T(8,128)S(1)} collective-permute-done((f32[2,96,128]{2,1,0:T(8,128)S(1)}, f32[2,96,128]{2,1,0:T(8,128)S(1)}, u32[]{:S(2)}, u32[]{:S(2)}) %collective-permute-start.6) | collective-permute-done | bytes 98336 | tf_op jit(solution)/shard_map/ppermute | solution.py:111
  49.1 1.8 %shard_map.53 = (f32[8,48,128]{2,1,0:T(8,128)S(1)}, f32[8,48,128]{2,1,0:T(8,128)S(1)}, f32[8,48,128]{2,1,0:T(8,128)S(1)}, f32[8,48,128]{2,1,0:T(8,128)S(1)}, f32[2,1,8,96,128]{4,3,2,1,0:T(8,128)S(1)}) custom-call(f32[96,7]{1,0:T(8,128)S(1)} %bitcast.14, f32[96,96]{1,0:T(8,128)S(1)} %shard_map.47.matrix, f32[8,96,128]{2,1,0:T(8,128)S(1)} %get-tuple-element.38.refs_0_, ...), custom_call_target="tpu_custom_call" | custom-call | flops 32560128 | bytes 4070016 | tf_op jit(solution)/shard_map/pallas_call | solution.py:434
  51.0 1.9 %collective-permute-start.13 = (f32[8,48,128]{2,1,0:T(8,128)S(1)}, f32[8,48,128]{2,1,0:T(8,128)S(1)}, u32[]{:S(2)}, u32[]{:S(2)}) collective-permute-start(f32[8,48,128]{2,1,0:T(8,128)S(1)} %get-tuple-element.42.refs_1_), channel_id=1, source_target_pairs={{2,4},{4,2},{6,8},{8,6},{10,12},{12,10},{14,16},{16,14},{18,20},{2... | collective-permute-start | bytes 589832 | tf_op jit(solution)/shard_map/ppermute | solution.py:113
  52.9 0.8 %collective-permute-start.10 = (f32[8,48,128]{2,1,0:T(8,128)S(1)}, f32[8,48,128]{2,1,0:T(8,128)S(1)}, u32[]{:S(2)}, u32[]{:S(2)}) collective-permute-start(f32[8,48,128]{2,1,0:T(8,128)S(1)} %get-tuple-element.43.refs_2_), channel_id=1, source_target_pairs={{0,2},{2,0},{4,6},{6,4},{8,10},{10,8},{12,14},{14,12},{16,18},{18,... | collective-permute-start | bytes 589832 | tf_op jit(solution)/shard_map/ppermute | solution.py:111
  53.7 2.3 %collective-permute-done.7.refs_5_ = f32[8,96,128]{2,1,0:T(8,128)S(1)} collective-permute-done((f32[8,96,128]{2,1,0:T(8,128)S(1)}, f32[8,96,128]{2,1,0:T(8,128)S(1)}, u32[]{:S(2)}, u32[]{:S(2)}) %collective-permute-start.7) | collective-permute-done | bytes 393248 | tf_op jit(solution)/shard_map/ppermute | solution.py:111
  56.0 4.8 %collective-permute-start.11 = (f32[8,48,128]{2,1,0:T(8,128)S(1)}, f32[8,48,128]{2,1,0:T(8,128)S(1)}, u32[]{:S(2)}, u32[]{:S(2)}) collective-permute-start(f32[8,48,128]{2,1,0:T(8,128)S(1)} %get-tuple-element.44.refs_3_), channel_id=1, source_target_pairs={{2,4},{4,2},{6,8},{8,6},{10,12},{12,10},{14,16},{16,14},{18,20},{2... | collective-permute-start | bytes 589832 | tf_op jit(solution)/shard_map/ppermute | solution.py:113
  61.0 1.3 %collective-permute-done.9.refs_7_ = f32[2,96,128]{2,1,0:T(8,128)S(1)} collective-permute-done((f32[2,96,128]{2,1,0:T(8,128)S(1)}, f32[2,96,128]{2,1,0:T(8,128)S(1)}, u32[]{:S(2)}, u32[]{:S(2)}) %collective-permute-start.9) | collective-permute-done | bytes 98336 | tf_op jit(solution)/shard_map/ppermute | solution.py:111
  62.3 1.8 %shard_map.55 = (f32[8,96,128]{2,1,0:T(8,128)S(1)}, f32[8,96,128]{2,1,0:T(8,128)S(1)}, f32[2,1,8,96,128]{4,3,2,1,0:T(8,128)S(1)}) custom-call(f32[96,7]{1,0:T(8,128)S(1)} %bitcast.16, f32[96,96]{1,0:T(8,128)S(1)} %shard_map.47.matrix, f32[8,48,128]{2,1,0:T(8,128)S(1)} %get-tuple-element.41.refs_0_, f32[8,48,128]{2,1,0:T(8,128)S(1)} %get-tuple-element.42.refs_1_, ...), custom_call_target="tpu_custom_call" | custom-call | flops 32560128 | bytes 4070016 | tf_op jit(solution)/shard_map/pallas_call | solution.py:434
  64.1 4.5 %collective-permute-done.12.refs_0_ = f32[8,48,128]{2,1,0:T(8,128)S(1)} collective-permute-done((f32[8,48,128]{2,1,0:T(8,128)S(1)}, f32[8,48,128]{2,1,0:T(8,128)S(1)}, u32[]{:S(2)}, u32[]{:S(2)}) %collective-permute-start.12) | collective-permute-done | bytes 196640 | tf_op jit(solution)/shard_map/ppermute | solution.py:111
  68.7 1.1 %shard_map.56.refs_2_ = f32[3072,128]{1,0:T(8,128)} custom-call(f32[96,7]{1,0:T(8,128)S(1)} %bitcast.17, f32[8,96,128]{2,1,0:T(8,128)S(1)} %get-tuple-element.46.even_ref, f32[8,96,128]{2,1,0:T(8,128)S(1)} %get-tuple-element.47.odd_ref, f32[2,1,8,96,128]{4,3,2,1,0:T(8,128)S(1)} %get-tuple-element.48.rest_ref, ...), custom_call_target="tpu_custom_call" | custom-call | flops 28333056 | bytes 3541632 | tf_op jit(solution)/shard_map/pallas_call | solution.py:434
  69.8 2.0 %collective-permute-done.10.refs_0_ = f32[8,48,128]{2,1,0:T(8,128)S(1)} collective-permute-done((f32[8,48,128]{2,1,0:T(8,128)S(1)}, f32[8,48,128]{2,1,0:T(8,128)S(1)}, u32[]{:S(2)}, u32[]{:S(2)}) %collective-permute-start.10) | collective-permute-done | bytes 196640 | tf_op jit(solution)/shard_map/ppermute | solution.py:111
  71.8 1.0 %collective-permute-done.11.refs_1_ = f32[8,48,128]{2,1,0:T(8,128)S(1)} collective-permute-done((f32[8,48,128]{2,1,0:T(8,128)S(1)}, f32[8,48,128]{2,1,0:T(8,128)S(1)}, u32[]{:S(2)}, u32[]{:S(2)}) %collective-permute-start.11) | collective-permute-done | bytes 196640 | tf_op jit(solution)/shard_map/ppermute | solution.py:113
  72.7 1.1 %shard_map.57 = f32[3072,128]{1,0:T(8,128)} custom-call(f32[96,7]{1,0:T(8,128)S(1)} %bitcast.18, f32[8,96,128]{2,1,0:T(8,128)S(1)} %get-tuple-element.46.even_ref, f32[8,96,128]{2,1,0:T(8,128)S(1)} %get-tuple-element.47.odd_ref, f32[2,1,8,96,128]{4,3,2,1,0:T(8,128)S(1)} %get-tuple-element.48.rest_ref, ...), custom_call_target="tpu_custom_call", output_to_operand_aliasing={{}: (6, {})} | custom-call | flops 40915968 | bytes 5114496 | tf_op jit(solution)/shard_map/pallas_call | solution.py:434
  (48 shorter events, 3.6 us)
Async XLA Ops:
  0.0 6.8 %copy-start.1 = (s32[3,192]{1,0:T(4,128)S(1)}, s32[3,192]{1,0:T(4,128)}, u32[]{:S(2)}) copy-start(s32[3,192]{1,0:T(4,128)} %signs_raw.1) | copy-start | bytes 6916
  0.0 6.8 %copy-start = (f32[3,192]{1,0:T(4,128)S(1)}, f32[3,192]{1,0:T(4,128)}, u32[]{:S(2)}) copy-start(f32[3,192]{1,0:T(4,128)} %param.5) | copy-start | bytes 6916
  0.0 7.7 %copy-start.2 = (f32[45]{0:T(128)S(1)}, f32[45]{0:T(128)}, u32[]{:S(2)}) copy-start(f32[45]{0:T(128)} %constant.233) | copy-start | bytes 544
  1.8 20.5 %collective-permute-start.1 = (f32[8,96,128]{2,1,0:T(8,128)S(1)}, f32[8,96,128]{2,1,0:T(8,128)S(1)}, u32[]{:S(2)}, u32[]{:S(2)}) collective-permute-start(f32[8,96,128]{2,1,0:T(8,128)S(1)} %get-tuple-element.32.refs_0_), channel_id=1, source_target_pairs={{0,2},{2,0},{4,6},{6,4},{8,10},{10,8},{12,14},{14,12},{16,18},{18,... | collective-permute-start | bytes 1179656 | tf_op jit(solution)/shard_map/ppermute | solution.py:111
  1.9 21.4 %collective-permute-start.2 = (f32[8,96,128]{2,1,0:T(8,128)S(1)}, f32[8,96,128]{2,1,0:T(8,128)S(1)}, u32[]{:S(2)}, u32[]{:S(2)}) collective-permute-start(f32[8,96,128]{2,1,0:T(8,128)S(1)} %get-tuple-element.33.refs_1_), channel_id=1, source_target_pairs={{2,4},{4,2},{6,8},{8,6},{10,12},{12,10},{14,16},{16,14},{18,20},{2... | collective-permute-start | bytes 1179656 | tf_op jit(solution)/shard_map/ppermute | solution.py:113
  7.1 6.8 %collective-permute-start = (f32[2,96,128]{2,1,0:T(8,128)S(1)}, f32[2,96,128]{2,1,0:T(8,128)S(1)}, u32[]{:S(2)}, u32[]{:S(2)}) collective-permute-start(f32[2,96,128]{2,1,0:T(8,128)S(1)} %shard_map.48), channel_id=1, source_target_pairs={{0,1},{1,0},{2,3},{3,2},{4,5},{5,4},{6,7},{7,6},{8,9},{9,8},{10,11... | collective-permute-start | bytes 294920 | tf_op jit(solution)/shard_map/ppermute | solution.py:111
  15.5 32.1 %collective-permute-start.4 = (f32[8,96,128]{2,1,0:T(8,128)S(1)}, f32[8,96,128]{2,1,0:T(8,128)S(1)}, u32[]{:S(2)}, u32[]{:S(2)}) collective-permute-start(f32[8,96,128]{2,1,0:T(8,128)S(1)} %get-tuple-element.35.refs_0_), channel_id=1, source_target_pairs={{0,2},{2,0},{4,6},{6,4},{8,10},{10,8},{12,14},{14,12},{16,18},{18,... | collective-permute-start | bytes 1179656 | tf_op jit(solution)/shard_map/ppermute | solution.py:111
  15.6 32.0 %collective-permute-start.5 = (f32[8,96,128]{2,1,0:T(8,128)S(1)}, f32[8,96,128]{2,1,0:T(8,128)S(1)}, u32[]{:S(2)}, u32[]{:S(2)}) collective-permute-start(f32[8,96,128]{2,1,0:T(8,128)S(1)} %get-tuple-element.36.refs_1_), channel_id=1, source_target_pairs={{2,4},{4,2},{6,8},{8,6},{10,12},{12,10},{14,16},{16,14},{18,20},{2... | collective-permute-start | bytes 1179656 | tf_op jit(solution)/shard_map/ppermute | solution.py:113
  23.4 1.4 %collective-permute-start.3 = (f32[2,96,128]{2,1,0:T(8,128)S(1)}, f32[2,96,128]{2,1,0:T(8,128)S(1)}, u32[]{:S(2)}, u32[]{:S(2)}) collective-permute-start(f32[2,96,128]{2,1,0:T(8,128)S(1)} %shard_map.50), channel_id=1, source_target_pairs={{0,1},{1,0},{2,3},{3,2},{4,5},{5,4},{6,7},{7,6},{8,9},{9,8},{10,11... | collective-permute-start | bytes 294920 | tf_op jit(solution)/shard_map/ppermute | solution.py:111
  26.6 29.4 %collective-permute-start.7 = (f32[8,96,128]{2,1,0:T(8,128)S(1)}, f32[8,96,128]{2,1,0:T(8,128)S(1)}, u32[]{:S(2)}, u32[]{:S(2)}) collective-permute-start(f32[8,96,128]{2,1,0:T(8,128)S(1)} %get-tuple-element.38.refs_0_), channel_id=1, source_target_pairs={{0,2},{2,0},{4,6},{6,4},{8,10},{10,8},{12,14},{14,12},{16,18},{18,... | collective-permute-start | bytes 1179656 | tf_op jit(solution)/shard_map/ppermute | solution.py:111
  26.7 34.1 %collective-permute-start.8 = (f32[8,96,128]{2,1,0:T(8,128)S(1)}, f32[8,96,128]{2,1,0:T(8,128)S(1)}, u32[]{:S(2)}, u32[]{:S(2)}) collective-permute-start(f32[8,96,128]{2,1,0:T(8,128)S(1)} %get-tuple-element.39.refs_1_), channel_id=1, source_target_pairs={{2,4},{4,2},{6,8},{8,6},{10,12},{12,10},{14,16},{16,14},{18,20},{2... | collective-permute-start | bytes 1179656 | tf_op jit(solution)/shard_map/ppermute | solution.py:113
  47.7 1.4 %collective-permute-start.6 = (f32[2,96,128]{2,1,0:T(8,128)S(1)}, f32[2,96,128]{2,1,0:T(8,128)S(1)}, u32[]{:S(2)}, u32[]{:S(2)}) collective-permute-start(f32[2,96,128]{2,1,0:T(8,128)S(1)} %shard_map.52), channel_id=1, source_target_pairs={{0,1},{1,0},{2,3},{3,2},{4,5},{5,4},{6,7},{7,6},{8,9},{9,8},{10,11... | collective-permute-start | bytes 294920 | tf_op jit(solution)/shard_map/ppermute | solution.py:111
  50.9 17.8 %collective-permute-start.12 = (f32[8,48,128]{2,1,0:T(8,128)S(1)}, f32[8,48,128]{2,1,0:T(8,128)S(1)}, u32[]{:S(2)}, u32[]{:S(2)}) collective-permute-start(f32[8,48,128]{2,1,0:T(8,128)S(1)} %get-tuple-element.41.refs_0_), channel_id=1, source_target_pairs={{0,2},{2,0},{4,6},{6,4},{8,10},{10,8},{12,14},{14,12},{16,18},{18,... | collective-permute-start | bytes 589832 | tf_op jit(solution)/shard_map/ppermute | solution.py:111
  51.0 17.7 %collective-permute-start.13 = (f32[8,48,128]{2,1,0:T(8,128)S(1)}, f32[8,48,128]{2,1,0:T(8,128)S(1)}, u32[]{:S(2)}, u32[]{:S(2)}) collective-permute-start(f32[8,48,128]{2,1,0:T(8,128)S(1)} %get-tuple-element.42.refs_1_), channel_id=1, source_target_pairs={{2,4},{4,2},{6,8},{8,6},{10,12},{12,10},{14,16},{16,14},{18,20},{2... | collective-permute-start | bytes 589832 | tf_op jit(solution)/shard_map/ppermute | solution.py:113
  52.9 18.8 %collective-permute-start.10 = (f32[8,48,128]{2,1,0:T(8,128)S(1)}, f32[8,48,128]{2,1,0:T(8,128)S(1)}, u32[]{:S(2)}, u32[]{:S(2)}) collective-permute-start(f32[8,48,128]{2,1,0:T(8,128)S(1)} %get-tuple-element.43.refs_2_), channel_id=1, source_target_pairs={{0,2},{2,0},{4,6},{6,4},{8,10},{10,8},{12,14},{14,12},{16,18},{18,... | collective-permute-start | bytes 589832 | tf_op jit(solution)/shard_map/ppermute | solution.py:111
  56.0 16.7 %collective-permute-start.11 = (f32[8,48,128]{2,1,0:T(8,128)S(1)}, f32[8,48,128]{2,1,0:T(8,128)S(1)}, u32[]{:S(2)}, u32[]{:S(2)}) collective-permute-start(f32[8,48,128]{2,1,0:T(8,128)S(1)} %get-tuple-element.44.refs_3_), channel_id=1, source_target_pairs={{2,4},{4,2},{6,8},{8,6},{10,12},{12,10},{14,16},{16,14},{18,20},{2... | collective-permute-start | bytes 589832 | tf_op jit(solution)/shard_map/ppermute | solution.py:113
  60.9 1.4 %collective-permute-start.9 = (f32[2,96,128]{2,1,0:T(8,128)S(1)}, f32[2,96,128]{2,1,0:T(8,128)S(1)}, u32[]{:S(2)}, u32[]{:S(2)}) collective-permute-start(f32[2,96,128]{2,1,0:T(8,128)S(1)} %shard_map.54), channel_id=1, source_target_pairs={{0,1},{1,0},{2,3},{3,2},{4,5},{5,4},{6,7},{7,6},{8,9},{9,8},{10,11... | collective-permute-start | bytes 294920 | tf_op jit(solution)/shard_map/ppermute | solution.py:111

commit v7 on v6

--- a/solution.py
+++ b/solution.py
@@ -119,8 +119,12 @@
         self.kk, self.ny, self.nz, self.nx = shape
         self.half = self.kk // 2
         self.rows = self.ny * self.nz
-        self.chunks = 3
-        self.piece = jax.ShapeDtypeStruct((self.ny, self.half // PIECES, self.nx), jnp.float32)
+        self.chunks = 2
+        cut = self.half * 2 // 3 // 16 * 16
+        self.pieces = [
+            jax.ShapeDtypeStruct((self.ny, size, self.nx), jnp.float32)
+            for size in (cut, self.half - cut)
+        ]
         self.z_two = z_peers > 2
         self.y_two = y_peers > 2
         self.layer = jax.ShapeDtypeStruct((self.ny, self.half, self.nx), jnp.float32)
@@ -230,8 +234,16 @@
     return loads[0::2], loads[1::2], rest, refs[2 * pieces + 1 :]
 
 
-def take(refs, y, start, size, half):
-    piece, inner = divmod(start, half // len(refs))
+def locate(refs, start):
+    piece = 0
+    while start >= refs[piece].shape[1]:
+        start -= refs[piece].shape[1]
+        piece += 1
+    return piece, start
+
+
+def take(refs, y, start, size):
+    piece, inner = locate(refs, start)
     return refs[piece][y, pl.ds(inner, size), :]
 
 
@@ -302,13 +314,13 @@
         for y in range(ny):
             for z in range(nz):
                 if z == nz - 1:
-                    p = jnp.where(even, take(evens, y, part * 16, 16, half), take(odds, y, part * 16, 16, half))
+                    p = jnp.where(even, take(evens, y, part * 16, 16), take(odds, y, part * 16, 16))
                 else:
                     p = rest_ref[0, z, y, rows, :]
                     if got is not None and z == 0:
                         p = p + speed_z * from_below(even, [g[y, rows, :] for g in got])
                 if z == 0:
-                    n = jnp.where(even, take(odds, y, part * 16, 16, half), take(evens, y, part * 16, 16, half))
+                    n = jnp.where(even, take(odds, y, part * 16, 16), take(evens, y, part * 16, 16))
                 else:
                     n = rest_ref[1, z - 1, y, rows, :]
                     if got is not None and z == nz - 1:
@@ -373,7 +385,7 @@
                     new_rest[1, z - 1, y, rows, :] = new_n
                 else:
                     bottom = new_n
-            piece, inner = divmod(part * 8, half // pieces)
+            piece, inner = locate(loads[0::2], part * 8)
             loads[2 * piece][y, pl.ds(inner, 8), :] = jnp.where(even, top, bottom)
             loads[2 * piece + 1][y, pl.ds(inner, 8), :] = jnp.where(even, bottom, top)
 
@@ -381,8 +393,8 @@
 def close_body(plan, piece, table, even_ref, odd_ref, rest_ref, *refs):
     count = 1 + plan.z_two
     got, (field, held, sems) = refs[:count], refs[-3:]
-    length = plan.half // PIECES
-    offset = piece * length
+    length = plan.pieces[piece].shape[1]
+    offset = sum(p.shape[1] for p in plan.pieces[:piece])
     copies = field_copies(plan, held, field, sems, offset, length)
     even = is_even("gz")
     nz = plan.nz
@@ -482,7 +494,7 @@
             exchange(loads[2 * piece], loads[2 * piece + 1], "gz") for piece in range(split_in)
         ]
         y_got = exchange(edges[0], edges[-1], "gy")
-        load_outs = [plan.layer] * 2 if split_out == 1 else [plan.piece] * (2 * split_out)
+        load_outs = [plan.layer] * 2 if split_out == 1 else [p for p in plan.pieces for _ in range(2)]
         *loads, rest = call(
             functools.partial(step_body, plan, step == 0, split_in, split_out),
             [*load_outs, plan.rest],

time: 74 us -> 74.1 us (level)
  no operation moved by 1% of the time
where the time goes in v7:
time: 74.1 us; the launch traced here: 73.7 us
  waiting for transfers between devices  35 us (47%)
  starting transfers between devices  19.9 us (27%)
  Pallas kernels  12.3 us (17%)
  other arithmetic  5.69 us (8%)
    ppermute x9, waiting for transfers between devices, exchange(): got = [lax.ppermute(even_load, axis, first)]  33.1 us
    ppermute x5, starting transfers between devices, exchange(): got.append(lax.ppermute(odd_load, axis, second))  18.5 us
    pallas_call x12, Pallas kernels, call(): pl.pallas_call(body, out_shape=outs, in_specs=in_specs, out_specs=[pl.Blo...  12.3 us
    another operation x3, other arithmetic, angular_matrix(): chol_lower = lax.linalg.cholesky(gram, symmetrize_input=False)  4.78 us
    ppermute x5, waiting for transfers between devices, exchange(): got.append(lax.ppermute(odd_load, axis, second))  1.92 us
  transfers between devices with their start and end apart: 14, of which 10 were waited for; matrix products, arithmetic and copies ran while one was open for 8% of the time, Pallas kernels for 13%

profile of v7, /device:TPU:2, one launch (start us, length us, event | category | flops | bytes accessed | tf_op | source)
XLA Modules:
  0.0 73.7 jit_solution(7351177517729543851)
XLA Ops:
  0.0 1.8 %shard_map.46 = (f32[8,96,128]{2,1,0:T(8,128)S(1)}, f32[8,96,128]{2,1,0:T(8,128)S(1)}, f32[2,1,8,96,128]{4,3,2,1,0:T(8,128)S(1)}) custom-call(s32[3,192]{1,0:T(4,128)} %signs_raw.1, f32[3072,128]{1,0:T(8,128)} %bitcast.19), custom_call_target="tpu_custom_call" | custom-call | flops 25184256 | bytes 3148032 | tf_op jit(solution)/shard_map/pallas_call | solution.py:446
  1.9 4.9 %collective-permute-start.2 = (f32[8,96,128]{2,1,0:T(8,128)S(1)}, f32[8,96,128]{2,1,0:T(8,128)S(1)}, u32[]{:S(2)}, u32[]{:S(2)}) collective-permute-start(f32[8,96,128]{2,1,0:T(8,128)S(1)} %get-tuple-element.33.refs_1_), channel_id=1, source_target_pairs={{2,4},{4,2},{6,8},{8,6},{10,12},{12,10},{14,16},{16,14},{18,20},{2... | collective-permute-start | bytes 1179656 | tf_op jit(solution)/shard_map/ppermute | solution.py:113
  7.8 4.1 %cholesky.18 = f32[45,45]{1,0:T(8,128)S(1)} custom-call(f32[45,45]{1,0:T(8,128)S(1)} %convolution_multiply_fusion), custom_call_target="Cholesky" | custom-call | tf_op jit(solution)/shard_map/cholesky | solution.py:64
  12.5 0.7 select_select_fusion
  13.9 1.7 %shard_map.49 = (f32[8,96,128]{2,1,0:T(8,128)S(1)}, f32[8,96,128]{2,1,0:T(8,128)S(1)}, f32[2,1,8,96,128]{4,3,2,1,0:T(8,128)S(1)}) custom-call(f32[96,7]{1,0:T(8,128)S(1)} %bitcast.10, f32[96,96]{1,0:T(8,128)S(1)} %shard_map.47.matrix, f32[8,96,128]{2,1,0:T(8,128)S(1)} %get-tuple-element.32.refs_0_, f32[8,96,128]{2,1,0:T(8,128)S(1)} %get-tuple-element.33.refs_1_, ...), custom_call_target="tpu_custom_call" | custom-call | flops 26268672 | bytes 3283584 | tf_op jit(solution)/shard_map/pallas_call | solution.py:446
  15.6 4.9 %collective-permute-start.5 = (f32[8,96,128]{2,1,0:T(8,128)S(1)}, f32[8,96,128]{2,1,0:T(8,128)S(1)}, u32[]{:S(2)}, u32[]{:S(2)}) collective-permute-start(f32[8,96,128]{2,1,0:T(8,128)S(1)} %get-tuple-element.36.refs_1_), channel_id=1, source_target_pairs={{2,4},{4,2},{6,8},{8,6},{10,12},{12,10},{14,16},{16,14},{18,20},{2... | collective-permute-start | bytes 1179656 | tf_op jit(solution)/shard_map/ppermute | solution.py:113
  20.5 1.8 %collective-permute-done.1.refs_3_ = f32[8,96,128]{2,1,0:T(8,128)S(1)} collective-permute-done((f32[8,96,128]{2,1,0:T(8,128)S(1)}, f32[8,96,128]{2,1,0:T(8,128)S(1)}, u32[]{:S(2)}, u32[]{:S(2)}) %collective-permute-start.1) | collective-permute-done | bytes 393248 | tf_op jit(solution)/shard_map/ppermute | solution.py:111
  22.3 1.0 %collective-permute-done.2.refs_4_ = f32[8,96,128]{2,1,0:T(8,128)S(1)} collective-permute-done((f32[8,96,128]{2,1,0:T(8,128)S(1)}, f32[8,96,128]{2,1,0:T(8,128)S(1)}, u32[]{:S(2)}, u32[]{:S(2)}) %collective-permute-start.2) | collective-permute-done | bytes 393248 | tf_op jit(solution)/shard_map/ppermute | solution.py:113
  23.5 1.3 %collective-permute-done.3.refs_5_ = f32[2,96,128]{2,1,0:T(8,128)S(1)} collective-permute-done((f32[2,96,128]{2,1,0:T(8,128)S(1)}, f32[2,96,128]{2,1,0:T(8,128)S(1)}, u32[]{:S(2)}, u32[]{:S(2)}) %collective-permute-start.3) | collective-permute-done | bytes 98336 | tf_op jit(solution)/shard_map/ppermute | solution.py:111
  24.8 1.8 %shard_map.51 = (f32[8,96,128]{2,1,0:T(8,128)S(1)}, f32[8,96,128]{2,1,0:T(8,128)S(1)}, f32[2,1,8,96,128]{4,3,2,1,0:T(8,128)S(1)}) custom-call(f32[96,7]{1,0:T(8,128)S(1)} %bitcast.12, f32[96,96]{1,0:T(8,128)S(1)} %shard_map.47.matrix, f32[8,96,128]{2,1,0:T(8,128)S(1)} %get-tuple-element.35.refs_0_, f32[8,96,128]{2,1,0:T(8,128)S(1)} %get-tuple-element.36.refs_1_, ...), custom_call_target="tpu_custom_call" | custom-call | flops 32560128 | bytes 4070016 | tf_op jit(solution)/shard_map/pallas_call | solution.py:446
  26.7 2.1 %collective-permute-start.8 = (f32[8,96,128]{2,1,0:T(8,128)S(1)}, f32[8,96,128]{2,1,0:T(8,128)S(1)}, u32[]{:S(2)}, u32[]{:S(2)}) collective-permute-start(f32[8,96,128]{2,1,0:T(8,128)S(1)} %get-tuple-element.39.refs_1_), channel_id=1, source_target_pairs={{2,4},{4,2},{6,8},{8,6},{10,12},{12,10},{14,16},{16,14},{18,20},{2... | collective-permute-start | bytes 1179656 | tf_op jit(solution)/shard_map/ppermute | solution.py:113
  28.8 18.8 %collective-permute-done.4.refs_3_ = f32[8,96,128]{2,1,0:T(8,128)S(1)} collective-permute-done((f32[8,96,128]{2,1,0:T(8,128)S(1)}, f32[8,96,128]{2,1,0:T(8,128)S(1)}, u32[]{:S(2)}, u32[]{:S(2)}) %collective-permute-start.4) | collective-permute-done | bytes 393248 | tf_op jit(solution)/shard_map/ppermute | solution.py:111
  47.8 1.3 %collective-permute-done.6.refs_5_ = f32[2,96,128]{2,1,0:T(8,128)S(1)} collective-permute-done((f32[2,96,128]{2,1,0:T(8,128)S(1)}, f32[2,96,128]{2,1,0:T(8,128)S(1)}, u32[]{:S(2)}, u32[]{:S(2)}) %collective-permute-start.6) | collective-permute-done | bytes 98336 | tf_op jit(solution)/shard_map/ppermute | solution.py:111
  49.1 1.8 %shard_map.53 = (f32[8,64,128]{2,1,0:T(8,128)S(1)}, f32[8,64,128]{2,1,0:T(8,128)S(1)}, f32[8,32,128]{2,1,0:T(8,128)S(1)}, f32[8,32,128]{2,1,0:T(8,128)S(1)}, f32[2,1,8,96,128]{4,3,2,1,0:T(8,128)S(1)}) custom-call(f32[96,7]{1,0:T(8,128)S(1)} %bitcast.14, f32[96,96]{1,0:T(8,128)S(1)} %shard_map.47.matrix, f32[8,96,128]{2,1,0:T(8,128)S(1)} %get-tuple-element.38.refs_0_, ...), custom_call_target="tpu_custom_call" | custom-call | flops 32560128 | bytes 4070016 | tf_op jit(solution)/shard_map/pallas_call | solution.py:446
  51.0 1.9 %collective-permute-start.13 = (f32[8,64,128]{2,1,0:T(8,128)S(1)}, f32[8,64,128]{2,1,0:T(8,128)S(1)}, u32[]{:S(2)}, u32[]{:S(2)}) collective-permute-start(f32[8,64,128]{2,1,0:T(8,128)S(1)} %get-tuple-element.42.refs_1_), channel_id=1, source_target_pairs={{2,4},{4,2},{6,8},{8,6},{10,12},{12,10},{14,16},{16,14},{18,20},{2... | collective-permute-start | bytes 786440 | tf_op jit(solution)/shard_map/ppermute | solution.py:113
  52.9 0.8 %collective-permute-start.10 = (f32[8,32,128]{2,1,0:T(8,128)S(1)}, f32[8,32,128]{2,1,0:T(8,128)S(1)}, u32[]{:S(2)}, u32[]{:S(2)}) collective-permute-start(f32[8,32,128]{2,1,0:T(8,128)S(1)} %get-tuple-element.43.refs_2_), channel_id=1, source_target_pairs={{0,2},{2,0},{4,6},{6,4},{8,10},{10,8},{12,14},{14,12},{16,18},{18,... | collective-permute-start | bytes 393224 | tf_op jit(solution)/shard_map/ppermute | solution.py:111
  53.7 2.3 %collective-permute-done.7.refs_5_ = f32[8,96,128]{2,1,0:T(8,128)S(1)} collective-permute-done((f32[8,96,128]{2,1,0:T(8,128)S(1)}, f32[8,96,128]{2,1,0:T(8,128)S(1)}, u32[]{:S(2)}, u32[]{:S(2)}) %collective-permute-start.7) | collective-permute-done | bytes 393248 | tf_op jit(solution)/shard_map/ppermute | solution.py:111
  56.0 4.8 %collective-permute-start.11 = (f32[8,32,128]{2,1,0:T(8,128)S(1)}, f32[8,32,128]{2,1,0:T(8,128)S(1)}, u32[]{:S(2)}, u32[]{:S(2)}) collective-permute-start(f32[8,32,128]{2,1,0:T(8,128)S(1)} %get-tuple-element.44.refs_3_), channel_id=1, source_target_pairs={{2,4},{4,2},{6,8},{8,6},{10,12},{12,10},{14,16},{16,14},{18,20},{2... | collective-permute-start | bytes 393224 | tf_op jit(solution)/shard_map/ppermute | solution.py:113
  61.0 1.3 %collective-permute-done.9.refs_7_ = f32[2,96,128]{2,1,0:T(8,128)S(1)} collective-permute-done((f32[2,96,128]{2,1,0:T(8,128)S(1)}, f32[2,96,128]{2,1,0:T(8,128)S(1)}, u32[]{:S(2)}, u32[]{:S(2)}) %collective-permute-start.9) | collective-permute-done | bytes 98336 | tf_op jit(solution)/shard_map/ppermute | solution.py:111
  62.3 1.8 %shard_map.55 = (f32[8,96,128]{2,1,0:T(8,128)S(1)}, f32[8,96,128]{2,1,0:T(8,128)S(1)}, f32[2,1,8,96,128]{4,3,2,1,0:T(8,128)S(1)}) custom-call(f32[96,7]{1,0:T(8,128)S(1)} %bitcast.16, f32[96,96]{1,0:T(8,128)S(1)} %shard_map.47.matrix, f32[8,64,128]{2,1,0:T(8,128)S(1)} %get-tuple-element.41.refs_0_, f32[8,64,128]{2,1,0:T(8,128)S(1)} %get-tuple-element.42.refs_1_, ...), custom_call_target="tpu_custom_call" | custom-call | flops 32560128 | bytes 4070016 | tf_op jit(solution)/shard_map/pallas_call | solution.py:446
  64.2 5.9 %collective-permute-done.12.refs_0_ = f32[8,64,128]{2,1,0:T(8,128)S(1)} collective-permute-done((f32[8,64,128]{2,1,0:T(8,128)S(1)}, f32[8,64,128]{2,1,0:T(8,128)S(1)}, u32[]{:S(2)}, u32[]{:S(2)}) %collective-permute-start.12) | collective-permute-done | bytes 262176 | tf_op jit(solution)/shard_map/ppermute | solution.py:111
  70.1 1.3 %shard_map.56.refs_2_ = f32[3072,128]{1,0:T(8,128)} custom-call(f32[96,7]{1,0:T(8,128)S(1)} %bitcast.17, f32[8,96,128]{2,1,0:T(8,128)S(1)} %get-tuple-element.46.even_ref, f32[8,96,128]{2,1,0:T(8,128)S(1)} %get-tuple-element.47.odd_ref, f32[2,1,8,96,128]{4,3,2,1,0:T(8,128)S(1)} %get-tuple-element.48.rest_ref, ...), custom_call_target="tpu_custom_call" | custom-call | flops 29381632 | bytes 3672704 | tf_op jit(solution)/shard_map/pallas_call | solution.py:446
  71.7 1.0 %collective-permute-done.11.refs_1_ = f32[8,32,128]{2,1,0:T(8,128)S(1)} collective-permute-done((f32[8,32,128]{2,1,0:T(8,128)S(1)}, f32[8,32,128]{2,1,0:T(8,128)S(1)}, u32[]{:S(2)}, u32[]{:S(2)}) %collective-permute-start.11) | collective-permute-done | bytes 131104 | tf_op jit(solution)/shard_map/ppermute | solution.py:113
  72.7 1.0 %shard_map.57 = f32[3072,128]{1,0:T(8,128)} custom-call(f32[96,7]{1,0:T(8,128)S(1)} %bitcast.18, f32[8,96,128]{2,1,0:T(8,128)S(1)} %get-tuple-element.46.even_ref, f32[8,96,128]{2,1,0:T(8,128)S(1)} %get-tuple-element.47.odd_ref, f32[2,1,8,96,128]{4,3,2,1,0:T(8,128)S(1)} %get-tuple-element.48.rest_ref, ...), custom_call_target="tpu_custom_call", output_to_operand_aliasing={{}: (6, {})} | custom-call | flops 39867392 | bytes 4983424 | tf_op jit(solution)/shard_map/pallas_call | solution.py:446
  (48 shorter events, 3.4 us)
Async XLA Ops:
  0.0 6.8 %copy-start.1 = (s32[3,192]{1,0:T(4,128)S(1)}, s32[3,192]{1,0:T(4,128)}, u32[]{:S(2)}) copy-start(s32[3,192]{1,0:T(4,128)} %signs_raw.1) | copy-start | bytes 6916
  0.0 6.8 %copy-start = (f32[3,192]{1,0:T(4,128)S(1)}, f32[3,192]{1,0:T(4,128)}, u32[]{:S(2)}) copy-start(f32[3,192]{1,0:T(4,128)} %param.5) | copy-start | bytes 6916
  0.0 7.7 %copy-start.2 = (f32[45]{0:T(128)S(1)}, f32[45]{0:T(128)}, u32[]{:S(2)}) copy-start(f32[45]{0:T(128)} %constant.233) | copy-start | bytes 544
  1.8 20.5 %collective-permute-start.1 = (f32[8,96,128]{2,1,0:T(8,128)S(1)}, f32[8,96,128]{2,1,0:T(8,128)S(1)}, u32[]{:S(2)}, u32[]{:S(2)}) collective-permute-start(f32[8,96,128]{2,1,0:T(8,128)S(1)} %get-tuple-element.32.refs_0_), channel_id=1, source_target_pairs={{0,2},{2,0},{4,6},{6,4},{8,10},{10,8},{12,14},{14,12},{16,18},{18,... | collective-permute-start | bytes 1179656 | tf_op jit(solution)/shard_map/ppermute | solution.py:111
  1.9 21.4 %collective-permute-start.2 = (f32[8,96,128]{2,1,0:T(8,128)S(1)}, f32[8,96,128]{2,1,0:T(8,128)S(1)}, u32[]{:S(2)}, u32[]{:S(2)}) collective-permute-start(f32[8,96,128]{2,1,0:T(8,128)S(1)} %get-tuple-element.33.refs_1_), channel_id=1, source_target_pairs={{2,4},{4,2},{6,8},{8,6},{10,12},{12,10},{14,16},{16,14},{18,20},{2... | collective-permute-start | bytes 1179656 | tf_op jit(solution)/shard_map/ppermute | solution.py:113
  7.1 6.8 %collective-permute-start = (f32[2,96,128]{2,1,0:T(8,128)S(1)}, f32[2,96,128]{2,1,0:T(8,128)S(1)}, u32[]{:S(2)}, u32[]{:S(2)}) collective-permute-start(f32[2,96,128]{2,1,0:T(8,128)S(1)} %shard_map.48), channel_id=1, source_target_pairs={{0,1},{1,0},{2,3},{3,2},{4,5},{5,4},{6,7},{7,6},{8,9},{9,8},{10,11... | collective-permute-start | bytes 294920 | tf_op jit(solution)/shard_map/ppermute | solution.py:111
  15.5 32.1 %collective-permute-start.4 = (f32[8,96,128]{2,1,0:T(8,128)S(1)}, f32[8,96,128]{2,1,0:T(8,128)S(1)}, u32[]{:S(2)}, u32[]{:S(2)}) collective-permute-start(f32[8,96,128]{2,1,0:T(8,128)S(1)} %get-tuple-element.35.refs_0_), channel_id=1, source_target_pairs={{0,2},{2,0},{4,6},{6,4},{8,10},{10,8},{12,14},{14,12},{16,18},{18,... | collective-permute-start | bytes 1179656 | tf_op jit(solution)/shard_map/ppermute | solution.py:111
  15.6 32.0 %collective-permute-start.5 = (f32[8,96,128]{2,1,0:T(8,128)S(1)}, f32[8,96,128]{2,1,0:T(8,128)S(1)}, u32[]{:S(2)}, u32[]{:S(2)}) collective-permute-start(f32[8,96,128]{2,1,0:T(8,128)S(1)} %get-tuple-element.36.refs_1_), channel_id=1, source_target_pairs={{2,4},{4,2},{6,8},{8,6},{10,12},{12,10},{14,16},{16,14},{18,20},{2... | collective-permute-start | bytes 1179656 | tf_op jit(solution)/shard_map/ppermute | solution.py:113
  23.4 1.4 %collective-permute-start.3 = (f32[2,96,128]{2,1,0:T(8,128)S(1)}, f32[2,96,128]{2,1,0:T(8,128)S(1)}, u32[]{:S(2)}, u32[]{:S(2)}) collective-permute-start(f32[2,96,128]{2,1,0:T(8,128)S(1)} %shard_map.50), channel_id=1, source_target_pairs={{0,1},{1,0},{2,3},{3,2},{4,5},{5,4},{6,7},{7,6},{8,9},{9,8},{10,11... | collective-permute-start | bytes 294920 | tf_op jit(solution)/shard_map/ppermute | solution.py:111
  26.6 29.4 %collective-permute-start.7 = (f32[8,96,128]{2,1,0:T(8,128)S(1)}, f32[8,96,128]{2,1,0:T(8,128)S(1)}, u32[]{:S(2)}, u32[]{:S(2)}) collective-permute-start(f32[8,96,128]{2,1,0:T(8,128)S(1)} %get-tuple-element.38.refs_0_), channel_id=1, source_target_pairs={{0,2},{2,0},{4,6},{6,4},{8,10},{10,8},{12,14},{14,12},{16,18},{18,... | collective-permute-start | bytes 1179656 | tf_op jit(solution)/shard_map/ppermute | solution.py:111
  26.7 34.2 %collective-permute-start.8 = (f32[8,96,128]{2,1,0:T(8,128)S(1)}, f32[8,96,128]{2,1,0:T(8,128)S(1)}, u32[]{:S(2)}, u32[]{:S(2)}) collective-permute-start(f32[8,96,128]{2,1,0:T(8,128)S(1)} %get-tuple-element.39.refs_1_), channel_id=1, source_target_pairs={{2,4},{4,2},{6,8},{8,6},{10,12},{12,10},{14,16},{16,14},{18,20},{2... | collective-permute-start | bytes 1179656 | tf_op jit(solution)/shard_map/ppermute | solution.py:113
  47.7 1.4 %collective-permute-start.6 = (f32[2,96,128]{2,1,0:T(8,128)S(1)}, f32[2,96,128]{2,1,0:T(8,128)S(1)}, u32[]{:S(2)}, u32[]{:S(2)}) collective-permute-start(f32[2,96,128]{2,1,0:T(8,128)S(1)} %shard_map.52), channel_id=1, source_target_pairs={{0,1},{1,0},{2,3},{3,2},{4,5},{5,4},{6,7},{7,6},{8,9},{9,8},{10,11... | collective-permute-start | bytes 294920 | tf_op jit(solution)/shard_map/ppermute | solution.py:111
  50.9 19.2 %collective-permute-start.12 = (f32[8,64,128]{2,1,0:T(8,128)S(1)}, f32[8,64,128]{2,1,0:T(8,128)S(1)}, u32[]{:S(2)}, u32[]{:S(2)}) collective-permute-start(f32[8,64,128]{2,1,0:T(8,128)S(1)} %get-tuple-element.41.refs_0_), channel_id=1, source_target_pairs={{0,2},{2,0},{4,6},{6,4},{8,10},{10,8},{12,14},{14,12},{16,18},{18,... | collective-permute-start | bytes 786440 | tf_op jit(solution)/shard_map/ppermute | solution.py:111
  51.0 19.1 %collective-permute-start.13 = (f32[8,64,128]{2,1,0:T(8,128)S(1)}, f32[8,64,128]{2,1,0:T(8,128)S(1)}, u32[]{:S(2)}, u32[]{:S(2)}) collective-permute-start(f32[8,64,128]{2,1,0:T(8,128)S(1)} %get-tuple-element.42.refs_1_), channel_id=1, source_target_pairs={{2,4},{4,2},{6,8},{8,6},{10,12},{12,10},{14,16},{16,14},{18,20},{2... | collective-permute-start | bytes 786440 | tf_op jit(solution)/shard_map/ppermute | solution.py:113
  52.9 18.8 %collective-permute-start.10 = (f32[8,32,128]{2,1,0:T(8,128)S(1)}, f32[8,32,128]{2,1,0:T(8,128)S(1)}, u32[]{:S(2)}, u32[]{:S(2)}) collective-permute-start(f32[8,32,128]{2,1,0:T(8,128)S(1)} %get-tuple-element.43.refs_2_), channel_id=1, source_target_pairs={{0,2},{2,0},{4,6},{6,4},{8,10},{10,8},{12,14},{14,12},{16,18},{18,... | collective-permute-start | bytes 393224 | tf_op jit(solution)/shard_map/ppermute | solution.py:111
  56.0 16.7 %collective-permute-start.11 = (f32[8,32,128]{2,1,0:T(8,128)S(1)}, f32[8,32,128]{2,1,0:T(8,128)S(1)}, u32[]{:S(2)}, u32[]{:S(2)}) collective-permute-start(f32[8,32,128]{2,1,0:T(8,128)S(1)} %get-tuple-element.44.refs_3_), channel_id=1, source_target_pairs={{2,4},{4,2},{6,8},{8,6},{10,12},{12,10},{14,16},{16,14},{18,20},{2... | collective-permute-start | bytes 393224 | tf_op jit(solution)/shard_map/ppermute | solution.py:113
  60.9 1.4 %collective-permute-start.9 = (f32[2,96,128]{2,1,0:T(8,128)S(1)}, f32[2,96,128]{2,1,0:T(8,128)S(1)}, u32[]{:S(2)}, u32[]{:S(2)}) collective-permute-start(f32[2,96,128]{2,1,0:T(8,128)S(1)} %shard_map.54), channel_id=1, source_target_pairs={{0,1},{1,0},{2,3},{3,2},{4,5},{5,4},{6,7},{7,6},{8,9},{9,8},{10,11... | collective-permute-start | bytes 294920 | tf_op jit(solution)/shard_map/ppermute | solution.py:111
